TPU v7x, 32 devices: a whole 2x2x4 slice. The times are simulated.
32 devices in a mesh: dp: 8 (over y, x, core), tensor: 4 (over z).
Axes of the slice: x: 2, y: 2, z: 4, core: 2. Of those that a mesh axis runs over, the one named last changes fastest.
Arguments:
- tokens: bfloat16 [2, 16, 10, 64, 1024], P(None, 'dp', None, 'tensor'), may hold values from -6 to 6
- conditioning: bfloat16 [2, 16, 1024], P(None, 'dp'), may hold values from -6 to 6
- frame_counts: int32 [2, 16], P(None, 'dp'), may hold values from 2 to 9, as said below
- w_qkv: bfloat16 [1024, 3, 1024], P('dp', None, 'tensor'), may hold values from -0.1875 to 0.1875
- w_out: bfloat16 [1024, 1024], P('dp', 'tensor'), may hold values from -1.5 to 1.5
- w_up: bfloat16 [1024, 4096], P('dp', 'tensor'), may hold values from -0.1875 to 0.1875
- w_down: bfloat16 [1024, 4096], P('dp', 'tensor'), may hold values from -0.09375 to 0.09375
- w_ada: bfloat16 [1024, 6144], P('dp', 'tensor'), may hold values from -0.1875 to 0.1875
- pos_table: float32 [16, 2025], P('tensor'), may hold values from -4 to 4
- cotangent: bfloat16 [2, 16, 10, 64, 1024], P(None, 'dp', None, 'tensor'), may hold values from -6 to 6
Outputs:
- block_out: bfloat16 [2, 16, 10, 64, 1024], P(None, 'dp', None, 'tensor')
- grad_tokens: bfloat16 [2, 16, 10, 64, 1024], P(None, 'dp', None, 'tensor')
- grad_cond: float32 [2, 16, 1024], P(None, 'dp')
- grad_w_qkv: float32 [1024, 3, 1024], P('dp', None, 'tensor')
- grad_w_out: float32 [1024, 1024], P('dp', 'tensor')
- grad_w_up: float32 [1024, 4096], P('dp', 'tensor')
- grad_w_down: float32 [1024, 4096], P('dp', 'tensor')
- grad_w_ada: float32 [1024, 6144], P('dp', 'tensor')
- grad_table: float32 [16, 2025], P('tensor')
Inputs may be any that keep to these rules, and one draw needn't show every extreme that they name: `frame_counts`: given frames of each clip; in every draw one clip has 2 and another 10 - 1.
All inputs are finite; a program needn't handle non-finite values.
Results may differ from a plain program's by a relative error of at most 0.018.
The roundings to bfloat16 on the way count: a program that leaves them out, or rounds other values in their place, can miss the bound.
Values may be sent and summed in bfloat16 or wider, within the bound.
No kernel may reach another device: no remote copies, remote signals or barrier semaphores. Data moves between devices by JAX's collectives and lax.ppermute only.
A program may use at most 192 MiB of HBM per device.

v0:
```python
import jax
import jax.numpy as jnp
from jax import lax
from jax.sharding import PartitionSpec as P

HEAD_DIM = 64
WIN_T = 5
WIN_S = 8
FRAMES = 10
SPATIAL = 64
OFFSETS = 2025


EPSILON = 1e-06
NEGATIVE = -1e30
HIGHEST = lax.Precision.HIGHEST


def offset_table():
    length_win = WIN_T * WIN_S * WIN_S
    places = jnp.arange(length_win)
    frame_at = places // (WIN_S * WIN_S)
    row_at = places // WIN_S % WIN_S
    col_at = places % WIN_S
    span_rows = 2 * WIN_S - 1
    index_out = (frame_at[:, None] - frame_at[None, :] + WIN_T - 1) * span_rows * span_rows
    index_out = index_out + (row_at[:, None] - row_at[None, :] + WIN_S - 1) * span_rows
    index_out = index_out + (col_at[:, None] - col_at[None, :] + WIN_S - 1)
    return index_out


def diff_onehot(count, spread):
    first = jnp.arange(count)[:, None, None]
    second = jnp.arange(count)[None, :, None]
    target = jnp.arange(spread)[None, None, :]
    return (first - second + count - 1 == target).astype(jnp.float32)


def ada_norm(values, shift_row, scale_row):
    center = values - jnp.mean(values, axis=-1, keepdims=True)
    spread = jnp.mean(center * center, axis=-1, keepdims=True)
    return center * lax.rsqrt(spread + EPSILON) * (1.0 + scale_row) + shift_row


def gather_tokens(local_rows):
    return lax.all_gather(local_rows, "tensor", axis=1, tiled=True)


def sum_tokens(partial_sum):
    return lax.psum_scatter(
        partial_sum.astype(jnp.bfloat16), "tensor", scatter_dimension=1, tiled=True
    ).astype(jnp.float32)


def gather_grads(local_rows):
    return lax.all_gather(local_rows, "tensor", axis=1, tiled=True)


def sum_grads(partial_sum):
    return lax.psum_scatter(
        partial_sum.astype(jnp.bfloat16), "tensor", scatter_dimension=1, tiled=True
    ).astype(jnp.float32)


def masked_scores(queries, keys_in, pos_bias, key_live):
    scores = (
        jnp.einsum("wqhe,wkhe->whqk", queries, keys_in, preferred_element_type=jnp.float32)
        * HEAD_DIM ** (-0.5)
        + pos_bias[None]
    )
    return jnp.where(key_live[:, None, None, :] > 0, scores, NEGATIVE)


def attend(queries, keys_in, values_in, pos_bias, key_live):
    masked = masked_scores(queries, keys_in, pos_bias, key_live)
    top_score = jnp.max(masked, axis=-1, keepdims=True)
    expo_part = jnp.exp(masked - top_score) * key_live[:, None, None, :]
    totals = jnp.maximum(jnp.sum(expo_part, axis=-1, keepdims=True), 1.0)
    weights_low = (expo_part / totals).astype(jnp.bfloat16)
    attended = jnp.einsum(
        "whqk,wkhe->wqhe", weights_low, values_in, preferred_element_type=jnp.float32
    )
    return (attended, top_score + jnp.log(totals))


def attend_back(queries, keys_in, values_in, pos_bias, key_live, log_total, grad_att):
    masked = masked_scores(queries, keys_in, pos_bias, key_live)
    weights_full = jnp.exp(masked - log_total) * key_live[:, None, None, :]
    grad_values = jnp.einsum(
        "whqk,wqhe->wkhe",
        weights_full.astype(jnp.bfloat16),
        grad_att,
        preferred_element_type=jnp.float32,
    )
    grad_weights = jnp.einsum(
        "wqhe,wkhe->whqk", grad_att, values_in, preferred_element_type=jnp.float32
    )
    row_inner = jnp.sum(weights_full * grad_weights, axis=-1, keepdims=True)
    grad_scores = (weights_full * (grad_weights - row_inner)).astype(jnp.bfloat16)
    score_scale = HEAD_DIM ** (-0.5)
    grad_queries = (
        jnp.einsum("whqk,wkhe->wqhe", grad_scores, keys_in, preferred_element_type=jnp.float32)
        * score_scale
    )
    grad_keys = (
        jnp.einsum("whqk,wqhe->wkhe", grad_scores, queries, preferred_element_type=jnp.float32)
        * score_scale
    )
    stacked = jnp.stack([grad_queries, grad_keys, grad_values], axis=2).astype(jnp.bfloat16)
    return (stacked, grad_scores)


def table_grad(grad_scores):
    folded = jnp.sum(grad_scores.astype(jnp.float32), axis=0)
    heads_local = folded.shape[0]
    shaped = folded.reshape(heads_local, WIN_T, WIN_S, WIN_S, WIN_T, WIN_S, WIN_S)
    col_pairs = diff_onehot(WIN_S, 2 * WIN_S - 1)
    frame_pairs = diff_onehot(WIN_T, 2 * WIN_T - 1)
    step_one = jnp.einsum("harcbsu,cuo->harbso", shaped, col_pairs, precision=HIGHEST)
    step_two = jnp.einsum("harbso,rsp->habpo", step_one, col_pairs, precision=HIGHEST)
    step_three = jnp.einsum("habpo,abt->htpo", step_two, frame_pairs, precision=HIGHEST)
    return step_three.reshape(heads_local, OFFSETS)


def body(
    tokens, conditioning, frame_counts, w_qkv, w_out, w_up, w_down, w_ada, pos_table, cotangent
):
    micro_count = tokens.shape[0]
    clip_dev = tokens.shape[1]
    spatial_local = tokens.shape[3]
    model_width = tokens.shape[-1]
    frames_all = clip_dev * FRAMES
    window_count = frames_all // WIN_T
    window_len = WIN_T * SPATIAL
    heads_local = pos_table.shape[0]
    ada_full = lax.all_gather(w_ada, "dp", axis=0, tiled=True)
    cond_float = conditioning.astype(jnp.float32).reshape(micro_count * clip_dev, model_width)
    cond_act = jax.nn.silu(cond_float).astype(jnp.bfloat16)
    mod_part = jnp.dot(cond_act, ada_full, preferred_element_type=jnp.float32)
    modulation = lax.all_gather(mod_part, "tensor", axis=1, tiled=True).reshape(
        micro_count, clip_dev, 6, model_width
    )
    offsets = offset_table()
    pos_bias = pos_table[:, offsets]
    frame_live = (
        jnp.arange(FRAMES)[None, :] < frame_counts.reshape(micro_count * clip_dev, 1)
    ).astype(jnp.float32)
    frame_live = frame_live.reshape(micro_count, frames_all)

    def frame_rows(mod_rows):
        return jnp.repeat(mod_rows, FRAMES, axis=0)[:, :, None, :]

    def per_clip(values):
        return jnp.sum(values.reshape(clip_dev, FRAMES, model_width), axis=1)

    def forward_step(unused_state, inputs):
        tok_rows, mod_rows, live_frames = inputs
        mods = frame_rows(mod_rows)
        layer = (
            lax.all_gather(w_qkv, "dp", axis=0, tiled=True),
            lax.all_gather(w_out, "dp", axis=0, tiled=True),
            lax.all_gather(w_up, "dp", axis=0, tiled=True),
            lax.all_gather(w_down, "dp", axis=0, tiled=True),
        )
        wq_full, wo_full, wu_full, wd_full = layer
        resid = tok_rows.astype(jnp.float32).reshape(frames_all, spatial_local, model_width)
        normed = ada_norm(resid, mods[:, 0], mods[:, 1]).astype(jnp.bfloat16)
        normed_full = gather_tokens(normed)
        qkv_full = jnp.einsum(
            "fsd,dcm->fscm", normed_full, wq_full, preferred_element_type=jnp.float32
        ).astype(jnp.bfloat16)
        split_heads = qkv_full.reshape(window_count, window_len, 3, heads_local, HEAD_DIM)
        key_live = jnp.repeat(live_frames, SPATIAL).reshape(window_count, window_len)
        attended, log_total = attend(
            split_heads[:, :, 0], split_heads[:, :, 1], split_heads[:, :, 2], pos_bias, key_live
        )
        attended = (
            attended.reshape(frames_all, SPATIAL, heads_local * HEAD_DIM)
            * live_frames[:, None, None]
        ).astype(jnp.bfloat16)
        branch_a = sum_tokens(
            jnp.einsum("fsk,dk->fsd", attended, wo_full, preferred_element_type=jnp.float32)
        )
        middle = resid + mods[:, 2] * branch_a
        normed_two = ada_norm(middle, mods[:, 3], mods[:, 4]).astype(jnp.bfloat16)
        normed_two_full = gather_tokens(normed_two)
        hidden = jnp.einsum(
            "fsd,dk->fsk", normed_two_full, wu_full, preferred_element_type=jnp.float32
        )
        activ = jax.nn.gelu(hidden).astype(jnp.bfloat16)
        branch_b = sum_tokens(
            jnp.einsum("fsk,dk->fsd", activ, wd_full, preferred_element_type=jnp.float32)
        )
        result = middle + mods[:, 5] * branch_b
        kept = (
            normed_full,
            qkv_full,
            log_total,
            attended,
            branch_a,
            middle,
            normed_two_full,
            hidden,
            branch_b,
        )
        return (unused_state, (result.astype(jnp.bfloat16).reshape(tok_rows.shape), kept))

    unused_end, (block_out, kept_all) = lax.scan(
        forward_step, jnp.zeros((), jnp.float32), (tokens, modulation, frame_live)
    )
    sum_init = tuple(
        (jnp.zeros(weight.shape, jnp.float32) for weight in (w_qkv, w_out, w_up, w_down))
    )
    table_init = jnp.zeros(pos_table.shape, jnp.float32)

    def backward_step(state_in, inputs):
        layer_acc, table_acc = state_in
        cot_rows, tok_rows, mod_rows, live_frames, kept = inputs
        mods = frame_rows(mod_rows)
        (
            normed_full,
            qkv_full,
            log_total,
            attended,
            branch_a,
            middle,
            normed_two_full,
            hidden,
            branch_b,
        ) = kept[:9]
        wq_full, wo_full, wu_full, wd_full = (
            lax.all_gather(w_qkv, "dp", axis=0, tiled=True),
            lax.all_gather(w_out, "dp", axis=0, tiled=True),
            lax.all_gather(w_up, "dp", axis=0, tiled=True),
            lax.all_gather(w_down, "dp", axis=0, tiled=True),
        )
        resid = tok_rows.astype(jnp.float32).reshape(frames_all, spatial_local, model_width)
        grad_result = cot_rows.astype(jnp.float32).reshape(frames_all, spatial_local, model_width)
        grad_branch_b = gather_grads((grad_result * mods[:, 5]).astype(jnp.bfloat16))
        grad_gate_b = per_clip(jnp.sum(grad_result * branch_b, axis=1))
        grad_activ = jnp.einsum(
            "fsd,dk->fsk", grad_branch_b, wd_full, preferred_element_type=jnp.float32
        )
        activ = jax.nn.gelu(hidden).astype(jnp.bfloat16)
        grad_down = jnp.einsum(
            "fsd,fsk->dk", grad_branch_b, activ, preferred_element_type=jnp.float32
        )
        grad_hidden = jax.vjp(jax.nn.gelu, hidden)[1](grad_activ)[0].astype(jnp.bfloat16)
        grad_up = jnp.einsum(
            "fsd,fsk->dk", normed_two_full, grad_hidden, preferred_element_type=jnp.float32
        )
        grad_normed_two = sum_grads(
            jnp.einsum("fsk,dk->fsd", grad_hidden, wu_full, preferred_element_type=jnp.float32)
        )
        pull_two = jax.vjp(ada_norm, middle, mods[:, 3], mods[:, 4])[1]
        grad_middle_norm, grad_shift_b, grad_scale_b = pull_two(grad_normed_two)
        grad_middle = grad_result + grad_middle_norm
        grad_branch_a = gather_grads((grad_middle * mods[:, 2]).astype(jnp.bfloat16))
        grad_gate_a = per_clip(jnp.sum(grad_middle * branch_a, axis=1))
        grad_attended = jnp.einsum(
            "fsd,dk->fsk", grad_branch_a, wo_full, preferred_element_type=jnp.float32
        ).astype(jnp.bfloat16)
        grad_attended = grad_attended * live_frames[:, None, None].astype(jnp.bfloat16)
        grad_outproj = jnp.einsum(
            "fsd,fsk->dk", grad_branch_a, attended, preferred_element_type=jnp.float32
        )
        split_heads = qkv_full.reshape(window_count, window_len, 3, heads_local, HEAD_DIM)
        key_live = jnp.repeat(live_frames, SPATIAL).reshape(window_count, window_len)
        grad_windows, grad_scores = attend_back(
            split_heads[:, :, 0],
            split_heads[:, :, 1],
            split_heads[:, :, 2],
            pos_bias,
            key_live,
            log_total,
            grad_attended.reshape(window_count, window_len, heads_local, HEAD_DIM),
        )
        grad_qkv = grad_windows.reshape(frames_all, SPATIAL, 3, heads_local * HEAD_DIM)
        grad_inproj = jnp.einsum(
            "fsd,fscm->dcm", normed_full, grad_qkv, preferred_element_type=jnp.float32
        )
        grad_normed = sum_grads(
            jnp.einsum("fscm,dcm->fsd", grad_qkv, wq_full, preferred_element_type=jnp.float32)
        )
        pull_one = jax.vjp(ada_norm, resid, mods[:, 0], mods[:, 1])[1]
        grad_resid_norm, grad_shift_a, grad_scale_a = pull_one(grad_normed)
        grad_input = (grad_middle + grad_resid_norm).astype(jnp.bfloat16).reshape(tok_rows.shape)
        grad_mod = jnp.stack(
            [
                per_clip(grad_shift_a[:, 0]),
                per_clip(grad_scale_a[:, 0]),
                grad_gate_a,
                per_clip(grad_shift_b[:, 0]),
                per_clip(grad_scale_b[:, 0]),
                grad_gate_b,
            ],
            axis=1,
        )
        layer_parts = (
            lax.psum_scatter(grad_inproj, "dp", scatter_dimension=0, tiled=True),
            lax.psum_scatter(grad_outproj, "dp", scatter_dimension=0, tiled=True),
            lax.psum_scatter(grad_up, "dp", scatter_dimension=0, tiled=True),
            lax.psum_scatter(grad_down, "dp", scatter_dimension=0, tiled=True),
        )
        layer_acc = tuple((accum + piece for accum, piece in zip(layer_acc, layer_parts)))
        table_acc = table_acc + table_grad(grad_scores)
        return ((layer_acc, table_acc), (grad_input, grad_mod))

    (layer_acc, table_acc), (grad_tokens, grad_mods) = lax.scan(
        backward_step, (sum_init, table_init), (cotangent, tokens, modulation, frame_live, kept_all)
    )
    grad_table = lax.psum(table_acc, "dp")
    grad_mod_cols = lax.psum_scatter(
        grad_mods.reshape(micro_count * clip_dev, 6 * model_width).astype(jnp.bfloat16),
        "tensor",
        scatter_dimension=1,
        tiled=True,
    ).astype(jnp.float32)
    ada_term = jnp.dot(cond_act.astype(jnp.float32).T, grad_mod_cols, precision=HIGHEST)
    grad_ada = lax.psum_scatter(ada_term, "dp", scatter_dimension=0, tiled=True)
    act_term = jnp.dot(grad_mod_cols, ada_full.astype(jnp.float32).T, precision=HIGHEST)
    grad_act = lax.psum(act_term, "tensor")
    grad_cond = jax.vjp(jax.nn.silu, cond_float)[1](grad_act)[0].reshape(
        micro_count, clip_dev, model_width
    )
    return (
        block_out,
        grad_tokens,
        grad_cond,
        layer_acc[0],
        layer_acc[1],
        layer_acc[2],
        layer_acc[3],
        grad_ada,
        grad_table,
    )


def solution(mesh):
    placed = (
        P(None, "dp", None, "tensor", None),
        P(None, "dp", None),
        P(None, "dp"),
        P("dp", None, "tensor"),
        P("dp", "tensor"),
        P("dp", "tensor"),
        P("dp", "tensor"),
        P("dp", "tensor"),
        P("tensor", None),
        P(None, "dp", None, "tensor", None),
    )
    return jax.shard_map(
        body,
        mesh=mesh,
        in_specs=placed,
        out_specs=(
            P(None, "dp", None, "tensor", None),
            P(None, "dp", None, "tensor", None),
            P(None, "dp", None),
            P("dp", None, "tensor"),
            P("dp", "tensor"),
            P("dp", "tensor"),
            P("dp", "tensor"),
            P("dp", "tensor"),
            P("tensor", None),
        ),
        check_vma=False,
    )
```

profile of v0, /device:TPU:0, one launch (start us, length us, event | category | flops | bytes accessed | tf_op | source)
XLA Modules:
  0.0 2312.4 jit_solution(17113410990596571601)
XLA Ops:
  10.5 338.6 %gather_fusion = f32[102400,4]{1,0:T(8,128)} fusion(f32[4,2025]{0,1:T(8,128)S(1)} %copy.97, s32[102400]{0:T(1024)S(1)} %broadcast_clamp_fusion), kind=kCustom, calls=%fused_computation | custom fusion | bytes 3686400 | tf_op jit(solution)/shard_map/gather | solution.py:144
  349.1 33.2 %copy.98 = f32[320,320,4]{0,1,2:T(8,128)} copy(f32[320,320,4]{2,1,0:T(8,128)} %bitcast.457) | data formatting | bytes 3276800 | tf_op jit(solution)/shard_map/gather | solution.py:144
  402.5 737.5 %while.56 = (s32[]{:T(128)}, bf16[2,2,10,16,1024]{4,3,2,1,0:T(8,128)(2,1)}, bf16[2,20,64,1024]{3,2,1,0:T(8,128)(2,1)}, bf16[2,20,64,3,256]{4,2,3,1,0:T(8,128)(2,...) while((s32[]{:T(128)}, ...), condition=%wide.region_9.10_spmd, body=%wide.region_0.9_spmd.sunk | while | flops 8526937088 | bytes 300191872 | solution.py:208
  448.5 57.0 %all-gather.16.cloned.1.call-done = bf16[20,64,1024]{2,1,0:T(8,128)(2,1)} async-done(((bf16[20,16,1024]{2,1,0:T(8,128)(2,1)}), bf16[20,64,1024]{2,1,0:T(8,128)(2,1)}) %all-gather.16.cloned.1.call-update) | async-done | bytes 2621456 | tf_op jit(solution)/shard_map/while/body/eval_jaxpr/all_gather | solution.py:46
  550.5 50.2 %reduce-scatter.17.cloned.1.call-done = bf16[20,16,1024]{2,1,0:T(8,128)(2,1)} async-done(((bf16[20,64,1024]{2,1,0:T(8,128)(2,1)}), bf16[20,16,1024]{2,1,0:T(8,128)(2,1)}) %reduce-scatter.17.cloned.1.call-update) | async-done | bytes 655376 | tf_op jit(solution)/shard_map/while/body/eval_jaxpr/reduce_scatter | solution.py:50
  605.6 24.6 %all-gather.22.cloned.1.call-done = bf16[1024,1024]{1,0:T(8,128)(2,1)} async-done(((bf16[128,1024]{1,0:T(8,128)(2,1)}), bf16[1024,1024]{1,0:T(8,128)(2,1)}) %all-gather.22.cloned.1.call-update) | async-done | bytes 2097168 | tf_op jit(solution)/shard_map/while/body/eval_jaxpr/all_gather | solution.py:162
  630.2 56.9 %all-gather.20.cloned.1.call-done = bf16[20,64,1024]{2,1,0:T(8,128)(2,1)} async-done(((bf16[20,16,1024]{2,1,0:T(8,128)(2,1)}), bf16[20,64,1024]{2,1,0:T(8,128)(2,1)}) %all-gather.20.cloned.1.call-update) | async-done | bytes 2621456 | tf_op jit(solution)/shard_map/while/body/eval_jaxpr/all_gather | solution.py:46
  696.3 19.5 all-gather.18.cloned.1.call-done
  734.8 41.2 %reduce-scatter.19.cloned.1.call-done = bf16[20,16,1024]{2,1,0:T(8,128)(2,1)} async-done(((bf16[20,64,1024]{2,1,0:T(8,128)(2,1)}), bf16[20,16,1024]{2,1,0:T(8,128)(2,1)}) %reduce-scatter.19.cloned.1.call-update) | async-done | bytes 655376 | tf_op jit(solution)/shard_map/while/body/eval_jaxpr/reduce_scatter | solution.py:50
  808.9 56.9 %all-gather.16.cloned.1.call-done = bf16[20,64,1024]{2,1,0:T(8,128)(2,1)} async-done(((bf16[20,16,1024]{2,1,0:T(8,128)(2,1)}), bf16[20,64,1024]{2,1,0:T(8,128)(2,1)}) %all-gather.16.cloned.1.call-update) | async-done | bytes 2621456 | tf_op jit(solution)/shard_map/while/body/eval_jaxpr/all_gather | solution.py:46
  910.7 50.2 %reduce-scatter.17.cloned.1.call-done = bf16[20,16,1024]{2,1,0:T(8,128)(2,1)} async-done(((bf16[20,64,1024]{2,1,0:T(8,128)(2,1)}), bf16[20,16,1024]{2,1,0:T(8,128)(2,1)}) %reduce-scatter.17.cloned.1.call-update) | async-done | bytes 655376 | tf_op jit(solution)/shard_map/while/body/eval_jaxpr/reduce_scatter | solution.py:50
  965.6 24.8 %all-gather.22.cloned.1.call-done = bf16[1024,1024]{1,0:T(8,128)(2,1)} async-done(((bf16[128,1024]{1,0:T(8,128)(2,1)}), bf16[1024,1024]{1,0:T(8,128)(2,1)}) %all-gather.22.cloned.1.call-update) | async-done | bytes 2097168 | tf_op jit(solution)/shard_map/while/body/eval_jaxpr/all_gather | solution.py:162
  990.3 57.0 %all-gather.20.cloned.1.call-done = bf16[20,64,1024]{2,1,0:T(8,128)(2,1)} async-done(((bf16[20,16,1024]{2,1,0:T(8,128)(2,1)}), bf16[20,64,1024]{2,1,0:T(8,128)(2,1)}) %all-gather.20.cloned.1.call-update) | async-done | bytes 2621456 | tf_op jit(solution)/shard_map/while/body/eval_jaxpr/all_gather | solution.py:46
  1056.6 19.4 all-gather.18.cloned.1.call-done
  1095.0 41.3 %reduce-scatter.19.cloned.1.call-done = bf16[20,16,1024]{2,1,0:T(8,128)(2,1)} async-done(((bf16[20,64,1024]{2,1,0:T(8,128)(2,1)}), bf16[20,16,1024]{2,1,0:T(8,128)(2,1)}) %reduce-scatter.19.cloned.1.call-update) | async-done | bytes 655376 | tf_op jit(solution)/shard_map/while/body/eval_jaxpr/reduce_scatter | solution.py:50
  1141.3 1060.3 %while.57 = (s32[]{:T(128)}, f32[128,3,256]{2,0,1:T(8,128)}, f32[128,256]{1,0:T(8,128)}, f32[128,1024]{1,0:T(8,128)}, f32[128,1024]{1,0:T(8,128)}, /*index=5*/f3...) while((s32[]{:T(128)}, f32[128,3,256]{2,0,1:T(8,128)}, ...), condition=%wide.region_39.40_spmd.clone, body=%wide.region_10.39_spmd.clone.sunk | while | flops 17337038848 | bytes 494624768 | solution.py:309
  1146.9 24.5 %all-gather.26.cloned.1.call-done = bf16[1024,1024]{1,0:T(8,128)(2,1)} async-done(((bf16[128,1024]{1,0:T(8,128)(2,1)}), bf16[1024,1024]{1,0:T(8,128)(2,1)}) %all-gather.26.cloned.1.call-update) | async-done | bytes 2097168 | tf_op jit(solution)/shard_map/while/body/eval_jaxpr/all_gather | solution.py:235
  1171.4 56.9 %all-gather.24.cloned.1.call-done = bf16[20,64,1024]{2,1,0:T(8,128)(2,1)} async-done(((bf16[20,16,1024]{2,1,0:T(8,128)(2,1)}), bf16[20,64,1024]{2,1,0:T(8,128)(2,1)}) %all-gather.24.cloned.1.call-update) | async-done | bytes 2621456 | tf_op jit(solution)/shard_map/while/body/eval_jaxpr/all_gather | solution.py:56
  1237.8 19.1 all-gather.28.cloned.1.call-done
  1265.6 49.5 %reduce-scatter.21.cloned.1.call-done = bf16[20,16,1024]{2,1,0:T(8,128)(2,1)} async-done(((bf16[20,64,1024]{2,1,0:T(8,128)(2,1)}), bf16[20,16,1024]{2,1,0:T(8,128)(2,1)}) %reduce-scatter.21.cloned.1.call-update) | async-done | bytes 655376 | tf_op jit(solution)/shard_map/while/body/eval_jaxpr/reduce_scatter | solution.py:60
  1460.7 52.8 %reduce-scatter.29.cloned.1.call-done = f32[128,1024]{1,0:T(8,128)} async-done(((f32[1024,1024]{1,0:T(8,128)}), f32[128,1024]{1,0:T(8,128)}) %reduce-scatter.29.cloned.1.call-update) | async-done | bytes 524304 | tf_op jit(solution)/shard_map/while/body/eval_jaxpr/reduce_scatter | solution.py:303
  1553.9 49.1 %reduce-scatter.23.cloned.1.call-done = f32[128,3,256]{2,0,1:T(8,128)} async-done(((f32[1024,3,256]{2,0,1:T(8,128)}), f32[128,3,256]{2,0,1:T(8,128)}) %reduce-scatter.23.cloned.1.call-update) | async-done | bytes 393232 | tf_op jit(solution)/shard_map/while/body/eval_jaxpr/reduce_scatter | solution.py:300
  1604.1 53.2 %reduce-scatter.31.cloned.1.call-done = bf16[20,16,1024]{2,1,0:T(8,128)(2,1)} async-done(((bf16[20,64,1024]{2,1,0:T(8,128)(2,1)}), bf16[20,16,1024]{2,1,0:T(8,128)(2,1)}) %reduce-scatter.31.cloned.1.call-update) | async-done | bytes 655376 | tf_op jit(solution)/shard_map/while/body/eval_jaxpr/reduce_scatter | solution.py:60
  1676.1 24.4 %all-gather.26.cloned.1.call-done = bf16[1024,1024]{1,0:T(8,128)(2,1)} async-done(((bf16[128,1024]{1,0:T(8,128)(2,1)}), bf16[1024,1024]{1,0:T(8,128)(2,1)}) %all-gather.26.cloned.1.call-update) | async-done | bytes 2097168 | tf_op jit(solution)/shard_map/while/body/eval_jaxpr/all_gather | solution.py:235
  1700.5 57.0 %all-gather.24.cloned.1.call-done = bf16[20,64,1024]{2,1,0:T(8,128)(2,1)} async-done(((bf16[20,16,1024]{2,1,0:T(8,128)(2,1)}), bf16[20,64,1024]{2,1,0:T(8,128)(2,1)}) %all-gather.24.cloned.1.call-update) | async-done | bytes 2621456 | tf_op jit(solution)/shard_map/while/body/eval_jaxpr/all_gather | solution.py:56
  1767.0 19.3 all-gather.28.cloned.1.call-done
  1794.9 49.5 %reduce-scatter.21.cloned.1.call-done = bf16[20,16,1024]{2,1,0:T(8,128)(2,1)} async-done(((bf16[20,64,1024]{2,1,0:T(8,128)(2,1)}), bf16[20,16,1024]{2,1,0:T(8,128)(2,1)}) %reduce-scatter.21.cloned.1.call-update) | async-done | bytes 655376 | tf_op jit(solution)/shard_map/while/body/eval_jaxpr/reduce_scatter | solution.py:60
  1990.0 52.7 %reduce-scatter.29.cloned.1.call-done = f32[128,1024]{1,0:T(8,128)} async-done(((f32[1024,1024]{1,0:T(8,128)}), f32[128,1024]{1,0:T(8,128)}) %reduce-scatter.29.cloned.1.call-update) | async-done | bytes 524304 | tf_op jit(solution)/shard_map/while/body/eval_jaxpr/reduce_scatter | solution.py:303
  2083.2 48.9 %reduce-scatter.23.cloned.1.call-done = f32[128,3,256]{2,0,1:T(8,128)} async-done(((f32[1024,3,256]{2,0,1:T(8,128)}), f32[128,3,256]{2,0,1:T(8,128)}) %reduce-scatter.23.cloned.1.call-update) | async-done | bytes 393232 | tf_op jit(solution)/shard_map/while/body/eval_jaxpr/reduce_scatter | solution.py:300
  2133.3 53.2 %reduce-scatter.31.cloned.1.call-done = bf16[20,16,1024]{2,1,0:T(8,128)(2,1)} async-done(((bf16[20,64,1024]{2,1,0:T(8,128)(2,1)}), bf16[20,16,1024]{2,1,0:T(8,128)(2,1)}) %reduce-scatter.31.cloned.1.call-update) | async-done | bytes 655376 | tf_op jit(solution)/shard_map/while/body/eval_jaxpr/reduce_scatter | solution.py:60
  2204.2 35.5 %reduce-scatter.15.cloned.1.call-done = bf16[1536,4]{1,0:T(8,128)(2,1)} async-done(((bf16[6144,4]{1,0:T(8,128)(2,1)}), bf16[1536,4]{1,0:T(8,128)(2,1)}) %reduce-scatter.15.cloned.1.call-update) | async-done | bytes 12304
  2244.5 25.4 %psum.15 = f32[4,2025]{1,0:T(4,128)} all-reduce(f32[4,2025]{1,0:T(4,128)} %get-tuple-element.701), channel_id=1, replica_groups=mesh['dp'=8,'tensor'=4] {'dp'}, use_global_device_ids=true, to_apply=%region_43.44 | all-reduce | flops 8100 | bytes 64800 | tf_op jit(solution)/shard_map/psum | solution.py:312
  (655 shorter events, 736.1 us)
Async XLA Ops:
  7.2 376.0 %all-gather.12.cloned.1.call-start = ((), (), s32[]{:S(2)}) async-start(), calls=%async_computation.10 | async-start | bytes 3538944 | tf_op jit(solution)/shard_map/all_gather | solution.py:136
  418.5 87.1 %all-gather.16.cloned.1.call-start = ((), (), s32[]{:S(2)}) async-start(), calls=%async_computation.14 | async-start | bytes 3276800 | tf_op jit(solution)/shard_map/while/body/eval_jaxpr/all_gather | solution.py:46
  425.7 174.9 %reduce-scatter.17.cloned.1.call-start = ((), (), s32[]{:S(2)}) async-start(), calls=%async_computation.15 | async-start | bytes 3276800 | tf_op jit(solution)/shard_map/while/body/eval_jaxpr/reduce_scatter | solution.py:50
  550.2 136.9 %all-gather.20.cloned.1.call-start = ((), (), s32[]{:S(2)}) async-start(), calls=%async_computation.17 | async-start | bytes 3276800 | tf_op jit(solution)/shard_map/while/body/eval_jaxpr/all_gather | solution.py:46
  604.8 111.0 %all-gather.18.cloned.1.call-start = ((), (), s32[]{:S(2)}) async-start(), calls=%async_computation.16 | async-start | bytes 2359296 | tf_op jit(solution)/shard_map/while/body/eval_jaxpr/all_gather | solution.py:163
  605.5 170.5 %reduce-scatter.19.cloned.1.call-start = ((), (), s32[]{:S(2)}) async-start(), calls=%async_computation.19 | async-start | bytes 3276800 | tf_op jit(solution)/shard_map/while/body/eval_jaxpr/reduce_scatter | solution.py:50
  780.6 85.1 %all-gather.16.cloned.1.call-start = ((), (), s32[]{:S(2)}) async-start(), calls=%async_computation.14 | async-start | bytes 3276800 | tf_op jit(solution)/shard_map/while/body/eval_jaxpr/all_gather | solution.py:46
  787.8 173.0 %reduce-scatter.17.cloned.1.call-start = ((), (), s32[]{:S(2)}) async-start(), calls=%async_computation.15 | async-start | bytes 3276800 | tf_op jit(solution)/shard_map/while/body/eval_jaxpr/reduce_scatter | solution.py:50
  910.3 137.0 %all-gather.20.cloned.1.call-start = ((), (), s32[]{:S(2)}) async-start(), calls=%async_computation.17 | async-start | bytes 3276800 | tf_op jit(solution)/shard_map/while/body/eval_jaxpr/all_gather | solution.py:46
  965.0 111.0 %all-gather.18.cloned.1.call-start = ((), (), s32[]{:S(2)}) async-start(), calls=%async_computation.16 | async-start | bytes 2359296 | tf_op jit(solution)/shard_map/while/body/eval_jaxpr/all_gather | solution.py:163
  965.5 170.7 %reduce-scatter.19.cloned.1.call-start = ((), (), s32[]{:S(2)}) async-start(), calls=%async_computation.19 | async-start | bytes 3276800 | tf_op jit(solution)/shard_map/while/body/eval_jaxpr/reduce_scatter | solution.py:50
  1141.9 86.5 %all-gather.24.cloned.1.call-start = ((), (), s32[]{:S(2)}) async-start(), calls=%async_computation.20 | async-start | bytes 3276800 | tf_op jit(solution)/shard_map/while/body/eval_jaxpr/all_gather | solution.py:56
  1146.3 110.6 %all-gather.28.cloned.1.call-start = ((), (), s32[]{:S(2)}) async-start(), calls=%async_computation.22 | async-start | bytes 2359296 | tf_op jit(solution)/shard_map/while/body/eval_jaxpr/all_gather | solution.py:234
  1146.9 168.2 %reduce-scatter.21.cloned.1.call-start = ((), (), s32[]{:S(2)}) async-start(), calls=%async_computation.23 | async-start | bytes 3276800 | tf_op jit(solution)/shard_map/while/body/eval_jaxpr/reduce_scatter | solution.py:60
  1262.8 114.3 %all-gather.30.cloned.1.call-start = ((), (), s32[]{:S(2)}) async-start(), calls=%async_computation.24 | async-start | bytes 3276800 | tf_op jit(solution)/shard_map/while/body/eval_jaxpr/all_gather | solution.py:56
  1322.5 115.7 %all-gather.32.cloned.1.call-start = ((), (), s32[]{:S(2)}) async-start(), calls=%async_computation.29 | async-start | bytes 1769472 | tf_op jit(solution)/shard_map/while/body/eval_jaxpr/all_gather | solution.py:232
  1323.2 135.6 %reduce-scatter.27.cloned.1.call-start = ((), (), s32[]{:S(2)}) async-start(), calls=%async_computation.27 | async-start | bytes 4718592 | tf_op jit(solution)/shard_map/while/body/eval_jaxpr/reduce_scatter | solution.py:302
  1329.6 183.9 %reduce-scatter.29.cloned.1.call-start = ((), (), s32[]{:S(2)}) async-start(), calls=%async_computation.28 | async-start | bytes 4718592 | tf_op jit(solution)/shard_map/while/body/eval_jaxpr/reduce_scatter | solution.py:303
  1339.0 213.9 %reduce-scatter.25.cloned.1.call-start = ((), (), s32[]{:S(2)}) async-start(), calls=%async_computation.26 | async-start | bytes 1179648 | tf_op jit(solution)/shard_map/while/body/eval_jaxpr/reduce_scatter | solution.py:301
  1425.0 177.9 %reduce-scatter.23.cloned.1.call-start = ((), (), s32[]{:S(2)}) async-start(), calls=%async_computation.25 | async-start | bytes 3538944 | tf_op jit(solution)/shard_map/while/body/eval_jaxpr/reduce_scatter | solution.py:300
  1438.1 219.1 %reduce-scatter.31.cloned.1.call-start = ((), (), s32[]{:S(2)}) async-start(), calls=%async_computation.30 | async-start | bytes 3276800 | tf_op jit(solution)/shard_map/while/body/eval_jaxpr/reduce_scatter | solution.py:60
  1670.9 86.6 %all-gather.24.cloned.1.call-start = ((), (), s32[]{:S(2)}) async-start(), calls=%async_computation.20 | async-start | bytes 3276800 | tf_op jit(solution)/shard_map/while/body/eval_jaxpr/all_gather | solution.py:56
  1675.3 111.0 %all-gather.28.cloned.1.call-start = ((), (), s32[]{:S(2)}) async-start(), calls=%async_computation.22 | async-start | bytes 2359296 | tf_op jit(solution)/shard_map/while/body/eval_jaxpr/all_gather | solution.py:234
  1676.1 168.3 %reduce-scatter.21.cloned.1.call-start = ((), (), s32[]{:S(2)}) async-start(), calls=%async_computation.23 | async-start | bytes 3276800 | tf_op jit(solution)/shard_map/while/body/eval_jaxpr/reduce_scatter | solution.py:60
  1792.1 114.3 %all-gather.30.cloned.1.call-start = ((), (), s32[]{:S(2)}) async-start(), calls=%async_computation.24 | async-start | bytes 3276800 | tf_op jit(solution)/shard_map/while/body/eval_jaxpr/all_gather | solution.py:56
  1851.8 115.7 %all-gather.32.cloned.1.call-start = ((), (), s32[]{:S(2)}) async-start(), calls=%async_computation.29 | async-start | bytes 1769472 | tf_op jit(solution)/shard_map/while/body/eval_jaxpr/all_gather | solution.py:232
  1852.6 135.4 %reduce-scatter.27.cloned.1.call-start = ((), (), s32[]{:S(2)}) async-start(), calls=%async_computation.27 | async-start | bytes 4718592 | tf_op jit(solution)/shard_map/while/body/eval_jaxpr/reduce_scatter | solution.py:302
  1858.9 183.8 %reduce-scatter.29.cloned.1.call-start = ((), (), s32[]{:S(2)}) async-start(), calls=%async_computation.28 | async-start | bytes 4718592 | tf_op jit(solution)/shard_map/while/body/eval_jaxpr/reduce_scatter | solution.py:303
  1868.3 213.9 %reduce-scatter.25.cloned.1.call-start = ((), (), s32[]{:S(2)}) async-start(), calls=%async_computation.26 | async-start | bytes 1179648 | tf_op jit(solution)/shard_map/while/body/eval_jaxpr/reduce_scatter | solution.py:301
  1954.2 178.0 %reduce-scatter.23.cloned.1.call-start = ((), (), s32[]{:S(2)}) async-start(), calls=%async_computation.25 | async-start | bytes 3538944 | tf_op jit(solution)/shard_map/while/body/eval_jaxpr/reduce_scatter | solution.py:300
  1967.5 219.0 %reduce-scatter.31.cloned.1.call-start = ((), (), s32[]{:S(2)}) async-start(), calls=%async_computation.30 | async-start | bytes 3276800 | tf_op jit(solution)/shard_map/while/body/eval_jaxpr/reduce_scatter | solution.py:60
  2204.2 101.1 %reduce-scatter.13.cloned.1.call-start = ((), (), s32[]{:S(2)}) async-start(), calls=%async_computation.11 | async-start | bytes 7077888 | tf_op jit(solution)/shard_map/reduce_scatter | solution.py:320
  (114 other events, 2168.5 us)
Sparse Core Ops, SparseCore 0:
  9.9 35.0 all-gather.11
  420.6 27.8 all-gather.13
  450.8 54.7 all-gather.15
  549.7 50.9 reduce-scatter.16
  602.5 27.5 all-gather.21
  632.2 54.7 all-gather.19
  723.9 52.0 reduce-scatter.18
  810.9 54.7 all-gather.15
  909.9 50.9 reduce-scatter.16
  962.7 27.5 all-gather.21
  992.6 54.7 all-gather.19
  1084.1 52.1 reduce-scatter.18
  1143.8 27.5 all-gather.25
  1173.5 54.7 all-gather.23
  1262.9 52.0 reduce-scatter.20
  1322.6 54.4 all-gather.29
  1407.4 51.3 reduce-scatter.26
  1462.2 51.3 reduce-scatter.28
  1516.9 35.9 reduce-scatter.24
  1556.7 46.2 reduce-scatter.22
  1605.1 52.0 reduce-scatter.30
  1672.9 27.5 all-gather.25
  1702.7 54.7 all-gather.23
  1792.2 52.0 reduce-scatter.20
  1852.0 54.4 all-gather.29
  1936.6 51.3 reduce-scatter.26
  1991.3 51.3 reduce-scatter.28
  2046.2 36.0 reduce-scatter.24
  2085.9 46.2 reduce-scatter.22
  2134.3 52.0 reduce-scatter.30
  2204.7 34.9 reduce-scatter.14
  2244.6 60.6 reduce-scatter.12
  (7 shorter events, 181.5 us)
where the time goes:
time: 2310 us
  waiting for transfers between devices  1230 us (53%)
  local copies, waits for them, and re-layouts  593 us (26%)
  matrix products  247 us (11%)
  other arithmetic  104 us (5%)
  blocking collectives  102 us (4%)
    gather x2, local copies, waits for them, and re-layouts, body(): pos_bias = pos_table[:, offsets]  372 us
    all_gather x4, waiting for transfers between devices, gather_tokens(): return lax.all_gather(local_rows, 'tensor', axis=1, tiled=True)  228 us
    reduce_scatter x4, waiting for transfers between devices, sum_grads(): lax.psum_scatter(partial_sum.astype(jnp.bfloat16), 'tensor', scatter_dime...  205 us
    reduce_scatter x4, waiting for transfers between devices, sum_tokens(): lax.psum_scatter(partial_sum.astype(jnp.bfloat16), 'tensor', scatter_dime...  183 us
    all_gather x4, waiting for transfers between devices, gather_grads(): return lax.all_gather(local_rows, 'tensor', axis=1, tiled=True)  139 us
    reduce_scatter x2, waiting for transfers between devices, backward_step(): lax.psum_scatter(grad_down, 'dp', scatter_dimension=0, tiled=True)  105 us
    reduce_scatter x2, waiting for transfers between devices, backward_step(): lax.psum_scatter(grad_inproj, 'dp', scatter_dimension=0, tiled=True)  98 us
    while x236, local copies, waits for them, and re-layouts  63.3 us
  transfers between devices with their start and end apart: 39, of which 36 were waited for; matrix products, arithmetic and copies ran while one was open for 32% of the time, Pallas kernels for 0%

commit v1 on v0

v1 whole, which is shorter than its diff:
```python
import functools

import jax
import jax.numpy as jnp
import numpy as np
from jax import lax
from jax.experimental import pallas as pl
from jax.experimental.pallas import tpu as pltpu
from jax.sharding import PartitionSpec as P

HEAD_DIM = 64
WIN_T = 5
WIN_S = 8
FRAMES = 10
SPATIAL = 64
OFFSETS = 2025

EPSILON = 1e-06
NEGATIVE = -1e30
HIGHEST = lax.Precision.HIGHEST
BF = jnp.bfloat16
F32 = jnp.float32
WINDOWS = FRAMES // WIN_T
WIN_LEN = WIN_T * SPATIAL
SPREAD = 2 * WIN_T - 1
DIAG = SPREAD * SPATIAL


def stage_bits(n_dp, core):
    bits = list(range(1, n_dp.bit_length() - 1))
    return bits if core == 0 else bits[::-1]


def stage_perm(n_dp, stage):
    return [(i, i ^ (1 << stage_bits(n_dp, i & 1)[stage])) for i in range(n_dp)]


def core_perm(n_dp):
    return [(i, i ^ 1) for i in range(n_dp)]


def ring(count, step):
    return [(i, (i + step) % count) for i in range(count)]


def stages(n_dp):
    return n_dp.bit_length() - 2


def dp_order(n_dp):
    half = n_dp // 2

    def mask(core, place):
        return sum(1 << b for t, b in enumerate(stage_bits(n_dp, core)) if place >> t & 1)

    return np.array(
        [[mask(c, k) for k in range(half)] + [1 ^ mask(1 - c, k) for k in range(half)] for c in (0, 1)],
        np.int32,
    )


def gather_weight(shard, n_dp, n_z):
    blocks = [shard]
    for _ in range(n_z - 1):
        blocks.append(lax.ppermute(blocks[-1], "tensor", ring(n_z, 1)))
    pieces = [jnp.concatenate(blocks, axis=1)]
    for t in range(stages(n_dp)):
        pieces = pieces + [lax.ppermute(p, "dp", stage_perm(n_dp, t)) for p in pieces]
    pieces = pieces + [lax.ppermute(p, "dp", core_perm(n_dp)) for p in pieces]
    return jnp.concatenate(pieces, axis=0)


def add_low(first, second):
    return (first.astype(F32) + second.astype(F32)).astype(BF)


def scatter_grad(grad, n_dp, n_z):
    rows = grad.shape[0] // n_dp
    pieces = [grad[i * rows : (i + 1) * rows] for i in range(n_dp)]
    for t in range(stages(n_dp), -1, -1):
        half = len(pieces) // 2
        perm = core_perm(n_dp) if t == stages(n_dp) else stage_perm(n_dp, t)
        got = [lax.ppermute(p, "dp", perm) for p in pieces[half:]]
        pieces = [add_low(a, b) for a, b in zip(pieces[:half], got)]
    width = grad.shape[1] // n_z
    part = [pieces[0][:, r * width : (r + 1) * width] for r in range(n_z)]
    total = part[n_z - 1]
    for r in range(n_z - 2, -1, -1):
        total = lax.ppermute(total, "tensor", ring(n_z, -1))
        total = add_low(part[r], total) if r else part[r].astype(F32) + total.astype(F32)
    return total


def shifted(pieces, n_z, sign):
    return [pieces[0]] + [lax.ppermute(pieces[r], "tensor", ring(n_z, sign * r)) for r in range(1, n_z)]


def butterfly_sum(value, axis, count):
    bit = 1
    while bit < count:
        value = value + lax.ppermute(value, axis, [(i, i ^ bit) for i in range(count)])
        bit *= 2
    return value


def pair_onehot():
    span = 2 * WIN_S - 1
    place = jnp.arange(SPATIAL)
    row, col = place // WIN_S, place % WIN_S
    offset = (row[:, None] - row[None, :] + WIN_S - 1) * span + (col[:, None] - col[None, :] + WIN_S - 1)
    return (jnp.arange(span * span)[:, None] == offset.reshape(1, -1)).astype(F32)


def spread_bias(table):
    heads = table.shape[0]
    rows = table.reshape(heads, SPREAD, -1)[:, ::-1].reshape(heads * SPREAD, -1)
    flat = jnp.dot(rows, pair_onehot(), precision=HIGHEST)
    flat = flat.reshape(heads, SPREAD, SPATIAL, SPATIAL)
    return flat.transpose(0, 2, 1, 3).reshape(heads, SPATIAL, DIAG)


def fold_bias(diag):
    heads = diag.shape[0]
    rows = diag.reshape(heads, SPATIAL, SPREAD, SPATIAL).transpose(0, 2, 1, 3)
    rows = rows.reshape(heads * SPREAD, SPATIAL * SPATIAL)
    folded = lax.dot_general(rows, pair_onehot(), (((1,), (1,)), ((), ())), precision=HIGHEST)
    return folded.reshape(heads, SPREAD, -1)[:, ::-1].reshape(heads, OFFSETS)


def dot_nt(a, b):
    return lax.dot_general(a, b, (((1,), (1,)), ((), ())), preferred_element_type=F32)


def dot_tn(a, b):
    return lax.dot_general(a, b, (((0,), (0,)), ((), ())), preferred_element_type=F32)


def attend_kernel(heads, count_ref, qkv_ref, bias_ref, att_ref, prob_ref):
    width = heads * HEAD_DIM
    live = (count_ref[0] - pl.program_id(1) * WIN_T) * SPATIAL
    key_live = lax.broadcasted_iota(jnp.int32, (WIN_LEN, WIN_LEN), 1) < live
    row_live = lax.broadcasted_iota(jnp.int32, (WIN_LEN, HEAD_DIM), 0) < live
    for h in range(heads):
        low = h * HEAD_DIM
        q = qkv_ref[:, low : low + HEAD_DIM]
        k = qkv_ref[:, width + low : width + low + HEAD_DIM]
        v = qkv_ref[:, 2 * width + low : 2 * width + low + HEAD_DIM]
        bias = jnp.concatenate(
            [bias_ref[h, :, (WIN_T - 1 - a) * SPATIAL : (WIN_T - 1 - a) * SPATIAL + WIN_LEN] for a in range(WIN_T)],
            axis=0,
        )
        scores = jnp.where(key_live, dot_nt(q, k) * HEAD_DIM**-0.5 + bias, NEGATIVE)
        top = jnp.max(scores, axis=1, keepdims=True)
        expo = jnp.where(key_live, jnp.exp(scores - top), 0.0)
        total = jnp.maximum(jnp.sum(expo, axis=1, keepdims=True), 1.0)
        probs = (expo * (1.0 / total)).astype(BF)
        prob_ref[0, h] = probs
        att = jnp.dot(probs, v, preferred_element_type=F32)
        att_ref[:, low : low + HEAD_DIM] = jnp.where(row_live, att, 0.0).astype(BF)


def attend_back_kernel(heads, count_ref, qkv_ref, prob_ref, gatt_ref, gqkv_ref, diag_ref):
    width = heads * HEAD_DIM
    live = (count_ref[0] - pl.program_id(1) * WIN_T) * SPATIAL
    row_live = lax.broadcasted_iota(jnp.int32, (WIN_LEN, HEAD_DIM), 0) < live

    @pl.when(pl.program_id(1) == 0)
    def _():
        diag_ref[...] = jnp.zeros_like(diag_ref)

    for h in range(heads):
        low = h * HEAD_DIM
        q = qkv_ref[:, low : low + HEAD_DIM]
        k = qkv_ref[:, width + low : width + low + HEAD_DIM]
        v = qkv_ref[:, 2 * width + low : 2 * width + low + HEAD_DIM]
        gatt = gatt_ref[:, low : low + HEAD_DIM]
        gatt = jnp.where(row_live, gatt, jnp.zeros_like(gatt))
        probs = prob_ref[0, h]
        full = probs.astype(F32)
        gvalues = dot_tn(probs, gatt)
        gprobs = dot_nt(gatt, v)
        inner = jnp.sum(full * gprobs, axis=1, keepdims=True)
        gscores = (full * (gprobs - inner)).astype(BF)
        gq = jnp.dot(gscores, k, preferred_element_type=F32) * HEAD_DIM**-0.5
        gk = dot_tn(gscores, q) * HEAD_DIM**-0.5
        gqkv_ref[:, low : low + HEAD_DIM] = gq.astype(BF)
        gqkv_ref[:, width + low : width + low + HEAD_DIM] = gk.astype(BF)
        gqkv_ref[:, 2 * width + low : 2 * width + low + HEAD_DIM] = gvalues.astype(BF)
        wide = gscores.astype(F32)
        for a in range(WIN_T):
            at = (WIN_T - 1 - a) * SPATIAL
            diag_ref[h, :, at : at + WIN_LEN] += wide[a * SPATIAL : (a + 1) * SPATIAL]


def attend(count, qkv, bias, n_z):
    heads = bias.shape[0] // n_z
    width = heads * HEAD_DIM
    return pl.pallas_call(
        functools.partial(attend_kernel, heads),
        grid_spec=pltpu.PrefetchScalarGridSpec(
            num_scalar_prefetch=1,
            grid=(n_z, WINDOWS),
            in_specs=[
                pl.BlockSpec((WIN_LEN, 3 * width), lambda r, w, c: (w, r)),
                pl.BlockSpec((heads, SPATIAL, DIAG), lambda r, w, c: (r, 0, 0)),
            ],
            out_specs=[
                pl.BlockSpec((WIN_LEN, width), lambda r, w, c: (w, r)),
                pl.BlockSpec((1, heads, WIN_LEN, WIN_LEN), lambda r, w, c: (w, r, 0, 0)),
            ],
        ),
        out_shape=[
            jax.ShapeDtypeStruct((WINDOWS * WIN_LEN, n_z * width), BF),
            jax.ShapeDtypeStruct((WINDOWS, n_z * heads, WIN_LEN, WIN_LEN), BF),
        ],
        compiler_params=pltpu.CompilerParams(vmem_limit_bytes=32 << 20),
        cost_estimate=pl.CostEstimate(flops=2 * 10**9, bytes_accessed=14 * 10**6, transcendentals=3 * 10**6),
        name="attend",
    )(count, qkv, bias)


def attend_back(count, qkv, probs, gatt, n_z):
    heads = probs.shape[1] // n_z
    width = heads * HEAD_DIM
    return pl.pallas_call(
        functools.partial(attend_back_kernel, heads),
        grid_spec=pltpu.PrefetchScalarGridSpec(
            num_scalar_prefetch=1,
            grid=(n_z, WINDOWS),
            in_specs=[
                pl.BlockSpec((WIN_LEN, 3 * width), lambda r, w, c: (w, r)),
                pl.BlockSpec((1, heads, WIN_LEN, WIN_LEN), lambda r, w, c: (w, r, 0, 0)),
                pl.BlockSpec((WIN_LEN, width), lambda r, w, c: (w, r)),
            ],
            out_specs=[
                pl.BlockSpec((WIN_LEN, 3 * width), lambda r, w, c: (w, r)),
                pl.BlockSpec((heads, SPATIAL, DIAG), lambda r, w, c: (r, 0, 0)),
            ],
        ),
        out_shape=[
            jax.ShapeDtypeStruct((WINDOWS * WIN_LEN, n_z * 3 * width), BF),
            jax.ShapeDtypeStruct((n_z * heads, SPATIAL, DIAG), F32),
        ],
        compiler_params=pltpu.CompilerParams(vmem_limit_bytes=32 << 20),
        cost_estimate=pl.CostEstimate(flops=5 * 10**9, bytes_accessed=18 * 10**6, transcendentals=0),
        name="attend_back",
    )(count, qkv, probs, gatt)


def normalize(values):
    center = values - jnp.mean(values, axis=-1, keepdims=True)
    scale = lax.rsqrt(jnp.mean(center * center, axis=-1, keepdims=True) + EPSILON)
    return center * scale, scale


def norm_back(normed, inv_sigma, scale_row, grad):
    u = (1.0 + scale_row) * grad
    return (u - jnp.mean(u, axis=-1, keepdims=True) - normed * jnp.mean(u * normed, axis=-1, keepdims=True)) * inv_sigma


def gelu_slope(v):
    c = np.float32(np.sqrt(2 / np.pi))
    t = jnp.tanh(c * (v + 0.044715 * v * v * v))
    return 0.5 * (1.0 + t) + 0.5 * v * (1.0 - t * t) * c * (1.0 + 3 * 0.044715 * v * v)


def dot(a, b):
    return jnp.dot(a, b, preferred_element_type=F32)


def body(
    n_dp, n_z, tokens, conditioning, frame_counts, w_qkv, w_out, w_up, w_down, w_ada, pos_table, cotangent
):
    micro, clip_dev, _, part, model = tokens.shape
    clips = micro * clip_dev
    assert clips == n_z and part * n_z == SPATIAL
    feature = model // n_dp
    d, z = lax.axis_index("dp"), lax.axis_index("tensor")
    count = lax.dynamic_slice_in_dim(frame_counts.reshape(clips), z, 1)

    order = jnp.asarray(dp_order(n_dp))[d & 1] ^ d
    source = (order[:, None] * feature + jnp.arange(feature)[None, :]).reshape(1, model)
    to_place = (jnp.arange(model)[:, None] == source).astype(BF)

    def placed(rows):
        return dot(rows, to_place).astype(BF)

    def unplaced(rows):
        return dot_nt(rows.astype(BF), to_place).astype(BF)

    def to_clip(rows):
        got = lax.all_to_all(rows.reshape(clips, FRAMES, part, model), "tensor", 0, 0, tiled=True)
        return got.transpose(1, 0, 2, 3).reshape(FRAMES * SPATIAL, model)

    def from_clip(rows):
        parts = rows.reshape(FRAMES, n_z, part, model).transpose(1, 0, 2, 3)
        return lax.all_to_all(parts, "tensor", 0, 0, tiled=True).reshape(tokens.shape)

    cond_float = conditioning.astype(F32).reshape(clips, model)
    cond_act = jax.nn.silu(cond_float).astype(BF)
    cond_mine = lax.all_to_all(
        cond_act.reshape(clips, n_dp, feature).transpose(1, 0, 2), "dp", 0, 0, tiled=True
    ).reshape(n_dp * clips, feature)
    mod_part = lax.all_to_all(dot(cond_mine, w_ada), ("dp", "tensor"), 0, 0, tiled=True)
    mods = jnp.sum(mod_part.reshape(n_dp, n_z, -1), axis=0).reshape(6, model)
    mods = jnp.dot(mods, to_place.astype(F32), precision=HIGHEST).reshape(6, 1, model)

    wq = gather_weight(w_qkv.reshape(feature, -1), n_dp, n_z)
    wo = gather_weight(w_out, n_dp, n_z)
    wu = gather_weight(w_up, n_dp, n_z)
    wd = gather_weight(w_down, n_dp, n_z)

    bias = spread_bias(jnp.concatenate(shifted([pos_table] * n_z, n_z, 1), axis=0))

    resid = placed(to_clip(tokens)).astype(F32)
    norm_a, inv_a = normalize(resid)
    normed_a = (norm_a * (1.0 + mods[1]) + mods[0]).astype(BF)
    qkv = dot(normed_a, wq).astype(BF)
    attended, probs = attend(count, qkv, bias, n_z)
    branch_a = dot_nt(attended, wo)
    middle = resid + mods[2] * branch_a
    norm_b, inv_b = normalize(middle)
    normed_b = (norm_b * (1.0 + mods[4]) + mods[3]).astype(BF)
    hidden = dot(normed_b, wu)
    activ = jax.nn.gelu(hidden).astype(BF)
    slope = gelu_slope(hidden).astype(BF)
    grad_result = placed(to_clip(cotangent)).astype(F32)
    grad_bb = (grad_result * mods[5]).astype(BF)
    grad_down = dot_tn(grad_bb, activ).astype(BF)
    out_down = scatter_grad(grad_down, n_dp, n_z)
    branch_b = dot_nt(activ, wd)
    block_out = from_clip(unplaced(middle + mods[5] * branch_b))

    grad_gate_b = jnp.sum(grad_result * branch_b, axis=0)
    grad_hidden = (dot(grad_bb, wd) * slope.astype(F32)).astype(BF)
    grad_up = dot_tn(normed_b, grad_hidden).astype(BF)
    out_up = scatter_grad(grad_up, n_dp, n_z)
    grad_nb = dot_nt(grad_hidden, wu)
    grad_shift_b = jnp.sum(grad_nb, axis=0)
    grad_scale_b = jnp.sum(grad_nb * norm_b, axis=0)
    grad_middle = grad_result + norm_back(norm_b, inv_b, mods[4], grad_nb)
    grad_ba = (grad_middle * mods[2]).astype(BF)
    grad_gate_a = jnp.sum(grad_middle * branch_a, axis=0)
    grad_out = dot_tn(grad_ba, attended).astype(BF)
    out_out = scatter_grad(grad_out, n_dp, n_z)
    grad_att = dot(grad_ba, wo).astype(BF)
    grad_qkv, diag = attend_back(count, qkv, probs, grad_att, n_z)
    grad_in = dot_tn(normed_a, grad_qkv).astype(BF)
    out_qkv = scatter_grad(grad_in, n_dp, n_z)
    grad_na = dot_nt(grad_qkv, wq)
    grad_shift_a = jnp.sum(grad_na, axis=0)
    grad_scale_a = jnp.sum(grad_na * norm_a, axis=0)
    grad_tokens = from_clip(unplaced(grad_middle + norm_back(norm_a, inv_a, mods[1], grad_na)))

    table = fold_bias(diag)
    heads = table.shape[0] // n_z
    own = shifted([table[r * heads : (r + 1) * heads] for r in range(n_z)], n_z, -1)
    grad_table = butterfly_sum(functools.reduce(lambda a, b: a + b, own), "dp", n_dp)

    grad_mod = jnp.stack([grad_shift_a, grad_scale_a, grad_gate_a, grad_shift_b, grad_scale_b, grad_gate_b])
    grad_mod = unplaced(grad_mod).reshape(1, n_z, -1)
    grad_mod = jnp.broadcast_to(grad_mod, (n_dp,) + grad_mod.shape[1:]).reshape(n_dp * n_z, -1)
    mod_cols = lax.all_to_all(grad_mod, ("dp", "tensor"), 0, 0, tiled=True)
    grad_ada = dot_tn(cond_mine, mod_cols)
    act_part = dot_nt(mod_cols, w_ada).reshape(n_dp, clips, feature)
    act_part = lax.all_to_all(act_part, "dp", 0, 0, tiled=True)
    grad_act = butterfly_sum(act_part, "tensor", n_z).transpose(1, 0, 2).reshape(clips, model)
    grad_cond = jax.vjp(jax.nn.silu, cond_float)[1](grad_act)[0].reshape(conditioning.shape)
    return (
        block_out,
        grad_tokens,
        grad_cond,
        out_qkv.reshape(w_qkv.shape),
        out_out,
        out_up,
        out_down,
        grad_ada,
        grad_table,
    )


def solution(mesh):
    rows = P(None, "dp", None, "tensor", None)
    weight = P("dp", "tensor")
    qkv_weight = P("dp", None, "tensor")
    cond = P(None, "dp", None)
    table = P("tensor", None)
    return jax.shard_map(
        functools.partial(body, mesh.shape["dp"], mesh.shape["tensor"]),
        mesh=mesh,
        in_specs=(rows, cond, P(None, "dp"), qkv_weight, weight, weight, weight, weight, table, rows),
        out_specs=(rows, rows, cond, qkv_weight, weight, weight, weight, weight, table),
        check_vma=False,
    )
```

time: 2310 us -> 683 us (0.30)
  waiting for transfers between devices: 1230 us -> 188 us
  local copies, waits for them, and re-layouts: 593 us -> 119 us
  starting transfers between devices: 2.52 us -> 146 us
  matrix products: 247 us -> 124 us
  blocking collectives: 102 us -> 0 us
  other arithmetic: 104 us -> 52.8 us
  Pallas kernels: 0 us -> 42.2 us
    reduce_scatter x17 -> x0, waiting for transfers between devices: 626 us -> none  [the longest x4 205 us: sum_grads(): lax.psum_scatter(partial_sum.astype(jnp.bfloat16), 'tensor', scatter_dime...]
    all_gather x21 -> x0, waiting for transfers between devices: 559 us -> none  [the longest x4 228 us: gather_tokens(): return lax.all_gather(local_rows, 'tensor', axis=1, tiled=True)]
    gather x2 -> x0, local copies, waits for them, and re-layouts: 372 us -> none  [body(): pos_bias = pos_table[:, offsets]]
    ppermute x0 -> x91, waiting for transfers between devices: none -> 176 us  [the longest x12 56 us: gather_weight(): lax.ppermute(p, 'dp', stage_perm(n_dp, t))]
    dot_general x47 -> x23, matrix products: 247 us -> 124 us  [the longest x8 42.9 us: dot_nt(): lax.dot_general(a, b, (((1,), (1,)), ((), ())), preferred_element_type=F32)]
    ppermute x0 -> x91, starting transfers between devices: none -> 106 us  [the longest x12 38.7 us: scatter_grad(): total = lax.ppermute(total, 'tensor', ring(n_z, -1))]
    while x236 -> x0, local copies, waits for them, and re-layouts: 63.3 us -> none
    reshape x31 -> x9, local copies, waits for them, and re-layouts: 71.4 us -> 9.81 us  [the longest x1 4.07 us: spread_bias(): return flat.transpose(0, 2, 1, 3).reshape(heads, SPATIAL, DIAG)]
  transfers between devices with their start and end apart: 39 -> 99, of which waited for: 36 -> 27; matrix products, arithmetic and copies ran while one was open for 32% -> 31% of each run, Pallas kernels for 0% -> 3%
where the time goes in v1:
time: 683 us; the launch traced here: 674 us
  waiting for transfers between devices  188 us (28%)
  starting transfers between devices  146 us (21%)
  matrix products  124 us (18%)
  local copies, waits for them, and re-layouts  119 us (17%)
  other arithmetic  52.8 us (8%)
  Pallas kernels  42.2 us (6%)
    ppermute x12, waiting for transfers between devices, gather_weight(): lax.ppermute(p, 'dp', stage_perm(n_dp, t))  56 us
    ppermute x28, waiting for transfers between devices, scatter_grad(): got = [lax.ppermute(p, 'dp', perm) for p in pieces[half:]]  54.2 us
    unnamed x131, local copies, waits for them, and re-layouts  53.8 us
    dot_general x8, matrix products, dot_nt(): lax.dot_general(a, b, (((1,), (1,)), ((), ())), preferred_element_type=F32)  42.9 us
    dot_general x7, matrix products, dot(): return jnp.dot(a, b, preferred_element_type=F32)  39 us
    ppermute x12, starting transfers between devices, scatter_grad(): total = lax.ppermute(total, 'tensor', ring(n_z, -1))  38.7 us
    dot_general x5, matrix products, dot_tn(): lax.dot_general(a, b, (((0,), (0,)), ((), ())), preferred_element_type=F32)  33.4 us
    convert_element_type x20, other arithmetic, add_low(): return (first.astype(F32) + second.astype(F32)).astype(BF)  32.6 us
  transfers between devices with their start and end apart: 99, of which 27 were waited for; matrix products, arithmetic and copies ran while one was open for 31% of the time, Pallas kernels for 3%

profile of v1, /device:TPU:0, one launch (start us, length us, event | category | flops | bytes accessed | tf_op | source)
XLA Modules:
  0.0 674.0 jit_solution(15614915560022569136)
XLA Ops:
  24.0 7.0 %all-to-all-start.2 = ((f32[32,1,1536]{2,1,0:T(1,128)}), f32[32,1,1536]{2,1,0:T(1,128)S(1)}, u32[]{:S(2)}, u32[]{:S(2)}) async-start(f32[32,1,1536]{2,1,0:T(1,128)} %copy.207), calls=%async_computation.2 | async-start | bytes 393216 | tf_op jit(solution)/shard_map/all_to_all | solution.py:304
  34.8 5.2 fusion.48
  40.0 6.4 copy.210
  57.3 5.4 collective-permute-done.15
  70.0 5.7 all-to-all-start
  88.7 19.8 %collective-permute-done.34 = bf16[128,1024]{1,0:T(8,128)(2,1)S(1)} collective-permute-done((bf16[128,1024]{1,0:T(8,128)(2,1)}, bf16[128,1024]{1,0:T(8,128)(2,1)S(1)}, u32[]{:S(2)}, u32[]{:S(2)}) %collective-permute-start.34) | collective-permute-done | bytes 262176 | tf_op jit(solution)/shard_map/ppermute | solution.py:65
  129.3 7.0 %collective-permute-done.3 = bf16[128,3072]{0,1:T(8,128)(2,1)} collective-permute-done((bf16[128,3072]{0,1:T(8,128)(2,1)}, bf16[128,3072]{0,1:T(8,128)(2,1)}, u32[]{:S(2)}, u32[]{:S(2)}) %collective-permute-start.3) | collective-permute-done | bytes 786464 | tf_op jit(solution)/shard_map/ppermute | solution.py:68
  143.2 15.5 %collective-permute-done.26 = bf16[128,4096]{1,0:T(8,128)(2,1)S(1)} collective-permute-done((bf16[128,4096]{1,0:T(8,128)(2,1)}, bf16[128,4096]{1,0:T(8,128)(2,1)S(1)}, u32[]{:S(2)}, u32[]{:S(2)}) %collective-permute-start.26) | collective-permute-done | bytes 1048608 | tf_op jit(solution)/shard_map/ppermute | solution.py:68
  160.7 8.3 %all-to-all-start.4 = ((bf16[4,10,16,1024]{3,2,1,0:T(8,128)(2,1)}), bf16[4,10,16,1024]{3,2,1,0:T(8,128)(2,1)}, u32[]{:S(2)}, u32[]{:S(2)}) async-start(bf16[4,10,16,1024]{3,2,1,0:T(8,128)(2,1)} %bitcast.147), calls=%async_computation.4 | async-start | bytes 2621440 | tf_op jit(solution)/shard_map/all_to_all | solution.py:292
  171.4 9.8 %collective-permute-done.36 = bf16[128,4096]{1,0:T(8,128)(2,1)} collective-permute-done((bf16[128,4096]{1,0:T(8,128)(2,1)}, bf16[128,4096]{1,0:T(8,128)(2,1)}, u32[]{:S(2)}, u32[]{:S(2)}) %collective-permute-start.36) | collective-permute-done | bytes 1048608 | tf_op jit(solution)/shard_map/ppermute | solution.py:68
  205.4 7.6 %collective-permute-done.28 = bf16[128,4096]{1,0:T(8,128)(2,1)S(1)} collective-permute-done((bf16[128,4096]{1,0:T(8,128)(2,1)S(1)}, bf16[128,4096]{1,0:T(8,128)(2,1)S(1)}, u32[]{:S(2)}, u32[]{:S(2)}) %collective-permute-start.28) | collective-permute-done | bytes 1048608 | tf_op jit(solution)/shard_map/ppermute | solution.py:68
  216.6 11.7 %collective-permute-done.38 = bf16[128,4096]{1,0:T(8,128)(2,1)} collective-permute-done((bf16[128,4096]{1,0:T(8,128)(2,1)}, bf16[128,4096]{1,0:T(8,128)(2,1)}, u32[]{:S(2)}, u32[]{:S(2)}) %collective-permute-start.38) | collective-permute-done | bytes 1048608 | tf_op jit(solution)/shard_map/ppermute | solution.py:68
  236.6 7.4 %convolution_convert_fusion.3.qkv_ref = bf16[640,3072]{1,0:T(8,128)(2,1)S(1)} fusion(bf16[1024,3072]{0,1:T(8,128)(2,1)} %constant_dynamic-update-slice_fusion, bf16[1024,640]{1,0:T(8,128)(2,1)S(1)} %copy-done.10, f32[1024]{0:T(1024)S(1)} %bitcast.172, f32[1024]{0:T(1024)S(1)} %bitcast.165, f32[640]{0:T(1024)S(1)} %add_rsqrt_fusion.1, ...), kind=kOutput, calls=%fused_computation.21 | convolution fusion | flops 4032430080 | bytes 11547648 | tf_op jit(solution)/shard_map/dot_general | solution.py:268
  244.1 21.1 %attend.1 = (bf16[640,1024]{1,0:T(8,128)(2,1)S(1)}, bf16[2,16,320,320]{3,2,1,0:T(8,128)(2,1)S(1)}) custom-call(s32[1]{0:T(128)} %dynamic_slice.7.count_ref, bf16[640,3072]{1,0:T(8,128)(2,1)S(1)} %convolution_convert_fusion.3.qkv_ref, f32[16,64,576]{2,1,0:T(8,128)S(1)} %copy.211.bias_ref), custom_call_target="tpu_custom_call" | custom-call | flops 2000000000 | bytes 14000000 | tf_op jit(solution)/shard_map/attend/pallas_call | solution.py:198
  269.9 6.0 fusion.88
  275.9 9.8 %convolution_convert_fusion = bf16[1024,4096]{1,0:T(8,128)(2,1)} fusion(bf16[1024,640]{1,0:T(8,128)(2,1)S(1)} %copy-done.39, f32[1024]{0:T(1024)S(1)} %bitcast.169, f32[640,4096]{1,0:T(8,128)S(1)} %fusion.88), kind=kOutput, calls=%fused_computation.18 | convolution fusion | flops 5398462464 | bytes 20189184 | tf_op jit(solution)/shard_map/dot_general | solution.py:135
  288.0 16.1 %multiply_convert_fusion = bf16[640,4096]{1,0:T(8,128)(2,1)} fusion(bf16[1024,4096]{1,0:T(8,128)(2,1)} %constant_dynamic-update-slice_fusion.42, f32[640,4096]{1,0:T(8,128)S(1)} %fusion.88, bf16[1024,640]{1,0:T(8,128)(2,1)} %fusion.62, f32[1024]{0:T(1024)S(1)} %bitcast.170), kind=kOutput, calls=%fused_computation.17 | convolution fusion | flops 5425725440 | bytes 25432064 | tf_op jit(solution)/shard_map/dot_general | solution.py:268
  304.1 8.7 %fusion.101 = (bf16[1024]{0:T(1024)(128)(2,1)S(1)}, f32[640,1024]{1,0:T(8,128)}) fusion(bf16[640,4096]{1,0:T(8,128)(2,1)} %multiply_convert_fusion, bf16[1024,4096]{1,0:T(8,128)(2,1)S(1)} %constant_dynamic-update-slice_fusion.27), kind=kOutput, calls=%fused_computation.231 | convolution fusion | flops 5369363456 | bytes 16254976 | tf_op jit(solution)/shard_map/dot_general | solution.py:131
  319.5 16.5 %multiply_reduce_fusion.1 = (bf16[1024]{0:T(1024)(128)(2,1)S(1)}, f32[640,1024]{0,1:T(8,128)}, bf16[1024]{0:T(1024)(128)(2,1)S(1)}, f32[640,1024]{0,1:T(8,128)}) fusion(f32[640,1024]{0,1:T(8,128)S(1)} %copy-done.36, f32[640]{0:T(1024)S(1)} %broadcast_multiply_fusion.2, f32[640]{0:T(1024)S(1)} %add_rsqrt_fusion, f32[640,1024]{0,1:T(8,128)S(1)} %get-tuple-element.98, ...), kind=kOutput, calls=%fused_computation.61 | convolution fusion | flops 5400819712 | bytes 33310720 | tf_op jit(solution)/shard_map/dot_general | solution.py:131
  341.6 13.3 %convolution_convert_fusion.1 = bf16[1024,4096]{1,0:T(8,128)(2,1)} fusion(bf16[640,4096]{1,0:T(8,128)(2,1)} %multiply_convert_fusion, f32[640,1024]{0,1:T(8,128)S(1)} %get-tuple-element.98, f32[1024]{0:T(1024)S(1)} %bitcast.160, f32[1024]{0:T(1024)S(1)} %bitcast.158, f32[640]{0:T(1024)S(1)} %add_rsqrt_fusion, f32[640]{0:T(1024)S(1)} %broadcast_multiply_fusion.4), kind=kOutput, calls=%fused_computation.19 | convolution fusion | flops 5376180224 | bytes 16266240 | tf_op jit(solution)/shard_map/dot_general | solution.py:135
  354.9 21.1 %attend_back.1 = (bf16[640,3072]{1,0:T(8,128)(2,1)S(1)}, f32[16,64,576]{2,1,0:T(8,128)S(1)}) custom-call(s32[1]{0:T(128)} %dynamic_slice.7.count_ref, bf16[640,3072]{1,0:T(8,128)(2,1)S(1)} %copy-done.5, bf16[2,16,320,320]{3,2,1,0:T(8,128)(2,1)S(1)} %bitcast.137, bf16[640,1024]{1,0:T(8,128)(2,1)S(1)} %convolution_convert_fusion.5.gatt_ref), custom_call_target="tpu_custom_call" | custom-call | flops 5000000000 | bytes 18000000 | tf_op jit(solution)/shard_map/attend_back/pallas_call | solution.py:225
  376.1 5.8 fusion.100
  381.9 7.3 %convolution_convert_fusion.2 = bf16[1024,3072]{1,0:T(8,128)(2,1)} fusion(bf16[640,3072]{1,0:T(8,128)(2,1)S(1)} %get-tuple-element.15, bf16[1024,640]{1,0:T(8,128)(2,1)S(1)} %copy-done.11, f32[1024]{0:T(1024)S(1)} %bitcast.173, f32[1024]{0:T(1024)S(1)} %bitcast.166, f32[640]{0:T(1024)S(1)} %add_rsqrt_fusion.1, f32[640]{0:T(1024)S(1)} %broadcast_multiply_fusion.5), kind=kOutput, calls=%fused_computation.20 | convolution fusion | flops 4033609728 | bytes 11547648 | tf_op jit(solution)/shard_map/dot_general | solution.py:135
  394.2 6.0 copy.228
  474.5 18.2 %collective-permute-done.43 = f32[8,4,128]{2,1,0:T(4,128)S(1)} collective-permute-done((f32[8,4,128]{2,1,0:T(4,128)S(1)}, f32[8,4,128]{2,1,0:T(4,128)S(1)}, u32[]{:S(2)}, u32[]{:S(2)}) %collective-permute-start.43) | collective-permute-done | bytes 16416 | tf_op jit(solution)/shard_map/ppermute | solution.py:101
  538.1 5.7 collective-permute-done.50
  546.7 12.2 %all-to-all-done.5 = bf16[4,10,16,1024]{3,2,1,0:T(8,128)(2,1)S(1)} async-done(((bf16[4,10,16,1024]{3,2,1,0:T(8,128)(2,1)}), bf16[4,10,16,1024]{3,2,1,0:T(8,128)(2,1)S(1)}, u32[]{:S(2)}, u32[]{:S(2)}) %all-to-all-start.5) | async-done | bytes 1310752 | tf_op jit(solution)/shard_map/all_to_all | solution.py:297
  569.5 13.8 %collective-permute-done.47 = bf16[128,3072]{1,0:T(8,128)(2,1)S(1)} collective-permute-done((bf16[128,3072]{1,0:T(8,128)(2,1)}, bf16[128,3072]{1,0:T(8,128)(2,1)S(1)}, u32[]{:S(2)}, u32[]{:S(2)}) %collective-permute-start.47) | collective-permute-done | bytes 786464 | tf_op jit(solution)/shard_map/ppermute | solution.py:83
  586.4 19.4 %collective-permute-done.67 = bf16[128,4096]{1,0:T(8,128)(2,1)S(1)} collective-permute-done((bf16[128,4096]{1,0:T(8,128)(2,1)S(1)}, bf16[128,4096]{1,0:T(8,128)(2,1)S(1)}, u32[]{:S(2)}, u32[]{:S(2)}) %collective-permute-start.67) | collective-permute-done | bytes 1048608 | tf_op jit(solution)/shard_map/ppermute | solution.py:83
  605.8 6.1 collective-permute-start.52
  615.4 12.6 %collective-permute-done.77 = bf16[128,4096]{1,0:T(8,128)(2,1)S(1)} collective-permute-done((bf16[128,4096]{1,0:T(8,128)(2,1)S(1)}, bf16[128,4096]{1,0:T(8,128)(2,1)S(1)}, u32[]{:S(2)}, u32[]{:S(2)}) %collective-permute-start.77) | collective-permute-done | bytes 1048608 | tf_op jit(solution)/shard_map/ppermute | solution.py:83
  635.2 5.4 collective-permute-done.82
  (444 shorter events, 330.0 us)
Async XLA Ops:
  0.7 30.4 %collective-permute-start.11 = (f32[4,2025]{1,0:T(4,128)}, f32[4,2025]{1,0:T(4,128)S(1)}, u32[]{:S(2)}, u32[]{:S(2)}) collective-permute-start(f32[4,2025]{1,0:T(4,128)} %param.19), channel_id=1, source_target_pairs={{0,2},{1,3},{2,0},{3,1},{4,6},{5,7},{6,4},{7,5},{8,10},{9,11},{10,... | collective-permute-start | bytes 97208 | tf_op jit(solution)/shard_map/ppermute | solution.py:95
  13.6 36.8 %collective-permute-start.13 = (bf16[128,256]{1,0:T(8,128)(2,1)}, bf16[128,256]{1,0:T(8,128)(2,1)S(1)}, u32[]{:S(2)}, u32[]{:S(2)}) collective-permute-start(bf16[128,256]{1,0:T(8,128)(2,1)} %param.15), channel_id=1, source_target_pairs={{0,1},{1,2},{2,3},{3,0},{4,5},{5,6},{6,7},{7,4},{8,9},{9,10},{10,1... | collective-permute-start | bytes 196616 | tf_op jit(solution)/shard_map/ppermute | solution.py:65
  13.7 52.6 %collective-permute-start.23 = (bf16[128,1024]{1,0:T(8,128)(2,1)}, bf16[128,1024]{1,0:T(8,128)(2,1)}, u32[]{:S(2)}, u32[]{:S(2)}) collective-permute-start(bf16[128,1024]{1,0:T(8,128)(2,1)} %param.16), channel_id=1, source_target_pairs={{0,1},{1,2},{2,3},{3,0},{4,5},{5,6},{6,7},{7,4},{8,9},{9,10},{10,1... | collective-permute-start | bytes 786440 | tf_op jit(solution)/shard_map/ppermute | solution.py:65
  24.0 46.0 %all-to-all-start.2 = ((f32[32,1,1536]{2,1,0:T(1,128)}), f32[32,1,1536]{2,1,0:T(1,128)S(1)}, u32[]{:S(2)}, u32[]{:S(2)}) async-start(f32[32,1,1536]{2,1,0:T(1,128)} %copy.207), calls=%async_computation.2 | async-start | bytes 393216 | tf_op jit(solution)/shard_map/all_to_all | solution.py:304
  31.1 37.1 %collective-permute-start.33 = (bf16[128,1024]{1,0:T(8,128)(2,1)}, bf16[128,1024]{1,0:T(8,128)(2,1)}, u32[]{:S(2)}, u32[]{:S(2)}) collective-permute-start(bf16[128,1024]{1,0:T(8,128)(2,1)} %param.17), channel_id=1, source_target_pairs={{0,1},{1,2},{2,3},{3,0},{4,5},{5,6},{6,7},{7,4},{8,9},{9,10},{10,1... | collective-permute-start | bytes 786440 | tf_op jit(solution)/shard_map/ppermute | solution.py:65
  32.9 31.9 %collective-permute-start = (bf16[128,768]{0,1:T(8,128)(2,1)S(1)}, bf16[128,768]{0,1:T(8,128)(2,1)}, u32[]{:S(2)}, u32[]{:S(2)}) collective-permute-start(bf16[128,768]{0,1:T(8,128)(2,1)S(1)} %bitcast.152), channel_id=1, source_target_pairs={{0,1},{1,2},{2,3},{3,0},{4,5},{5,6},{6,7},{7,4},{8,9},{9,10},{10,1... | collective-permute-start | bytes 589832 | tf_op jit(solution)/shard_map/ppermute | solution.py:65
  63.3 55.3 %collective-permute-start.19 = (bf16[128,1024]{1,0:T(8,128)(2,1)}, bf16[128,1024]{1,0:T(8,128)(2,1)}, u32[]{:S(2)}, u32[]{:S(2)}) collective-permute-start(bf16[128,1024]{1,0:T(8,128)(2,1)} %get-tuple-element.146), channel_id=1, source_target_pairs={{0,4},{4,0},{8,12},{12,8},{16,20},{20,16},{24,28},{28,24},{1,5},{5... | collective-permute-start | bytes 786440 | tf_op jit(solution)/shard_map/ppermute | solution.py:69
  70.0 90.7 %all-to-all-start = ((bf16[4,10,16,1024]{3,2,1,0:T(8,128)(2,1)}), bf16[4,10,16,1024]{3,2,1,0:T(8,128)(2,1)}, u32[]{:S(2)}, u32[]{:S(2)}) async-start(bf16[4,10,16,1024]{3,2,1,0:T(8,128)(2,1)} %bitcast.146), calls=%async_computation | async-start | bytes 2621440 | tf_op jit(solution)/shard_map/all_to_all | solution.py:292
  82.9 42.1 %collective-permute-start.21 = (bf16[128,1024]{1,0:T(8,128)(2,1)}, bf16[128,1024]{1,0:T(8,128)(2,1)S(1)}, u32[]{:S(2)}, u32[]{:S(2)}) collective-permute-start(bf16[128,1024]{1,0:T(8,128)(2,1)} %collective-permute-done.17), channel_id=1, source_target_pairs={{0,4},{4,0},{8,12},{12,8},{16,20},{20,16},{24,28},{28,24},{1,5},{5... | collective-permute-start | bytes 786440 | tf_op jit(solution)/shard_map/ppermute | solution.py:69
  86.3 36.4 %collective-permute-start.20 = (bf16[128,1024]{1,0:T(8,128)(2,1)}, bf16[128,1024]{1,0:T(8,128)(2,1)S(1)}, u32[]{:S(2)}, u32[]{:S(2)}) collective-permute-start(bf16[128,1024]{1,0:T(8,128)(2,1)} %collective-permute-done.16), channel_id=1, source_target_pairs={{0,4},{4,0},{8,12},{12,8},{16,20},{20,16},{24,28},{28,24},{1,5},{5... | collective-permute-start | bytes 786440 | tf_op jit(solution)/shard_map/ppermute | solution.py:69
  125.0 33.7 %collective-permute-start.26 = (bf16[128,4096]{1,0:T(8,128)(2,1)}, bf16[128,4096]{1,0:T(8,128)(2,1)S(1)}, u32[]{:S(2)}, u32[]{:S(2)}) collective-permute-start(bf16[128,4096]{1,0:T(8,128)(2,1)} %get-tuple-element.126), channel_id=1, source_target_pairs={{0,8},{4,20},{8,0},{12,28},{16,24},{20,4},{24,16},{28,12},{1,9},{5... | collective-permute-start | bytes 3145736 | tf_op jit(solution)/shard_map/ppermute | solution.py:68
  127.2 71.0 %collective-permute-start.6 = (bf16[128,3072]{0,1:T(8,128)(2,1)}, bf16[128,3072]{0,1:T(8,128)(2,1)}, u32[]{:S(2)}, u32[]{:S(2)}) collective-permute-start(bf16[128,3072]{0,1:T(8,128)(2,1)} %get-tuple-element.124), channel_id=1, source_target_pairs={{0,4},{4,0},{8,12},{12,8},{16,20},{20,16},{24,28},{28,24},{1,5},{5... | collective-permute-start | bytes 2359304 | tf_op jit(solution)/shard_map/ppermute | solution.py:69
  128.2 84.9 %collective-permute-start.29 = (bf16[128,4096]{1,0:T(8,128)(2,1)}, bf16[128,4096]{1,0:T(8,128)(2,1)}, u32[]{:S(2)}, u32[]{:S(2)}) collective-permute-start(bf16[128,4096]{1,0:T(8,128)(2,1)} %get-tuple-element.126), channel_id=1, source_target_pairs={{0,4},{4,0},{8,12},{12,8},{16,20},{20,16},{24,28},{28,24},{1,5},{5... | collective-permute-start | bytes 3145736 | tf_op jit(solution)/shard_map/ppermute | solution.py:69
  136.3 32.7 %collective-permute-start.27 = (bf16[128,4096]{1,0:T(8,128)(2,1)}, bf16[128,4096]{1,0:T(8,128)(2,1)}, u32[]{:S(2)}, u32[]{:S(2)}) collective-permute-start(bf16[128,4096]{1,0:T(8,128)(2,1)} %get-tuple-element.126), channel_id=1, source_target_pairs={{0,16},{4,12},{8,24},{12,4},{16,0},{20,28},{24,8},{28,20},{1,17},{... | collective-permute-start | bytes 3145736 | tf_op jit(solution)/shard_map/ppermute | solution.py:68
  141.4 39.8 %collective-permute-start.36 = (bf16[128,4096]{1,0:T(8,128)(2,1)}, bf16[128,4096]{1,0:T(8,128)(2,1)}, u32[]{:S(2)}, u32[]{:S(2)}) collective-permute-start(bf16[128,4096]{1,0:T(8,128)(2,1)} %get-tuple-element.134), channel_id=1, source_target_pairs={{0,8},{4,20},{8,0},{12,28},{16,24},{20,4},{24,16},{28,12},{1,9},{5... | collective-permute-start | bytes 3145736 | tf_op jit(solution)/shard_map/ppermute | solution.py:68
  169.1 61.6 %collective-permute-start.39 = (bf16[128,4096]{1,0:T(8,128)(2,1)}, bf16[128,4096]{1,0:T(8,128)(2,1)}, u32[]{:S(2)}, u32[]{:S(2)}) collective-permute-start(bf16[128,4096]{1,0:T(8,128)(2,1)} %get-tuple-element.134), channel_id=1, source_target_pairs={{0,4},{4,0},{8,12},{12,8},{16,20},{20,16},{24,28},{28,24},{1,5},{5... | collective-permute-start | bytes 3145736 | tf_op jit(solution)/shard_map/ppermute | solution.py:69
  228.3 41.5 %collective-permute-start.32 = (bf16[128,4096]{1,0:T(8,128)(2,1)S(1)}, bf16[128,4096]{1,0:T(8,128)(2,1)S(1)}, u32[]{:S(2)}, u32[]{:S(2)}) collective-permute-start(bf16[128,4096]{1,0:T(8,128)(2,1)S(1)} %collective-permute-done.28), channel_id=1, source_target_pairs={{0,4},{4,0},{8,12},{12,8},{16,20},{20,16},{24,28},{28,24},{1,5},{5... | collective-permute-start | bytes 3145736 | tf_op jit(solution)/shard_map/ppermute | solution.py:69
  230.6 55.0 %collective-permute-start.42 = (bf16[128,4096]{1,0:T(8,128)(2,1)}, bf16[128,4096]{1,0:T(8,128)(2,1)}, u32[]{:S(2)}, u32[]{:S(2)}) collective-permute-start(bf16[128,4096]{1,0:T(8,128)(2,1)} %collective-permute-done.38), channel_id=1, source_target_pairs={{0,4},{4,0},{8,12},{12,8},{16,20},{20,16},{24,28},{28,24},{1,5},{5... | collective-permute-start | bytes 3145736 | tf_op jit(solution)/shard_map/ppermute | solution.py:69
  390.2 102.5 %collective-permute-start.55 = (bf16[128,1024]{1,0:T(8,128)(2,1)}, bf16[128,1024]{1,0:T(8,128)(2,1)}, u32[]{:S(2)}, u32[]{:S(2)}) collective-permute-start(bf16[128,1024]{1,0:T(8,128)(2,1)} %get-tuple-element.117), channel_id=1, source_target_pairs={{0,4},{4,0},{8,12},{12,8},{16,20},{20,16},{24,28},{28,24},{1,5},{5... | collective-permute-start | bytes 786440 | tf_op jit(solution)/shard_map/ppermute | solution.py:83
  390.2 53.0 %collective-permute-start.59 = (bf16[128,1024]{1,0:T(8,128)(2,1)}, bf16[128,1024]{1,0:T(8,128)(2,1)}, u32[]{:S(2)}, u32[]{:S(2)}) collective-permute-start(bf16[128,1024]{1,0:T(8,128)(2,1)} %get-tuple-element.118), channel_id=1, source_target_pairs={{0,4},{4,0},{8,12},{12,8},{16,20},{20,16},{24,28},{28,24},{1,5},{5... | collective-permute-start | bytes 786440 | tf_op jit(solution)/shard_map/ppermute | solution.py:83
  451.0 110.9 %collective-permute-start.45 = (bf16[128,3072]{1,0:T(8,128)(2,1)}, bf16[128,3072]{1,0:T(8,128)(2,1)}, u32[]{:S(2)}, u32[]{:S(2)}) collective-permute-start(bf16[128,3072]{1,0:T(8,128)(2,1)} %get-tuple-element.111), channel_id=1, source_target_pairs={{0,4},{4,0},{8,12},{12,8},{16,20},{20,16},{24,28},{28,24},{1,5},{5... | collective-permute-start | bytes 2359304 | tf_op jit(solution)/shard_map/ppermute | solution.py:83
  456.5 36.8 %collective-permute-start.57 = (bf16[128,1024]{1,0:T(8,128)(2,1)}, bf16[128,1024]{1,0:T(8,128)(2,1)}, u32[]{:S(2)}, u32[]{:S(2)}) collective-permute-start(bf16[128,1024]{1,0:T(8,128)(2,1)} %get-tuple-element.121), channel_id=1, source_target_pairs={{0,16},{4,12},{8,24},{12,4},{16,0},{20,28},{24,8},{28,20},{1,17},{... | collective-permute-start | bytes 786440 | tf_op jit(solution)/shard_map/ppermute | solution.py:83
  460.2 33.2 %collective-permute-start.61 = (bf16[128,1024]{1,0:T(8,128)(2,1)}, bf16[128,1024]{1,0:T(8,128)(2,1)}, u32[]{:S(2)}, u32[]{:S(2)}) collective-permute-start(bf16[128,1024]{1,0:T(8,128)(2,1)} %add_convert_fusion.29), channel_id=1, source_target_pairs={{0,8},{4,20},{8,0},{12,28},{16,24},{20,4},{24,16},{28,12},{1,9},{5... | collective-permute-start | bytes 786440 | tf_op jit(solution)/shard_map/ppermute | solution.py:83
  466.6 56.3 %all-to-all-start.3 = ((bf16[4,10,16,1024]{3,2,1,0:T(8,128)(2,1)}), bf16[4,10,16,1024]{3,2,1,0:T(8,128)(2,1)S(1)}, u32[]{:S(2)}, u32[]{:S(2)}) async-start(bf16[4,10,16,1024]{3,2,1,0:T(8,128)(2,1)} %bitcast.135), calls=%async_computation.3 | async-start | bytes 2621440 | tf_op jit(solution)/shard_map/all_to_all | solution.py:297
  493.3 33.5 %collective-permute-start.69 = (bf16[128,4096]{1,0:T(8,128)(2,1)}, bf16[128,4096]{1,0:T(8,128)(2,1)}, u32[]{:S(2)}, u32[]{:S(2)}) collective-permute-start(bf16[128,4096]{1,0:T(8,128)(2,1)} %get-tuple-element.106), channel_id=1, source_target_pairs={{0,4},{4,0},{8,12},{12,8},{16,20},{20,16},{24,28},{28,24},{1,5},{5... | collective-permute-start | bytes 3145736 | tf_op jit(solution)/shard_map/ppermute | solution.py:83
  522.9 36.0 %all-to-all-start.5 = ((bf16[4,10,16,1024]{3,2,1,0:T(8,128)(2,1)}), bf16[4,10,16,1024]{3,2,1,0:T(8,128)(2,1)S(1)}, u32[]{:S(2)}, u32[]{:S(2)}) async-start(bf16[4,10,16,1024]{3,2,1,0:T(8,128)(2,1)} %bitcast.144), calls=%async_computation.5 | async-start | bytes 2621440 | tf_op jit(solution)/shard_map/all_to_all | solution.py:297
  527.2 31.7 %collective-permute-start.68 = (bf16[128,4096]{1,0:T(8,128)(2,1)}, bf16[128,4096]{1,0:T(8,128)(2,1)}, u32[]{:S(2)}, u32[]{:S(2)}) collective-permute-start(bf16[128,4096]{1,0:T(8,128)(2,1)} %get-tuple-element.107), channel_id=1, source_target_pairs={{0,4},{4,0},{8,12},{12,8},{16,20},{20,16},{24,28},{28,24},{1,5},{5... | collective-permute-start | bytes 3145736 | tf_op jit(solution)/shard_map/ppermute | solution.py:83
  561.9 43.9 %collective-permute-start.67 = (bf16[128,4096]{1,0:T(8,128)(2,1)S(1)}, bf16[128,4096]{1,0:T(8,128)(2,1)S(1)}, u32[]{:S(2)}, u32[]{:S(2)}) collective-permute-start(bf16[128,4096]{1,0:T(8,128)(2,1)S(1)} %copy-done.18), channel_id=1, source_target_pairs={{0,16},{4,12},{8,24},{12,4},{16,0},{20,28},{24,8},{28,20},{1,17},{... | collective-permute-start | bytes 3145736 | tf_op jit(solution)/shard_map/ppermute | solution.py:83
  566.6 45.3 %collective-permute-start.71 = (bf16[128,4096]{1,0:T(8,128)(2,1)S(1)}, bf16[128,4096]{1,0:T(8,128)(2,1)S(1)}, u32[]{:S(2)}, u32[]{:S(2)}) collective-permute-start(bf16[128,4096]{1,0:T(8,128)(2,1)S(1)} %add_convert_fusion.10), channel_id=1, source_target_pairs={{0,8},{4,20},{8,0},{12,28},{16,24},{20,4},{24,16},{28,12},{1,9},{5... | collective-permute-start | bytes 3145736 | tf_op jit(solution)/shard_map/ppermute | solution.py:83
  569.5 45.9 %collective-permute-start.75 = (bf16[128,4096]{1,0:T(8,128)(2,1)S(1)}, bf16[128,4096]{1,0:T(8,128)(2,1)S(1)}, u32[]{:S(2)}, u32[]{:S(2)}) collective-permute-start(bf16[128,4096]{1,0:T(8,128)(2,1)S(1)} %copy-done.19), channel_id=1, source_target_pairs={{0,4},{4,0},{8,12},{12,8},{16,20},{20,16},{24,28},{28,24},{1,5},{5... | collective-permute-start | bytes 3145736 | tf_op jit(solution)/shard_map/ppermute | solution.py:83
  583.3 44.7 %collective-permute-start.77 = (bf16[128,4096]{1,0:T(8,128)(2,1)S(1)}, bf16[128,4096]{1,0:T(8,128)(2,1)S(1)}, u32[]{:S(2)}, u32[]{:S(2)}) collective-permute-start(bf16[128,4096]{1,0:T(8,128)(2,1)S(1)} %copy-done.17), channel_id=1, source_target_pairs={{0,16},{4,12},{8,24},{12,4},{16,0},{20,28},{24,8},{28,20},{1,17},{... | collective-permute-start | bytes 3145736 | tf_op jit(solution)/shard_map/ppermute | solution.py:83
  584.0 44.1 %collective-permute-start.81 = (bf16[128,4096]{1,0:T(8,128)(2,1)S(1)}, bf16[128,4096]{1,0:T(8,128)(2,1)S(1)}, u32[]{:S(2)}, u32[]{:S(2)}) collective-permute-start(bf16[128,4096]{1,0:T(8,128)(2,1)S(1)} %add_convert_fusion.3), channel_id=1, source_target_pairs={{0,8},{4,20},{8,0},{12,28},{16,24},{20,4},{24,16},{28,12},{1,9},{5... | collective-permute-start | bytes 3145736 | tf_op jit(solution)/shard_map/ppermute | solution.py:83
  (113 other events, 1977.5 us)

commit v2 on v1

v2 whole, which is shorter than its diff:
```python
import functools

import jax
import jax.numpy as jnp
import numpy as np
from jax import lax
from jax.experimental import pallas as pl
from jax.experimental.pallas import tpu as pltpu
from jax.sharding import PartitionSpec as P

HEAD_DIM = 64
WIN_T = 5
WIN_S = 8
FRAMES = 10
SPATIAL = 64
OFFSETS = 2025

EPSILON = 1e-06
NEGATIVE = -1e30
HIGHEST = lax.Precision.HIGHEST
BF = jnp.bfloat16
F32 = jnp.float32
WINDOWS = FRAMES // WIN_T
WIN_LEN = WIN_T * SPATIAL
SPREAD = 2 * WIN_T - 1
DIAG = SPREAD * SPATIAL
GROUPS = 4
VMEM = 56 << 20


def stage_bits(n_dp, core):
    bits = list(range(1, n_dp.bit_length() - 1))
    return bits if core == 0 else bits[::-1]


def stage_perm(n_dp, stage):
    return [(i, i ^ (1 << stage_bits(n_dp, i & 1)[stage])) for i in range(n_dp)]


def core_perm(n_dp):
    return [(i, i ^ 1) for i in range(n_dp)]


def ring(count, step):
    return [(i, (i + step) % count) for i in range(count)]


def stages(n_dp):
    return n_dp.bit_length() - 2


def dp_order(n_dp):
    half = n_dp // 2

    def mask(core, place):
        return sum(1 << b for t, b in enumerate(stage_bits(n_dp, core)) if place >> t & 1)

    return np.array(
        [[mask(c, k) for k in range(half)] + [1 ^ mask(1 - c, k) for k in range(half)] for c in (0, 1)],
        np.int32,
    )


def merged(pieces):
    if len(pieces) <= GROUPS:
        return pieces
    return [jnp.concatenate(pieces[i : i + 2], axis=0) for i in range(0, len(pieces), 2)]


def gather_steps(n_dp, n_z, shard, direct):
    blocks = [shard]
    if direct:
        blocks = yield shifted([shard] * n_z, n_z, 1)
    else:
        for _ in range(n_z - 1):
            blocks = yield blocks + [lax.ppermute(blocks[-1], "tensor", ring(n_z, 1))]
    pieces = [jnp.concatenate(blocks, axis=1)]
    for t in range(stages(n_dp)):
        perm = stage_perm(n_dp, t)
        pieces = yield merged(pieces + [lax.ppermute(p, "dp", perm) for p in pieces])
    yield pieces + [lax.ppermute(p, "dp", core_perm(n_dp)) for p in pieces]


def add_low(first, second):
    return (first.astype(F32) + second.astype(F32)).astype(BF)


def scatter_steps(n_dp, n_z, halves, direct):
    keep, send = halves
    for t in range(stages(n_dp), -1, -1):
        perm = core_perm(n_dp) if t == stages(n_dp) else stage_perm(n_dp, t)
        got = lax.ppermute(send, "dp", perm)
        if t:
            rows = keep.shape[0] // 2
            keep, send = yield add_low(keep[:rows], got[:rows]), add_low(keep[rows:], got[rows:])
    width = keep.shape[1] // n_z
    part = [add_low(keep[:, r * width : (r + 1) * width], got[:, r * width : (r + 1) * width]) for r in range(n_z)]
    part = yield part
    if direct:
        yield functools.reduce(lambda a, b: a + b, [p.astype(F32) for p in shifted(part, n_z, -1)])
        return
    for r in range(n_z - 2, -1, -1):
        total = lax.ppermute(part[r + 1], "tensor", ring(n_z, -1))
        if r:
            part = yield part[:r] + [add_low(part[r], total)]
        else:
            yield part[0].astype(F32) + total.astype(F32)


class Chain:
    def __init__(self, name, steps, total):
        self.name, self.steps, self.left, self.value = name, steps, total, None

    def step(self):
        with jax.named_scope(f"{self.name}_{self.left}_left"):
            self.value = self.steps.send(self.value)
        self.left -= 1


def slot(chains, *values, free=()):
    chains = [c for c in chains if c.left]
    for chain in chains + [c for c in free if c.left]:
        chain.step()
    held, values = lax.optimization_barrier(([c.value for c in chains], values))
    for chain, value in zip(chains, held):
        chain.value = value
    return values[0] if len(values) == 1 else values


def whole(chain):
    while chain.left:
        slot([chain])
    return chain.value


def shifted(pieces, n_z, sign):
    return [pieces[0]] + [lax.ppermute(pieces[r], "tensor", ring(n_z, sign * r)) for r in range(1, n_z)]


def exchange_steps(pieces, n_z, sign):
    pieces = list(pieces)
    for group in ([n_z // 2], [r for r in range(1, n_z) if r != n_z // 2]):
        for r in group:
            pieces[r] = lax.ppermute(pieces[r], "tensor", ring(n_z, sign * r))
        pieces = yield pieces


def butterfly_steps(value, axis, count):
    bit = 1
    while bit < count:
        value = yield value + lax.ppermute(value, axis, [(i, i ^ bit) for i in range(count)])
        bit *= 2


def pair_onehot(place):
    span = 2 * WIN_S - 1
    row, col = place // WIN_S, place % WIN_S
    offset = (row[None, :] - row[:, None] + WIN_S - 1) * span + (col[None, :] - col[:, None] + WIN_S - 1)
    return (jnp.arange(span * span)[:, None] == offset.reshape(1, -1)).astype(F32)


def spread_bias(table, place):
    heads = table.shape[0]
    flat = jnp.dot(table.reshape(heads * SPREAD, -1), pair_onehot(place), precision=HIGHEST)
    return flat.reshape(heads, SPREAD, SPATIAL, SPATIAL)


def fold_bias(diag, place):
    heads = diag.shape[0]
    rows = diag.reshape(heads * SPREAD, SPATIAL * SPATIAL)
    folded = lax.dot_general(rows, pair_onehot(place), (((1,), (1,)), ((), ())), precision=HIGHEST)
    return folded.reshape(heads, OFFSETS)


def dot(a, b):
    return jnp.dot(a, b, preferred_element_type=F32)


def dot_nt(a, b):
    return lax.dot_general(a, b, (((1,), (1,)), ((), ())), preferred_element_type=F32)


def dot_tn(a, b):
    return lax.dot_general(a, b, (((0,), (0,)), ((), ())), preferred_element_type=F32)


def params():
    return pltpu.CompilerParams(vmem_limit_bytes=VMEM)


COST = pl.CostEstimate(flops=10**6, bytes_accessed=10**4, transcendentals=0)


class Pieces:
    def __init__(self, pieces, width, take, at):
        self.many, self.pieces = len(at(0)), len(pieces)
        self.arrays = [p for p in pieces for _ in range(self.many)]
        self.width, self.take, self.at = width, take, at
        self.rows = sum(p.shape[0] for p in pieces)

    def specs(self):
        return [
            pl.BlockSpec((a.shape[0], self.width), lambda j, p, i=i % self.many: (0, self.at(j)[i]))
            for i, a in enumerate(self.arrays)
        ]

    def load(self, refs, places):
        rows = [
            jnp.concatenate([r[:, : self.take] for r in refs[i : i + self.many]], axis=1)
            for i in range(0, len(refs), self.many)
        ]
        return jnp.concatenate(rows, axis=0)


class Gathered:
    def __init__(self, array):
        self.arrays = [array]
        self.count, self.width = array.shape[0], array.shape[3]
        self.rows = array.shape[0] * array.shape[2]

    def specs(self):
        n_dp, _, rows, columns = self.arrays[0].shape
        return [pl.BlockSpec((n_dp, 1, rows, columns), lambda j, p: (0, p[n_dp + j], 0, 0))]

    def load(self, refs, places):
        return jnp.concatenate([refs[0][places[k], 0] for k in range(self.count)], axis=0)


def rows_times(places, x, weight, columns, tile, finish, extra, outs, name):
    length, depth = x.shape
    count = len(weight.arrays)

    def kernel(places_ref, x_ref, *refs):
        w = weight.load(refs[:count], places_ref)
        done = finish(dot(x_ref[...], w), *(r[...] for r in refs[count : count + len(extra)]))
        for ref, value in zip(refs[count + len(extra) :], done):
            ref[...] = value

    tall = pl.BlockSpec((length, tile), lambda j, p: (0, j))
    return pl.pallas_call(
        kernel,
        grid_spec=pltpu.PrefetchScalarGridSpec(
            num_scalar_prefetch=1,
            grid=(columns // tile,),
            in_specs=[pl.BlockSpec((length, depth), lambda j, p: (0, 0))] + weight.specs() + [tall] * len(extra),
            out_specs=[tall] * len(outs),
        ),
        out_shape=[jax.ShapeDtypeStruct((length, columns), t) for t in outs],
        compiler_params=params(),
        cost_estimate=COST,
        name=name,
    )(places, x, *weight.arrays, *extra)


def rows_times_t(places, x, weight, tile, name):
    length, depth = x.shape
    count = len(weight.arrays)

    def kernel(places_ref, x_ref, *refs):
        term = dot_nt(x_ref[...], weight.load(refs[:count], places_ref))

        @pl.when(pl.program_id(0) == 0)
        def _():
            refs[count][...] = term

        @pl.when(pl.program_id(0) > 0)
        def _():
            refs[count][...] += term

    return pl.pallas_call(
        kernel,
        grid_spec=pltpu.PrefetchScalarGridSpec(
            num_scalar_prefetch=1,
            grid=(depth // tile,),
            in_specs=[pl.BlockSpec((length, tile), lambda j, p: (0, j))] + weight.specs(),
            out_specs=pl.BlockSpec((length, weight.rows), lambda j, p: (0, 0)),
        ),
        out_shape=jax.ShapeDtypeStruct((length, weight.rows), F32),
        compiler_params=params(),
        cost_estimate=COST,
        name=name,
    )(places, x, *weight.arrays)


def rows_against(x, y, tile, name, places=None, n_dp=1):
    length, depth = x.shape
    columns = y.shape[1]
    rows = depth // n_dp

    def kernel(places_ref, x_ref, y_ref, *refs):
        turned = refs[-1]

        @pl.when(pl.program_id(0) == 0)
        def _():
            turned[...] = x_ref[...].T

        result = dot(turned[...], y_ref[...]).astype(BF)
        if n_dp == 1:
            refs[0][...] = result[: depth // 2]
            refs[1][...] = result[depth // 2 :]
        else:
            for k in range(n_dp):
                refs[0][places_ref[k]] = result[k * rows : (k + 1) * rows]

    if n_dp == 1:
        shape = jax.ShapeDtypeStruct((depth // 2, columns), BF)
        half = pl.BlockSpec((depth // 2, tile), lambda j, p: (0, j))
        out_shape, out_specs = [shape, shape], [half, half]
        places = jnp.zeros((1,), jnp.int32)
    else:
        out_shape = jax.ShapeDtypeStruct((n_dp, rows, columns), BF)
        out_specs = pl.BlockSpec((n_dp, rows, tile), lambda j, p: (0, 0, j))
    return pl.pallas_call(
        kernel,
        grid_spec=pltpu.PrefetchScalarGridSpec(
            num_scalar_prefetch=1,
            grid=(columns // tile,),
            in_specs=[
                pl.BlockSpec((length, depth), lambda j, p: (0, 0)),
                pl.BlockSpec((length, tile), lambda j, p: (0, j)),
            ],
            out_specs=out_specs,
            scratch_shapes=[pltpu.VMEM((depth, length), BF)],
        ),
        out_shape=out_shape,
        compiler_params=params(),
        cost_estimate=COST,
        name=name,
    )(places, x, y)


def head_cols(kind, h, width):
    return slice(kind * width + h * HEAD_DIM, kind * width + (h + 1) * HEAD_DIM)


def attend_kernel(heads, count_ref, qkv_ref, bias_ref, att_ref, prob_ref):
    width = heads * HEAD_DIM
    scale = jnp.asarray(HEAD_DIM**-0.5, BF)
    key_at = lax.broadcasted_iota(jnp.int32, (WIN_LEN, WIN_LEN), 0)
    row_at = lax.broadcasted_iota(jnp.int32, (WIN_LEN, width), 0)
    att = [[] for _ in range(WINDOWS)]
    for h in range(heads):
        bias = jnp.concatenate(
            [
                jnp.concatenate([bias_ref[h, a - b + WIN_T - 1] for a in range(WIN_T)], axis=1)
                for b in range(WIN_T)
            ],
            axis=0,
        )
        for w in range(WINDOWS):
            live = (count_ref[0] - w * WIN_T) * SPATIAL
            rows = slice(w * WIN_LEN, (w + 1) * WIN_LEN)
            q = qkv_ref[rows, head_cols(0, h, width)] * scale
            k = qkv_ref[rows, head_cols(1, h, width)]
            v = qkv_ref[rows, head_cols(2, h, width)]
            scores = jnp.where(key_at < live, dot_nt(k, q) + bias, NEGATIVE)
            top = jnp.max(scores, axis=0, keepdims=True)
            expo = jnp.exp(scores - top)
            total = jnp.maximum(jnp.sum(expo, axis=0, keepdims=True), 1.0)
            probs = (expo * jnp.where(live > 0, 1.0 / total, 0.0)).astype(BF)
            prob_ref[w, h] = probs
            att[w].append(dot_tn(v, probs))
    for w in range(WINDOWS):
        live = (count_ref[0] - w * WIN_T) * SPATIAL
        whole = jnp.concatenate(att[w], axis=0).T
        att_ref[w * WIN_LEN : (w + 1) * WIN_LEN, :] = jnp.where(row_at < live, whole, 0.0).astype(BF)


def attend_back_kernel(heads, count_ref, qkv_ref, prob_ref, gatt_ref, gqkv_ref, diag_ref):
    width = heads * HEAD_DIM
    scale = jnp.asarray(HEAD_DIM**-0.5, BF)
    row_at = lax.broadcasted_iota(jnp.int32, (WIN_LEN, HEAD_DIM), 0)
    grad_q = [[] for _ in range(WINDOWS)]
    for h in range(heads):
        both = None
        for w in range(WINDOWS):
            live = (count_ref[0] - w * WIN_T) * SPATIAL
            rows = slice(w * WIN_LEN, (w + 1) * WIN_LEN)
            q = qkv_ref[rows, head_cols(0, h, width)] * scale
            k = qkv_ref[rows, head_cols(1, h, width)] * scale
            v = qkv_ref[rows, head_cols(2, h, width)]
            gatt = gatt_ref[rows, head_cols(0, h, width)]
            gatt = jnp.where(row_at < live, gatt, jnp.zeros_like(gatt))
            probs = prob_ref[w, h]
            full = probs.astype(F32)
            gqkv_ref[rows, head_cols(2, h, width)] = dot(probs, gatt).astype(BF)
            gprobs = dot_nt(v, gatt)
            inner = jnp.sum(full * gprobs, axis=0, keepdims=True)
            gscores = (full * (gprobs - inner)).astype(BF)
            gqkv_ref[rows, head_cols(1, h, width)] = dot(gscores, q).astype(BF)
            grad_q[w].append(dot_tn(k, gscores))
            wide = gscores.astype(F32)
            both = wide if both is None else both + wide
        blocks = [both[b * SPATIAL : (b + 1) * SPATIAL] for b in range(WIN_T)]
        for t in range(SPREAD):
            pairs = [(b, b + t - WIN_T + 1) for b in range(WIN_T) if 0 <= b + t - WIN_T + 1 < WIN_T]
            diag_ref[h, t] = functools.reduce(
                lambda x, y: x + y, [blocks[b][:, a * SPATIAL : (a + 1) * SPATIAL] for b, a in pairs]
            )
    for w in range(WINDOWS):
        whole = jnp.concatenate(grad_q[w], axis=0).T
        gqkv_ref[w * WIN_LEN : (w + 1) * WIN_LEN, 0:width] = whole.astype(BF)


def attend(count, qkv, bias, n_z):
    heads = bias.shape[0] // n_z
    width = heads * HEAD_DIM
    length = WINDOWS * WIN_LEN
    return pl.pallas_call(
        functools.partial(attend_kernel, heads),
        grid_spec=pltpu.PrefetchScalarGridSpec(
            num_scalar_prefetch=1,
            grid=(n_z,),
            in_specs=[
                pl.BlockSpec((length, 3 * width), lambda r, c: (0, r)),
                pl.BlockSpec((heads, SPREAD, SPATIAL, SPATIAL), lambda r, c: (r, 0, 0, 0)),
            ],
            out_specs=[
                pl.BlockSpec((length, width), lambda r, c: (0, r)),
                pl.BlockSpec((WINDOWS, heads, WIN_LEN, WIN_LEN), lambda r, c: (0, r, 0, 0)),
            ],
        ),
        out_shape=[
            jax.ShapeDtypeStruct((length, n_z * width), BF),
            jax.ShapeDtypeStruct((WINDOWS, n_z * heads, WIN_LEN, WIN_LEN), BF),
        ],
        compiler_params=params(),
        cost_estimate=COST,
        name="attend",
    )(count, qkv, bias)


def attend_back(count, qkv, probs, gatt, n_z):
    heads = probs.shape[1] // n_z
    width = heads * HEAD_DIM
    length = WINDOWS * WIN_LEN
    return pl.pallas_call(
        functools.partial(attend_back_kernel, heads),
        grid_spec=pltpu.PrefetchScalarGridSpec(
            num_scalar_prefetch=1,
            grid=(n_z,),
            in_specs=[
                pl.BlockSpec((length, 3 * width), lambda r, c: (0, r)),
                pl.BlockSpec((WINDOWS, heads, WIN_LEN, WIN_LEN), lambda r, c: (0, r, 0, 0)),
                pl.BlockSpec((length, width), lambda r, c: (0, r)),
            ],
            out_specs=[
                pl.BlockSpec((length, 3 * width), lambda r, c: (0, r)),
                pl.BlockSpec((heads, SPREAD, SPATIAL, SPATIAL), lambda r, c: (r, 0, 0, 0)),
            ],
        ),
        out_shape=[
            jax.ShapeDtypeStruct((length, n_z * 3 * width), BF),
            jax.ShapeDtypeStruct((n_z * heads, SPREAD, SPATIAL, SPATIAL), F32),
        ],
        compiler_params=params(),
        cost_estimate=COST,
        name="attend_back",
    )(count, qkv, probs, gatt)


def normalize(values):
    center = values - jnp.mean(values, axis=-1, keepdims=True)
    scale = lax.rsqrt(jnp.mean(center * center, axis=-1, keepdims=True) + EPSILON)
    return center * scale, scale


def norm_back(normed, inv_sigma, scale_row, grad):
    u = (1.0 + scale_row) * grad
    return (u - jnp.mean(u, axis=-1, keepdims=True) - normed * jnp.mean(u * normed, axis=-1, keepdims=True)) * inv_sigma


def gelu_and_slope(v):
    c = float(np.sqrt(2 / np.pi))
    square = v * v
    h = 0.5 + 0.5 * jnp.tanh(v * (c + (0.044715 * c) * square))
    slope = h + h * (1.0 - h) * (v * (2 * c + (6 * 0.044715 * c) * square))
    return (v * h).astype(BF), slope.astype(BF)


def body(
    n_dp, n_z, tokens, conditioning, frame_counts, w_qkv, w_out, w_up, w_down, w_ada, pos_table, cotangent
):
    micro, clip_dev, _, part, model = tokens.shape
    clips = micro * clip_dev
    assert clips == n_z and part * n_z == SPATIAL
    feature = model // n_dp
    qkv_tile, hidden_tile, out_tile = 3 * w_out.shape[1], w_up.shape[1], w_out.shape[1]
    d, z = lax.axis_index("dp"), lax.axis_index("tensor")
    count = lax.dynamic_slice_in_dim(frame_counts.reshape(clips), z, 1)

    order = jnp.asarray(dp_order(n_dp))[d & 1] ^ d
    source = (order[:, None] * feature + jnp.arange(feature)[None, :]).reshape(1, model)
    to_place = (jnp.arange(model)[:, None] == source).astype(BF)

    places = jnp.concatenate([order, (z - jnp.arange(n_z)) % n_z]).astype(jnp.int32)

    def placed(rows):
        return dot(rows, to_place).astype(BF)

    def unplaced(rows):
        return dot_nt(rows.astype(BF), to_place).astype(BF)

    place = jnp.arange(SPATIAL)
    place = (z - place // part) % n_z * part + place % part

    def for_clips(rows):
        rows = rows.reshape(clips, FRAMES, part, model)
        return [lax.dynamic_index_in_dim(rows, (z + r) % n_z, 0, False) for r in range(n_z)]

    def to_clip(parts):
        with jax.named_scope("tokens_in"):
            return shifted(parts, n_z, 1)

    def in_order(got):
        return placed(jnp.stack(got, axis=1).reshape(FRAMES * SPATIAL, model)).astype(F32)

    def from_clip(rows):
        rows = rows.reshape(FRAMES, n_z, part, model)
        return [rows[:, r] for r in range(n_z)]

    def by_clip(got):
        whole_rows = jnp.zeros((clips, FRAMES, part, model), BF)
        for r in range(n_z):
            whole_rows = lax.dynamic_update_index_in_dim(whole_rows, got[r], (z + r) % n_z, 0)
        return whole_rows.reshape(tokens.shape)

    def gather(name, shard, direct=True):
        return Chain("gather_" + name, gather_steps(n_dp, n_z, shard, direct), stages(n_dp) + (2 if direct else n_z))

    def scatter(name, halves, direct=True):
        return Chain("scatter_" + name, scatter_steps(n_dp, n_z, halves, direct), stages(n_dp) + (2 if direct else n_z))

    def sum_dp(name, halves):
        return Chain("scatter_" + name, scatter_steps(n_dp, n_z, halves, True), stages(n_dp) + 1)

    def exchange(name, pieces, sign):
        return Chain(name, exchange_steps(pieces, n_z, sign), 2)

    def butterfly(name, value, axis, size):
        return Chain(name, butterfly_steps(value, axis, size), size.bit_length() - 1)

    both = jnp.concatenate([w_qkv.reshape(feature, -1), w_out], axis=1)
    per_tile = both.shape[1] // out_tile
    wa = gather("attention", both)

    cond_float = conditioning.astype(F32).reshape(clips, model)
    cond_act = jax.nn.silu(cond_float).astype(BF)
    cond_mine = lax.all_to_all(
        cond_act.reshape(clips, n_dp, feature).transpose(1, 0, 2), "dp", 0, 0, tiled=True
    ).reshape(n_dp * clips, feature)
    mod_part = lax.all_to_all(dot(cond_mine, w_ada), ("dp", "tensor"), 0, 0, tiled=True)
    to_place, got_tokens, pos_table, places, count, mod_part = slot(
        [wa], to_place, for_clips(tokens), pos_table, places, count, mod_part
    )
    table = lax.all_to_all(jnp.broadcast_to(pos_table, (n_z,) + pos_table.shape), "tensor", 0, 0, tiled=True)
    mods = jnp.sum(mod_part.reshape(n_dp, n_z, -1), axis=0).reshape(6, model)
    mods = jnp.dot(mods, to_place.astype(F32), precision=HIGHEST).reshape(6, 1, model)
    got_tokens, table, mods, w_up = slot([wa], to_clip(got_tokens), table, mods, w_up)
    wu = Gathered(lax.all_gather(w_up, ("dp", "tensor"), axis=0).reshape(n_dp, n_z, feature, -1))
    resid = in_order(got_tokens)
    norm_a, inv_a = normalize(resid)
    normed_a = (norm_a * (1.0 + mods[1]) + mods[0]).astype(BF)
    normed_a, w_down = lax.optimization_barrier((normed_a, w_down))
    wd = gather("down", w_down)
    table = table[::-1]
    table = lax.dynamic_slice_in_dim(jnp.concatenate([table, table], axis=0), n_z - 1 - z, n_z, axis=0)
    bias = spread_bias(table.reshape(-1, OFFSETS), place)
    bias, normed_a, cotangent = slot([wa, wd], bias, normed_a, for_clips(cotangent))
    normed_a = slot([wa], normed_a)

    w_in = Pieces(whole(wa), both.shape[1], qkv_tile, lambda j: [j])
    w_mix = Pieces(wa.value, out_tile, out_tile, lambda j: [(2 * j + i) * per_tile + per_tile - 1 for i in (0, 1)])
    qkv, = rows_times(places, normed_a, w_in, qkv_tile * n_z, qkv_tile, lambda v: (v.astype(BF),), (), (BF,), "qkv")
    attended, probs = attend(count, qkv, bias, n_z)
    attended, probs, got_cotangent = slot([], attended, probs, to_clip(cotangent))
    branch_a = rows_times_t(places, attended, w_mix, 2 * out_tile, "out")
    middle = resid + mods[2] * branch_a
    norm_b, inv_b = normalize(middle)
    normed_b = (norm_b * (1.0 + mods[4]) + mods[3]).astype(BF)
    normed_b, got_cotangent = slot([wd], normed_b, got_cotangent)
    activ, slope = rows_times(places, normed_b, wu, hidden_tile * n_z, hidden_tile, gelu_and_slope, (), (BF, BF), "up")
    grad_result = in_order(got_cotangent)
    grad_bb = (grad_result * mods[5]).astype(BF)
    gd = rows_against(grad_bb, activ, hidden_tile, "grad_down")
    activ, slope, grad_bb, gd = slot([wd], activ, slope, grad_bb, gd)
    gd = scatter("down", gd)
    activ, slope, grad_bb = slot([wd, gd], activ, slope, grad_bb)

    wd = Pieces(whole(wd), hidden_tile, hidden_tile, lambda j: [j])
    grad_hidden, = rows_times(
        places, grad_bb, wd, hidden_tile * n_z, hidden_tile, lambda v, s: ((v * s.astype(F32)).astype(BF),), (slope,), (BF,),
        "grad_hidden",
    )
    gu = rows_against(normed_b, grad_hidden, hidden_tile, "grad_up", places, n_dp)
    grad_hidden, gu, activ = slot([gd], grad_hidden, gu, activ)
    gu = lax.psum_scatter(gu.reshape(model, -1), "dp", scatter_dimension=0, tiled=True)
    grad_nb = rows_times_t(places, grad_hidden, wu, hidden_tile, "grad_normed_b")
    branch_b = rows_times_t(places, activ, wd, hidden_tile, "down")
    grad_nb, branch_b = slot([gd], grad_nb, branch_b)
    grad_middle = grad_result + norm_back(norm_b, inv_b, mods[4], grad_nb)
    grad_ba = (grad_middle * mods[2]).astype(BF)
    go = rows_against(grad_ba, attended, out_tile * n_z, "grad_out")
    grad_att, = rows_times(
        places, grad_ba, w_mix, out_tile * n_z, 2 * out_tile, lambda v: (v.astype(BF),), (), (BF,), "grad_att"
    )
    block_out = from_clip(unplaced(middle + mods[5] * branch_b))
    grad_att, grad_middle, go, block_out = slot([gd], grad_att, grad_middle, go, block_out)
    go = sum_dp("out", go)
    out_rows = exchange("tokens_out", block_out, -1)
    grad_qkv, diag = attend_back(count, qkv, probs, grad_att, n_z)
    grad_qkv, diag = slot([go, out_rows], grad_qkv, diag)
    gq = rows_against(normed_a, grad_qkv, qkv_tile, "grad_qkv")
    gq, grad_qkv, gu = slot([go, out_rows], gq, grad_qkv, gu)
    gq = sum_dp("qkv", gq)
    grad_na = rows_times_t(places, grad_qkv, w_in, qkv_tile, "grad_normed_a")
    up_rows = shifted([gu[:, r * hidden_tile : (r + 1) * hidden_tile] for r in range(n_z)], n_z, -1)
    table = fold_bias(diag, place)
    grad_na, up_rows, table = slot([gq, go], grad_na, up_rows, table)
    out_up = functools.reduce(lambda a, b: a + b, [p.astype(F32) for p in up_rows])
    grad_tokens = from_clip(unplaced(grad_middle + norm_back(norm_a, inv_a, mods[1], grad_na)))
    in_rows = exchange("tokens_out", grad_tokens, -1)
    heads = table.shape[0] // n_z
    own = shifted([table[r * heads : (r + 1) * heads] for r in range(n_z)], n_z, -1)
    grad_mod = unplaced(
        jnp.stack(
            [
                jnp.sum(grad_na, axis=0),
                jnp.sum(grad_na * norm_a, axis=0),
                jnp.sum(grad_middle * branch_a, axis=0),
                jnp.sum(grad_nb, axis=0),
                jnp.sum(grad_nb * norm_b, axis=0),
                jnp.sum(grad_result * branch_b, axis=0),
            ]
        )
    ).reshape(1, n_z, -1)
    grad_mod = jnp.broadcast_to(grad_mod, (n_dp,) + grad_mod.shape[1:]).reshape(n_dp * n_z, -1)
    grad_mod, own = slot([gq, in_rows], grad_mod, functools.reduce(lambda a, b: a + b, own))

    table = butterfly("table", own, "dp", n_dp)
    block_out = by_clip(whole(out_rows))
    mod_cols = lax.all_to_all(grad_mod, ("dp", "tensor"), 0, 0, tiled=True)
    mod_cols, block_out, out_up = slot([gq, in_rows, table], mod_cols, block_out, out_up)
    pairs = [jnp.concatenate(p, axis=1) for p in zip(whole(gq), whole(go))]
    act_part = dot_nt(mod_cols, w_ada).reshape(n_dp, clips, feature)
    act_part = lax.all_to_all(act_part, "dp", 0, 0, tiled=True)
    act_part, pairs = slot([table], act_part, shifted(pairs, n_z, -1))
    pairs = functools.reduce(lambda a, b: a + b, [p.astype(F32) for p in pairs])
    grad_ada = dot_tn(cond_mine, mod_cols)
    grad_tokens = by_clip(whole(in_rows))
    act = butterfly("act", act_part, "tensor", n_z)
    slot([table, act])
    grad_act = whole(act).transpose(1, 0, 2).reshape(clips, model)
    grad_cond = jax.vjp(jax.nn.silu, cond_float)[1](grad_act)[0].reshape(conditioning.shape)
    grad_table = whole(table)
    return (
        block_out,
        grad_tokens,
        grad_cond,
        pairs[:, :qkv_tile].reshape(w_qkv.shape),
        pairs[:, qkv_tile:],
        out_up,
        whole(gd),
        grad_ada,
        grad_table,
    )


def solution(mesh):
    rows = P(None, "dp", None, "tensor", None)
    weight = P("dp", "tensor")
    qkv_weight = P("dp", None, "tensor")
    cond = P(None, "dp", None)
    table = P("tensor", None)
    return jax.shard_map(
        functools.partial(body, mesh.shape["dp"], mesh.shape["tensor"]),
        mesh=mesh,
        in_specs=(rows, cond, P(None, "dp"), qkv_weight, weight, weight, weight, weight, table, rows),
        out_specs=(rows, rows, cond, qkv_weight, weight, weight, weight, weight, table),
        check_vma=False,
    )
```

time: 683 us -> 511 us (0.75)
  Pallas kernels: 42.2 us -> 155 us
  matrix products: 124 us -> 25.7 us
  waiting for transfers between devices: 188 us -> 101 us
  local copies, waits for them, and re-layouts: 119 us -> 49 us
  starting transfers between devices: 146 us -> 98.8 us
  between operations: 2.12 us -> 15.4 us
    ppermute x85 -> x34, waiting for transfers between devices: 176 us -> 40.2 us  [the longest x9 19.6 us: scatter_steps(): got = lax.ppermute(send, 'dp', perm)]
    pallas_call x0 -> x12, Pallas kernels: none -> 119 us  [the longest x4 42 us: rows_times(): pl.pallas_call(kernel, grid_spec=pltpu.PrefetchScalarGridSpec(num_scalar_...]
    ppermute x85 -> x34, starting transfers between devices: 90.3 us -> 34 us  [the longest x6 11 us: exchange_steps(): pieces[r] = lax.ppermute(pieces[r], 'tensor', ring(n_z, sign * r))]
    unnamed x131 -> x154, local copies, waits for them, and re-layouts: 53.8 us -> 12 us
    dot_general x7 -> x3, matrix products: 39 us -> 4.83 us  [dot(): return jnp.dot(a, b, preferred_element_type=F32)]
    dot_general x8 -> x4, matrix products: 42.9 us -> 9.61 us  [dot_nt(): lax.dot_general(a, b, (((1,), (1,)), ((), ())), preferred_element_type=F32)]
    ppermute x6 -> x24, starting transfers between devices: 16 us -> 49 us  [shifted(): lax.ppermute(pieces[r], 'tensor', ring(n_z, sign * r))]
    dot_general x5 -> x1, matrix products: 33.4 us -> 1.16 us  [dot_tn(): lax.dot_general(a, b, (((0,), (0,)), ((), ())), preferred_element_type=F32)]
  transfers between devices with their start and end apart: 99 -> 65, of which waited for: 27 -> 20; matrix products, arithmetic and copies ran while one was open for 31% -> 23% of each run, Pallas kernels for 3% -> 31%
where the time goes in v2:
time: 511 us; the launch traced here: 503 us
  Pallas kernels  155 us (30%)
  waiting for transfers between devices  101 us (20%)
  starting transfers between devices  98.8 us (19%)
  other arithmetic  58.1 us (11%)
  local copies, waits for them, and re-layouts  49 us (10%)
  matrix products  25.7 us (5%)
  between operations  15.4 us (3%)
    ppermute x24, starting transfers between devices, shifted(): lax.ppermute(pieces[r], 'tensor', ring(n_z, sign * r))  49 us
    pallas_call x4, Pallas kernels, rows_times(): pl.pallas_call(kernel, grid_spec=pltpu.PrefetchScalarGridSpec(num_scalar_...  42 us
    pallas_call x4, Pallas kernels, rows_times_t(): pl.pallas_call(kernel, grid_spec=pltpu.PrefetchScalarGridSpec(num_scalar_...  40.9 us
    pallas_call x4, Pallas kernels, rows_against(): pl.pallas_call(kernel, grid_spec=pltpu.PrefetchScalarGridSpec(num_scalar_...  36.4 us
    ppermute x24, waiting for transfers between devices, shifted(): lax.ppermute(pieces[r], 'tensor', ring(n_z, sign * r))  23.9 us
    all_to_all x1, waiting for transfers between devices, body(): lax.all_to_all(jnp.broadcast_to(pos_table, (n_z,) + pos_table.shape), 'te...  22.6 us
    convert_element_type x9, other arithmetic, add_low(): return (first.astype(F32) + second.astype(F32)).astype(BF)  20 us
    ppermute x9, waiting for transfers between devices, scatter_steps(): got = lax.ppermute(send, 'dp', perm)  19.6 us
  transfers between devices with their start and end apart: 65, of which 20 were waited for; matrix products, arithmetic and copies ran while one was open for 23% of the time, Pallas kernels for 31%

profile of v2, /device:TPU:0, one launch (start us, length us, event | category | flops | bytes accessed | tf_op | source)
XLA Modules:
  0.0 503.5 jit_solution(10203486548439026256)
XLA Ops:
  32.7 10.1 %all-to-all-done.1 = f32[32,1,1536]{2,1,0:T(1,128)S(1)} async-done(((f32[32,1,1536]{2,1,0:T(1,128)}), f32[32,1,1536]{2,1,0:T(1,128)S(1)}, u32[]{:S(2)}, u32[]{:S(2)}) %all-to-all-start.1) | async-done | bytes 196640 | tf_op jit(solution)/shard_map/all_to_all | solution.py:552
  57.6 22.6 %all-to-all-done.2 = f32[4,4,2025]{2,1,0:T(4,128)S(1)} async-done(((f32[4,4,2025]{2,1,0:T(4,128)}), f32[4,4,2025]{2,1,0:T(4,128)S(1)}, u32[]{:S(2)}, u32[]{:S(2)}) %all-to-all-start.2) | async-done | bytes 129632 | tf_op jit(solution)/shard_map/all_to_all | solution.py:556
  100.5 4.5 fusion.27
  105.1 9.5 %collective-permute-done.10 = bf16[128,1024]{1,0:T(8,128)(2,1)} collective-permute-done((bf16[128,1024]{1,0:T(8,128)(2,1)}, bf16[128,1024]{1,0:T(8,128)(2,1)}, u32[]{:S(2)}, u32[]{:S(2)}) %collective-permute-start.10) | collective-permute-done | bytes 262176 | tf_op jit(solution)/shard_map/gather_down_4_left/ppermute | solution.py:137
  119.3 11.6 %collective-permute-start.17 = (bf16[10,16,1024]{2,1,0:T(8,128)(2,1)}, bf16[10,16,1024]{2,1,0:T(8,128)(2,1)}, u32[]{:S(2)}, u32[]{:S(2)}) collective-permute-start(bf16[10,16,1024]{2,1,0:T(8,128)(2,1)} %get-tuple-element.226), channel_id=1, source_target_pairs={{0,1},{1,2},{2,3},{3,0},{4,5},{5,6},{6,7},{7,4},{8,9},{9,10},{10,1... | collective-permute-start | bytes 983048 | tf_op jit(solution)/shard_map/tokens_in/ppermute | solution.py:137
  143.2 10.3 %qkv.1.qkv_ref = bf16[640,3072]{1,0:T(8,128)(2,1)} custom-call(s32[12]{0:T(128)} %pad_add_fusion.places_ref, bf16[640,1024]{1,0:T(8,128)(2,1)} %fusion.9.x_ref, bf16[128,4096]{1,0:T(8,128)(2,1)} %copy-done.1, bf16[128,4096]{1,0:T(8,128)(2,1)} %copy-done.2, bf16[128,4096]{1,0:T(8,128)(2,1)} %copy-done.3, ...), custom_call_target="tpu_custom_call" | custom-call | flops 1000000 | bytes 10000 | tf_op jit(solution)/shard_map/qkv/pallas_call | solution.py:240
  153.5 16.6 %attend.1 = (bf16[640,1024]{1,0:T(8,128)(2,1)}, bf16[2,16,320,320]{3,2,1,0:T(8,128)(2,1)}) custom-call(s32[1]{0:T(128)} %dynamic_slice.39.count_ref, bf16[640,3072]{1,0:T(8,128)(2,1)} %qkv.1.qkv_ref, f32[16,9,64,64]{3,2,1,0:T(8,128)} %copy.69.bias_ref), custom_call_target="tpu_custom_call" | custom-call | flops 1000000 | bytes 10000 | tf_op jit(solution)/shard_map/attend/pallas_call | solution.py:409
  170.2 6.0 %out.1 = f32[640,1024]{1,0:T(8,128)} custom-call(s32[12]{0:T(128)} %pad_add_fusion.places_ref, bf16[640,1024]{1,0:T(8,128)(2,1)} %get-tuple-element.229.x_ref.y_ref, bf16[128,4096]{1,0:T(8,128)(2,1)} %copy-done.1, bf16[128,4096]{1,0:T(8,128)(2,1)} %copy-done.1, bf16[128,4096]{1,0:T(8,128)(2,1)} %copy-done.2, bf16[128,4096]{1,0:T(8,128)(2,1)} %copy-done.2, ...), custom_call_target="tpu_custom_call" | custom-call | flops 1000000 | bytes 10000 | tf_op jit(solution)/shard_map/out/pallas_call | solution.py:270
  186.9 14.5 %up.1 = (bf16[640,4096]{1,0:T(8,128)(2,1)}, bf16[640,4096]{1,0:T(8,128)(2,1)}) custom-call(s32[12]{0:T(128)} %pad_add_fusion.places_ref, bf16[640,1024]{1,0:T(8,128)(2,1)} %add_convert_fusion.5.x_ref, bf16[8,4,128,1024]{3,2,1,0:T(8,128)(2,1)} %bitcast.119), custom_call_target="tpu_custom_call" | custom-call | flops 1000000 | bytes 10000 | tf_op jit(solution)/shard_map/up/pallas_call | solution.py:240
  201.4 10.7 %grad_down.1 = (bf16[512,4096]{1,0:T(8,128)(2,1)}, bf16[512,4096]{1,0:T(8,128)(2,1)}) custom-call(s32[1]{0:T(128)} %constant.214.clone.1.places_ref, bf16[640,1024]{1,0:T(8,128)(2,1)} %get-tuple-element.257.x_ref, bf16[640,4096]{1,0:T(8,128)(2,1)} %get-tuple-element.271.y_ref.x_ref), custom_call_target="tpu_custom_call" | custom-call | flops 1000000 | bytes 10000 | tf_op jit(solution)/shard_map/grad_down/pallas_call | solution.py:313
  213.2 6.4 %collective-permute-done.26 = bf16[512,4096]{1,0:T(8,128)(2,1)S(1)} collective-permute-done((bf16[512,4096]{1,0:T(8,128)(2,1)}, bf16[512,4096]{1,0:T(8,128)(2,1)S(1)}, u32[]{:S(2)}, u32[]{:S(2)}) %collective-permute-start.26) | collective-permute-done | bytes 4194336 | tf_op jit(solution)/shard_map/scatter_down_4_left/ppermute | solution.py:92
  219.6 4.3 add_convert_fusion
  226.5 11.9 %grad_hidden.1.y_ref.x_ref = bf16[640,4096]{1,0:T(8,128)(2,1)} custom-call(s32[12]{0:T(128)} %pad_add_fusion.places_ref, bf16[640,1024]{1,0:T(8,128)(2,1)} %get-tuple-element.257.x_ref, bf16[128,4096]{1,0:T(8,128)(2,1)} %constant_dynamic-update-slice_fusion.4.refs_0_, bf16[128,4096]{1,0:T(8,128)(2,1)} %collective-permute-done.12.refs_1_, ...), custom_call_target="tpu_custom_call" | custom-call | flops 1000000 | bytes 10000 | tf_op jit(solution)/shard_map/grad_hidden/pallas_call | solution.py:240
  238.3 11.7 %grad_up.1 = bf16[8,128,4096]{2,1,0:T(8,128)(2,1)} custom-call(s32[12]{0:T(128)} %pad_add_fusion.places_ref, bf16[640,1024]{1,0:T(8,128)(2,1)} %add_convert_fusion.5.x_ref, bf16[640,4096]{1,0:T(8,128)(2,1)} %grad_hidden.1.y_ref.x_ref), custom_call_target="tpu_custom_call" | custom-call | flops 1000000 | bytes 10000 | tf_op jit(solution)/shard_map/grad_up/pallas_call | solution.py:313
  256.0 11.4 %down.1 = f32[640,1024]{1,0:T(8,128)} custom-call(s32[12]{0:T(128)} %pad_add_fusion.places_ref, bf16[640,4096]{1,0:T(8,128)(2,1)} %get-tuple-element.271.y_ref.x_ref, bf16[128,4096]{1,0:T(8,128)(2,1)} %constant_dynamic-update-slice_fusion.4.refs_0_, bf16[128,4096]{1,0:T(8,128)(2,1)} %collective-permute-done.12.refs_1_, ...), custom_call_target="tpu_custom_call" | custom-call | flops 1000000 | bytes 10000 | tf_op jit(solution)/shard_map/down/pallas_call | solution.py:270
  267.4 13.1 %grad_normed_b.1 = f32[640,1024]{1,0:T(8,128)} custom-call(s32[12]{0:T(128)} %pad_add_fusion.places_ref, bf16[640,4096]{1,0:T(8,128)(2,1)} %grad_hidden.1.y_ref.x_ref, bf16[8,4,128,1024]{3,2,1,0:T(8,128)(2,1)} %bitcast.120), custom_call_target="tpu_custom_call" | custom-call | flops 1000000 | bytes 10000 | tf_op jit(solution)/shard_map/grad_normed_b/pallas_call | solution.py:270
  281.7 9.2 %collective-permute-start.29 = (bf16[128,1024]{1,0:T(8,128)(2,1)}, bf16[128,1024]{1,0:T(8,128)(2,1)}, u32[]{:S(2)}, u32[]{:S(2)}) collective-permute-start(bf16[128,1024]{1,0:T(8,128)(2,1)} %get-tuple-element.273), channel_id=1, source_target_pairs={{0,3},{1,0},{2,1},{3,2},{4,7},{5,4},{6,5},{7,6},{8,11},{9,8},{10,9... | collective-permute-start | bytes 786440 | tf_op jit(solution)/shard_map/scatter_down_1_left/ppermute | solution.py:137
  292.8 4.0 multiply_convert_fusion
  296.8 4.9 grad_out.1
  301.7 5.3 %grad_att.1.gatt_ref = bf16[640,1024]{1,0:T(8,128)(2,1)} custom-call(s32[12]{0:T(128)} %pad_add_fusion.places_ref, bf16[640,1024]{1,0:T(8,128)(2,1)} %get-tuple-element.415.x_ref, bf16[128,4096]{1,0:T(8,128)(2,1)} %copy-done.1, bf16[128,4096]{1,0:T(8,128)(2,1)} %copy-done.1, bf16[128,4096]{1,0:T(8,128)(2,1)} %copy-done.2, bf16[128,4096]{1,0:T(8,128)(2,1)} %copy-done.2, ...), custom_call_target="tpu_custom_call" | custom-call | flops 1000000 | bytes 10000 | tf_op jit(solution)/shard_map/grad_att/pallas_call | solution.py:240
  312.6 4.5 collective-permute-start.33
  317.1 19.0 %attend_back.1 = (bf16[640,3072]{1,0:T(8,128)(2,1)}, f32[16,9,64,64]{3,2,1,0:T(8,128)}) custom-call(s32[1]{0:T(128)} %dynamic_slice.39.count_ref, bf16[640,3072]{1,0:T(8,128)(2,1)} %qkv.1.qkv_ref, bf16[2,16,320,320]{3,2,1,0:T(8,128)(2,1)} %get-tuple-element.286.prob_ref, bf16[640,1024]{1,0:T(8,128)(2,1)} %grad_att.1.gatt_ref), custom_call_target="tpu_custom_call" | custom-call | flops 1000000 | bytes 10000 | tf_op jit(solution)/shard_map/attend_back/pallas_call | solution.py:437
  339.8 9.2 %grad_qkv.1 = (bf16[512,3072]{1,0:T(8,128)(2,1)}, bf16[512,3072]{1,0:T(8,128)(2,1)}) custom-call(s32[1]{0:T(128)} %constant.214.clone.1.places_ref, bf16[640,1024]{1,0:T(8,128)(2,1)} %fusion.9.x_ref, bf16[640,3072]{1,0:T(8,128)(2,1)} %get-tuple-element.304.y_ref.x_ref), custom_call_target="tpu_custom_call" | custom-call | flops 1000000 | bytes 10000 | tf_op jit(solution)/shard_map/grad_qkv/pallas_call | solution.py:313
  350.0 4.4 collective-permute-done.35
  371.6 10.4 %grad_normed_a.1 = f32[640,1024]{1,0:T(8,128)} custom-call(s32[12]{0:T(128)} %pad_add_fusion.places_ref, bf16[640,3072]{1,0:T(8,128)(2,1)} %get-tuple-element.304.y_ref.x_ref, bf16[128,4096]{1,0:T(8,128)(2,1)} %copy-done.1, bf16[128,4096]{1,0:T(8,128)(2,1)} %copy-done.2, bf16[128,4096]{1,0:T(8,128)(2,1)} %copy-done.3, ...), custom_call_target="tpu_custom_call" | custom-call | flops 1000000 | bytes 10000 | tf_op jit(solution)/shard_map/grad_normed_a/pallas_call | solution.py:270
  383.4 4.4 add_convert_fusion.2
  387.8 6.4 %collective-permute-done.40 = bf16[128,1024]{1,0:T(8,128)(2,1)S(1)} collective-permute-done((bf16[128,1024]{1,0:T(8,128)(2,1)}, bf16[128,1024]{1,0:T(8,128)(2,1)S(1)}, u32[]{:S(2)}, u32[]{:S(2)}) %collective-permute-start.40) | collective-permute-done | bytes 262176 | tf_op jit(solution)/shard_map/ppermute | solution.py:137
  403.5 5.0 convolution_convert_fusion
  412.4 11.3 %collective-permute-done.42 = bf16[256,3072]{1,0:T(8,128)(2,1)} collective-permute-done((bf16[256,3072]{1,0:T(8,128)(2,1)}, bf16[256,3072]{1,0:T(8,128)(2,1)}, u32[]{:S(2)}, u32[]{:S(2)}) %collective-permute-start.42) | collective-permute-done | bytes 1572896 | tf_op jit(solution)/shard_map/scatter_qkv_2_left/ppermute | solution.py:92
  449.0 8.2 %collective-permute-done.49 = bf16[10,16,1024]{2,1,0:T(8,128)(2,1)S(1)} collective-permute-done((bf16[10,16,1024]{2,1,0:T(8,128)(2,1)}, bf16[10,16,1024]{2,1,0:T(8,128)(2,1)S(1)}, u32[]{:S(2)}, u32[]{:S(2)}) %collective-permute-start.49) | collective-permute-done | bytes 327712 | tf_op jit(solution)/shard_map/tokens_out_1_left/ppermute | solution.py:144
  474.1 6.3 %collective-permute-done.53 = bf16[128,1024]{1,0:T(8,128)(2,1)} collective-permute-done((bf16[128,1024]{1,0:T(8,128)(2,1)}, bf16[128,1024]{1,0:T(8,128)(2,1)}, u32[]{:S(2)}, u32[]{:S(2)}) %collective-permute-start.53) | collective-permute-done | bytes 262176 | tf_op jit(solution)/shard_map/ppermute | solution.py:137
  480.5 6.1 %collective-permute-start.56 = (f32[8,4,128]{2,1,0:T(4,128)S(1)}, f32[8,4,128]{2,1,0:T(4,128)S(1)}, u32[]{:S(2)}, u32[]{:S(2)}) collective-permute-start(f32[8,4,128]{2,1,0:T(4,128)S(1)} %all-to-all-done.4), channel_id=1, source_target_pairs={{0,1},{1,0},{2,3},{3,2},{4,5},{5,4},{6,7},{7,6},{8,9},{9,8},{10,11... | collective-permute-start | bytes 49160 | tf_op jit(solution)/shard_map/act_2_left/ppermute | solution.py:151
  (384 shorter events, 194.3 us)
Async XLA Ops:
  9.4 33.4 %collective-permute-start = (bf16[128,1024]{1,0:T(8,128)(2,1)S(1)}, bf16[128,1024]{1,0:T(8,128)(2,1)S(1)}, u32[]{:S(2)}, u32[]{:S(2)}) collective-permute-start(bf16[128,1024]{1,0:T(8,128)(2,1)S(1)} %pad_maximum_fusion.2), channel_id=1, source_target_pairs={{0,1},{1,2},{2,3},{3,0},{4,5},{5,6},{6,7},{7,4},{8,9},{9,10},{10,1... | collective-permute-start | bytes 786440 | tf_op jit(solution)/shard_map/gather_attention_4_left/ppermute | solution.py:137
  12.5 30.3 %collective-permute-start.1 = (bf16[128,1024]{1,0:T(8,128)(2,1)S(1)}, bf16[128,1024]{1,0:T(8,128)(2,1)S(1)}, u32[]{:S(2)}, u32[]{:S(2)}) collective-permute-start(bf16[128,1024]{1,0:T(8,128)(2,1)S(1)} %pad_maximum_fusion.2), channel_id=1, source_target_pairs={{0,2},{1,3},{2,0},{3,1},{4,6},{5,7},{6,4},{7,5},{8,10},{9,11},{10,... | collective-permute-start | bytes 786440 | tf_op jit(solution)/shard_map/gather_attention_4_left/ppermute | solution.py:137
  15.0 27.8 %collective-permute-start.2 = (bf16[128,1024]{1,0:T(8,128)(2,1)S(1)}, bf16[128,1024]{1,0:T(8,128)(2,1)S(1)}, u32[]{:S(2)}, u32[]{:S(2)}) collective-permute-start(bf16[128,1024]{1,0:T(8,128)(2,1)S(1)} %pad_maximum_fusion.2), channel_id=1, source_target_pairs={{0,3},{1,0},{2,1},{3,2},{4,7},{5,4},{6,5},{7,6},{8,11},{9,8},{10,9... | collective-permute-start | bytes 786440 | tf_op jit(solution)/shard_map/gather_attention_4_left/ppermute | solution.py:137
  44.6 35.6 %collective-permute-start.3 = (bf16[128,4096]{1,0:T(8,128)(2,1)S(1)}, bf16[128,4096]{1,0:T(8,128)(2,1)S(1)}, u32[]{:S(2)}, u32[]{:S(2)}) collective-permute-start(bf16[128,4096]{1,0:T(8,128)(2,1)S(1)} %constant_dynamic-update-slice_fusion.refs_0_.refs_1_), channel_id=1, source_target_pairs={{0,8},{4,20},{8,0},{12,28},{16,24},{20,4},{24,16},{28,12},{1,9},{5... | collective-permute-start | bytes 3145736 | tf_op jit(solution)/shard_map/gather_attention_3_left/ppermute | solution.py:80
  45.7 34.5 %collective-permute-start.4 = (bf16[10,16,1024]{2,1,0:T(8,128)(2,1)}, bf16[10,16,1024]{2,1,0:T(8,128)(2,1)}, u32[]{:S(2)}, u32[]{:S(2)}) collective-permute-start(bf16[10,16,1024]{2,1,0:T(8,128)(2,1)} %get-tuple-element.186), channel_id=1, source_target_pairs={{0,1},{1,2},{2,3},{3,0},{4,5},{5,6},{6,7},{7,4},{8,9},{9,10},{10,1... | collective-permute-start | bytes 983048 | tf_op jit(solution)/shard_map/tokens_in/ppermute | solution.py:137
  46.3 33.9 %collective-permute-start.5 = (bf16[10,16,1024]{2,1,0:T(8,128)(2,1)S(1)}, bf16[10,16,1024]{2,1,0:T(8,128)(2,1)}, u32[]{:S(2)}, u32[]{:S(2)}) collective-permute-start(bf16[10,16,1024]{2,1,0:T(8,128)(2,1)S(1)} %get-tuple-element.187), channel_id=1, source_target_pairs={{0,2},{1,3},{2,0},{3,1},{4,6},{5,7},{6,4},{7,5},{8,10},{9,11},{10,... | collective-permute-start | bytes 983048 | tf_op jit(solution)/shard_map/tokens_in/ppermute | solution.py:137
  48.3 31.9 %collective-permute-start.6 = (bf16[10,16,1024]{2,1,0:T(8,128)(2,1)S(1)}, bf16[10,16,1024]{2,1,0:T(8,128)(2,1)}, u32[]{:S(2)}, u32[]{:S(2)}) collective-permute-start(bf16[10,16,1024]{2,1,0:T(8,128)(2,1)S(1)} %get-tuple-element.188), channel_id=1, source_target_pairs={{0,3},{1,0},{2,1},{3,2},{4,7},{5,4},{6,5},{7,6},{8,11},{9,8},{10,9... | collective-permute-start | bytes 983048 | tf_op jit(solution)/shard_map/tokens_in/ppermute | solution.py:137
  51.1 29.1 %all-to-all-start.2 = ((f32[4,4,2025]{2,1,0:T(4,128)}), f32[4,4,2025]{2,1,0:T(4,128)S(1)}, u32[]{:S(2)}, u32[]{:S(2)}) async-start(f32[4,4,2025]{2,1,0:T(4,128)} %broadcast_in_dim.56), calls=%async_computation.2 | async-start | bytes 262144 | tf_op jit(solution)/shard_map/all_to_all | solution.py:556
  54.4 132.5 %all-gather.3.cloned.1.call-start = ((), (), s32[]{:S(2)}) async-start(), calls=%async_computation.7 | async-start | bytes 8650752 | tf_op jit(solution)/shard_map/all_gather | solution.py:560
  80.2 274.8 %reduce-scatter.2.cloned.1.call-start = ((), (), s32[]{:S(2)}) async-start(), calls=%async_computation.6 | async-start | bytes 9437184 | tf_op jit(solution)/shard_map/reduce_scatter | solution.py:597
  84.5 30.1 %collective-permute-start.7 = (bf16[128,4096]{1,0:T(8,128)(2,1)S(1)}, bf16[128,4096]{1,0:T(8,128)(2,1)S(1)}, u32[]{:S(2)}, u32[]{:S(2)}) collective-permute-start(bf16[128,4096]{1,0:T(8,128)(2,1)S(1)} %constant_dynamic-update-slice_fusion.refs_0_.refs_1_), channel_id=1, source_target_pairs={{0,16},{4,12},{8,24},{12,4},{16,0},{20,28},{24,8},{28,20},{1,17},{... | collective-permute-start | bytes 3145736 | tf_op jit(solution)/shard_map/gather_attention_2_left/ppermute | solution.py:80
  85.4 29.2 %collective-permute-start.8 = (bf16[128,4096]{1,0:T(8,128)(2,1)S(1)}, bf16[128,4096]{1,0:T(8,128)(2,1)}, u32[]{:S(2)}, u32[]{:S(2)}) collective-permute-start(bf16[128,4096]{1,0:T(8,128)(2,1)S(1)} %collective-permute-done.3.refs_1_.refs_2_.refs_3_), channel_id=1, source_target_pairs={{0,16},{4,12},{8,24},{12,4},{16,0},{20,28},{24,8},{28,20},{1,17},{... | collective-permute-start | bytes 3145736 | tf_op jit(solution)/shard_map/gather_attention_2_left/ppermute | solution.py:80
  92.4 22.2 %collective-permute-start.10 = (bf16[128,1024]{1,0:T(8,128)(2,1)}, bf16[128,1024]{1,0:T(8,128)(2,1)}, u32[]{:S(2)}, u32[]{:S(2)}) collective-permute-start(bf16[128,1024]{1,0:T(8,128)(2,1)} %param.17), channel_id=1, source_target_pairs={{0,2},{1,3},{2,0},{3,1},{4,6},{5,7},{6,4},{7,5},{8,10},{9,11},{10,... | collective-permute-start | bytes 786440 | tf_op jit(solution)/shard_map/gather_down_4_left/ppermute | solution.py:137
  92.4 22.2 %collective-permute-start.11 = (bf16[128,1024]{1,0:T(8,128)(2,1)}, bf16[128,1024]{1,0:T(8,128)(2,1)}, u32[]{:S(2)}, u32[]{:S(2)}) collective-permute-start(bf16[128,1024]{1,0:T(8,128)(2,1)} %param.17), channel_id=1, source_target_pairs={{0,3},{1,0},{2,1},{3,2},{4,7},{5,4},{6,5},{7,6},{8,11},{9,8},{10,9... | collective-permute-start | bytes 786440 | tf_op jit(solution)/shard_map/gather_down_4_left/ppermute | solution.py:137
  115.2 25.1 %collective-permute-start.15 = (bf16[128,4096]{1,0:T(8,128)(2,1)S(1)}, bf16[128,4096]{1,0:T(8,128)(2,1)S(1)}, u32[]{:S(2)}, u32[]{:S(2)}) collective-permute-start(bf16[128,4096]{1,0:T(8,128)(2,1)S(1)} %collective-permute-done.7.refs_2_.refs_4_.refs_5_), channel_id=1, source_target_pairs={{0,4},{4,0},{8,12},{12,8},{16,20},{20,16},{24,28},{28,24},{1,5},{5... | collective-permute-start | bytes 3145736 | tf_op jit(solution)/shard_map/gather_attention_1_left/ppermute | solution.py:81
  115.3 26.8 %collective-permute-start.16 = (bf16[128,4096]{1,0:T(8,128)(2,1)}, bf16[128,4096]{1,0:T(8,128)(2,1)S(1)}, u32[]{:S(2)}, u32[]{:S(2)}) collective-permute-start(bf16[128,4096]{1,0:T(8,128)(2,1)} %collective-permute-done.8.refs_3_.refs_6_.refs_7_), channel_id=1, source_target_pairs={{0,4},{4,0},{8,12},{12,8},{16,20},{20,16},{24,28},{28,24},{1,5},{5... | collective-permute-start | bytes 3145736 | tf_op jit(solution)/shard_map/gather_attention_1_left/ppermute | solution.py:81
  119.3 50.8 %collective-permute-start.17 = (bf16[10,16,1024]{2,1,0:T(8,128)(2,1)}, bf16[10,16,1024]{2,1,0:T(8,128)(2,1)}, u32[]{:S(2)}, u32[]{:S(2)}) collective-permute-start(bf16[10,16,1024]{2,1,0:T(8,128)(2,1)} %get-tuple-element.226), channel_id=1, source_target_pairs={{0,1},{1,2},{2,3},{3,0},{4,5},{5,6},{6,7},{7,4},{8,9},{9,10},{10,1... | collective-permute-start | bytes 983048 | tf_op jit(solution)/shard_map/tokens_in/ppermute | solution.py:137
  132.6 37.5 %collective-permute-start.18 = (bf16[10,16,1024]{2,1,0:T(8,128)(2,1)}, bf16[10,16,1024]{2,1,0:T(8,128)(2,1)S(1)}, u32[]{:S(2)}, u32[]{:S(2)}) collective-permute-start(bf16[10,16,1024]{2,1,0:T(8,128)(2,1)} %get-tuple-element.227), channel_id=1, source_target_pairs={{0,2},{1,3},{2,0},{3,1},{4,6},{5,7},{6,4},{7,5},{8,10},{9,11},{10,... | collective-permute-start | bytes 983048 | tf_op jit(solution)/shard_map/tokens_in/ppermute | solution.py:137
  132.7 37.4 %collective-permute-start.19 = (bf16[10,16,1024]{2,1,0:T(8,128)(2,1)S(1)}, bf16[10,16,1024]{2,1,0:T(8,128)(2,1)S(1)}, u32[]{:S(2)}, u32[]{:S(2)}) collective-permute-start(bf16[10,16,1024]{2,1,0:T(8,128)(2,1)S(1)} %copy-done.32), channel_id=1, source_target_pairs={{0,3},{1,0},{2,1},{3,2},{4,7},{5,4},{6,5},{7,6},{8,11},{9,8},{10,9... | collective-permute-start | bytes 983048 | tf_op jit(solution)/shard_map/tokens_in/ppermute | solution.py:137
  140.3 40.3 %collective-permute-start.12 = (bf16[128,4096]{1,0:T(8,128)(2,1)}, bf16[128,4096]{1,0:T(8,128)(2,1)}, u32[]{:S(2)}, u32[]{:S(2)}) collective-permute-start(bf16[128,4096]{1,0:T(8,128)(2,1)} %constant_dynamic-update-slice_fusion.4.refs_0_), channel_id=1, source_target_pairs={{0,8},{4,20},{8,0},{12,28},{16,24},{20,4},{24,16},{28,12},{1,9},{5... | collective-permute-start | bytes 3145736 | tf_op jit(solution)/shard_map/gather_down_3_left/ppermute | solution.py:80
  180.6 31.4 %collective-permute-start.20 = (bf16[128,4096]{1,0:T(8,128)(2,1)}, bf16[128,4096]{1,0:T(8,128)(2,1)}, u32[]{:S(2)}, u32[]{:S(2)}) collective-permute-start(bf16[128,4096]{1,0:T(8,128)(2,1)} %constant_dynamic-update-slice_fusion.4.refs_0_), channel_id=1, source_target_pairs={{0,16},{4,12},{8,24},{12,4},{16,0},{20,28},{24,8},{28,20},{1,17},{... | collective-permute-start | bytes 3145736 | tf_op jit(solution)/shard_map/gather_down_2_left/ppermute | solution.py:80
  180.6 31.4 %collective-permute-start.21 = (bf16[128,4096]{1,0:T(8,128)(2,1)}, bf16[128,4096]{1,0:T(8,128)(2,1)}, u32[]{:S(2)}, u32[]{:S(2)}) collective-permute-start(bf16[128,4096]{1,0:T(8,128)(2,1)} %collective-permute-done.12.refs_1_), channel_id=1, source_target_pairs={{0,16},{4,12},{8,24},{12,4},{16,0},{20,28},{24,8},{28,20},{1,17},{... | collective-permute-start | bytes 3145736 | tf_op jit(solution)/shard_map/gather_down_2_left/ppermute | solution.py:80
  225.5 26.4 %collective-permute-start.27 = (bf16[256,4096]{1,0:T(8,128)(2,1)}, bf16[256,4096]{1,0:T(8,128)(2,1)}, u32[]{:S(2)}, u32[]{:S(2)}) collective-permute-start(bf16[256,4096]{1,0:T(8,128)(2,1)} %get-tuple-element.256), channel_id=1, source_target_pairs={{0,16},{4,12},{8,24},{12,4},{16,0},{20,28},{24,8},{28,20},{1,17},{... | collective-permute-start | bytes 6291464 | tf_op jit(solution)/shard_map/scatter_down_3_left/ppermute | solution.py:92
  255.6 24.9 %collective-permute-start.28 = (bf16[128,4096]{1,0:T(8,128)(2,1)}, bf16[128,4096]{1,0:T(8,128)(2,1)S(1)}, u32[]{:S(2)}, u32[]{:S(2)}) collective-permute-start(bf16[128,4096]{1,0:T(8,128)(2,1)} %get-tuple-element.269), channel_id=1, source_target_pairs={{0,8},{4,20},{8,0},{12,28},{16,24},{20,4},{24,16},{28,12},{1,9},{5... | collective-permute-start | bytes 3145736 | tf_op jit(solution)/shard_map/scatter_down_2_left/ppermute | solution.py:92
  281.7 27.1 %collective-permute-start.29 = (bf16[128,1024]{1,0:T(8,128)(2,1)}, bf16[128,1024]{1,0:T(8,128)(2,1)}, u32[]{:S(2)}, u32[]{:S(2)}) collective-permute-start(bf16[128,1024]{1,0:T(8,128)(2,1)} %get-tuple-element.273), channel_id=1, source_target_pairs={{0,3},{1,0},{2,1},{3,2},{4,7},{5,4},{6,5},{7,6},{8,11},{9,8},{10,9... | collective-permute-start | bytes 786440 | tf_op jit(solution)/shard_map/scatter_down_1_left/ppermute | solution.py:137
  312.5 23.5 %collective-permute-start.32 = (bf16[512,1024]{1,0:T(8,128)(2,1)S(1)}, bf16[512,1024]{1,0:T(8,128)(2,1)S(1)}, u32[]{:S(2)}, u32[]{:S(2)}) collective-permute-start(bf16[512,1024]{1,0:T(8,128)(2,1)S(1)} %copy-done.69), channel_id=1, source_target_pairs={{0,4},{4,0},{8,12},{12,8},{16,20},{20,16},{24,28},{28,24},{1,5},{5... | collective-permute-start | bytes 3145736 | tf_op jit(solution)/shard_map/scatter_out_3_left/ppermute | solution.py:92
  312.6 23.9 %collective-permute-start.33 = (bf16[10,16,1024]{2,1,0:T(8,128)(2,1)S(1)}, bf16[10,16,1024]{2,1,0:T(8,128)(2,1)S(1)}, u32[]{:S(2)}, u32[]{:S(2)}) collective-permute-start(bf16[10,16,1024]{2,1,0:T(8,128)(2,1)S(1)} %get-tuple-element.284), channel_id=1, source_target_pairs={{0,2},{1,3},{2,0},{3,1},{4,6},{5,7},{6,4},{7,5},{8,10},{9,11},{10,... | collective-permute-start | bytes 983048 | tf_op jit(solution)/shard_map/tokens_out_2_left/ppermute | solution.py:144
  355.1 28.3 %collective-permute-start.37 = (bf16[512,3072]{1,0:T(8,128)(2,1)}, bf16[512,3072]{1,0:T(8,128)(2,1)}, u32[]{:S(2)}, u32[]{:S(2)}) collective-permute-start(bf16[512,3072]{1,0:T(8,128)(2,1)} %get-tuple-element.301), channel_id=1, source_target_pairs={{0,4},{4,0},{8,12},{12,8},{16,20},{20,16},{24,28},{28,24},{1,5},{5... | collective-permute-start | bytes 9437192 | tf_op jit(solution)/shard_map/scatter_qkv_3_left/ppermute | solution.py:92
  369.7 24.5 %collective-permute-start.40 = (bf16[128,1024]{1,0:T(8,128)(2,1)}, bf16[128,1024]{1,0:T(8,128)(2,1)S(1)}, u32[]{:S(2)}, u32[]{:S(2)}) collective-permute-start(bf16[128,1024]{1,0:T(8,128)(2,1)} %get-tuple-element.457), channel_id=1, source_target_pairs={{0,2},{1,3},{2,0},{3,1},{4,6},{5,7},{6,4},{7,5},{8,10},{9,11},{10,... | collective-permute-start | bytes 786440 | tf_op jit(solution)/shard_map/ppermute | solution.py:137
  370.2 24.0 %collective-permute-start.41 = (bf16[128,1024]{1,0:T(8,128)(2,1)S(1)}, bf16[128,1024]{1,0:T(8,128)(2,1)S(1)}, u32[]{:S(2)}, u32[]{:S(2)}) collective-permute-start(bf16[128,1024]{1,0:T(8,128)(2,1)S(1)} %get-tuple-element.456), channel_id=1, source_target_pairs={{0,1},{1,2},{2,3},{3,0},{4,5},{5,6},{6,7},{7,4},{8,9},{9,10},{10,1... | collective-permute-start | bytes 786440 | tf_op jit(solution)/shard_map/ppermute | solution.py:137
  402.9 20.7 %collective-permute-start.42 = (bf16[256,3072]{1,0:T(8,128)(2,1)}, bf16[256,3072]{1,0:T(8,128)(2,1)}, u32[]{:S(2)}, u32[]{:S(2)}) collective-permute-start(bf16[256,3072]{1,0:T(8,128)(2,1)} %get-tuple-element.308), channel_id=1, source_target_pairs={{0,16},{4,12},{8,24},{12,4},{16,0},{20,28},{24,8},{28,20},{1,17},{... | collective-permute-start | bytes 4718600 | tf_op jit(solution)/shard_map/scatter_qkv_2_left/ppermute | solution.py:92
  460.5 20.0 %collective-permute-start.53 = (bf16[128,1024]{1,0:T(8,128)(2,1)}, bf16[128,1024]{1,0:T(8,128)(2,1)}, u32[]{:S(2)}, u32[]{:S(2)}) collective-permute-start(bf16[128,1024]{1,0:T(8,128)(2,1)} %pad_maximum_fusion.5), channel_id=1, source_target_pairs={{0,2},{1,3},{2,0},{3,1},{4,6},{5,7},{6,4},{7,5},{8,10},{9,11},{10,... | collective-permute-start | bytes 786440 | tf_op jit(solution)/shard_map/ppermute | solution.py:137
  (104 other events, 1224.4 us)
Sparse Core Ops, SparseCore 0:
  80.4 102.2 all-gather.2
  255.7 76.2 reduce-scatter.1

commit v3 on v2

--- a/solution.py
+++ b/solution.py
@@ -5,6 +5,7 @@
 import numpy as np
 from jax import lax
 from jax.experimental import pallas as pl
+from jax.experimental.layout import Layout, with_layout_constraint
 from jax.experimental.pallas import tpu as pltpu
 from jax.sharding import PartitionSpec as P
 
@@ -25,7 +26,7 @@
 SPREAD = 2 * WIN_T - 1
 DIAG = SPREAD * SPATIAL
 GROUPS = 4
-VMEM = 56 << 20
+VMEM = 48 << 20
 
 
 def stage_bits(n_dp, core):
@@ -61,50 +62,93 @@
     )
 
 
-def merged(pieces):
-    if len(pieces) <= GROUPS:
-        return pieces
-    return [jnp.concatenate(pieces[i : i + 2], axis=0) for i in range(0, len(pieces), 2)]
-
-
-def gather_steps(n_dp, n_z, shard, direct):
-    blocks = [shard]
-    if direct:
-        blocks = yield shifted([shard] * n_z, n_z, 1)
+def join(blocks, axis):
+    return join_parts(blocks, axis, [blocks[0].shape[1]])[0]
+
+
+def join_parts(blocks, axis, widths):
+    rows, count = blocks[0].shape[0], len(blocks)
+
+    def kernel(*refs):
+        low = 0
+        for out, width in zip(refs[count:], widths):
+            for i, ref in enumerate(refs[:count]):
+                if axis == 0:
+                    out[i * rows : (i + 1) * rows, :] = ref[:, low : low + width]
+                else:
+                    out[:, i * width : (i + 1) * width] = ref[:, low : low + width]
+            low += width
+
+    shapes = [(rows * count, w) if axis == 0 else (rows, w * count) for w in widths]
+    return pl.pallas_call(
+        kernel,
+        out_shape=[jax.ShapeDtypeStruct(s, blocks[0].dtype) for s in shapes],
+        compiler_params=params(),
+        cost_estimate=COST,
+        name="join",
+    )(*blocks)
+
+
+def place_perm(n_dp, place):
+    order = dp_order(n_dp)
+    return [(i, i ^ int(order[i & 1, place])) for i in range(n_dp)]
+
+
+def gather_steps(n_dp, n_z, rows, at_once):
+    if at_once:
+        rows = yield [rows] + [lax.ppermute(rows, "dp", place_perm(n_dp, k)) for k in range(1, n_dp // 2)]
     else:
-        for _ in range(n_z - 1):
-            blocks = yield blocks + [lax.ppermute(blocks[-1], "tensor", ring(n_z, 1))]
-    pieces = [jnp.concatenate(blocks, axis=1)]
-    for t in range(stages(n_dp)):
-        perm = stage_perm(n_dp, t)
-        pieces = yield merged(pieces + [lax.ppermute(p, "dp", perm) for p in pieces])
-    yield pieces + [lax.ppermute(p, "dp", core_perm(n_dp)) for p in pieces]
-
-
-def add_low(first, second):
-    return (first.astype(F32) + second.astype(F32)).astype(BF)
-
-
-def scatter_steps(n_dp, n_z, halves, direct):
+        for t in range(stages(n_dp)):
+            got = lax.ppermute(rows, "dp", stage_perm(n_dp, t))
+            rows, got = yield rows, got
+            rows = join([rows, got], 0) if t < stages(n_dp) - 1 else [rows, got]
+    yield rows + [lax.ppermute(p, "dp", core_perm(n_dp)) for p in rows]
+
+
+def add_low(first, *others):
+    return functools.reduce(lambda a, b: a + b, [o.astype(F32) for o in others], first.astype(F32)).astype(BF)
+
+
+def scatter_steps(n_dp, n_z, halves, at_once):
     keep, send = halves
-    for t in range(stages(n_dp), -1, -1):
-        perm = core_perm(n_dp) if t == stages(n_dp) else stage_perm(n_dp, t)
-        got = lax.ppermute(send, "dp", perm)
-        if t:
+    got = lax.ppermute(send, "dp", core_perm(n_dp))
+    if at_once:
+        count = n_dp // 2
+        rows = keep.shape[0] // count
+        mine = yield [add_low(keep[k * rows : (k + 1) * rows], got[k * rows : (k + 1) * rows]) for k in range(count)]
+        terms = mine[:1] + [lax.ppermute(mine[k], "dp", place_perm(n_dp, k)) for k in range(1, count)]
+    else:
+        for t in range(stages(n_dp) - 1, -1, -1):
             rows = keep.shape[0] // 2
             keep, send = yield add_low(keep[:rows], got[:rows]), add_low(keep[rows:], got[rows:])
-    width = keep.shape[1] // n_z
-    part = [add_low(keep[:, r * width : (r + 1) * width], got[:, r * width : (r + 1) * width]) for r in range(n_z)]
-    part = yield part
-    if direct:
-        yield functools.reduce(lambda a, b: a + b, [p.astype(F32) for p in shifted(part, n_z, -1)])
+            got = lax.ppermute(send, "dp", stage_perm(n_dp, t))
+        terms = [keep, got]
+    if at_once:
+        yield terms
         return
-    for r in range(n_z - 2, -1, -1):
-        total = lax.ppermute(part[r + 1], "tensor", ring(n_z, -1))
-        if r:
-            part = yield part[:r] + [add_low(part[r], total)]
-        else:
-            yield part[0].astype(F32) + total.astype(F32)
+    width = terms[0].shape[1] // n_z
+    yield [add_low(*(v[:, r * width : (r + 1) * width] for v in terms)) for r in range(n_z)]
+
+
+def attention_parts(terms, beside, n_z):
+    rows = beside.shape[0]
+    wide, narrow = terms[0].shape[1] // n_z, beside.shape[1] // n_z
+
+    def kernel(*refs):
+        for r, out in enumerate(refs[-n_z:]):
+            total = refs[0][:, r * wide : (r + 1) * wide].astype(F32)
+            for ref in refs[1 : -n_z - 1]:
+                total = total + ref[:, r * wide : (r + 1) * wide].astype(F32)
+            out[:, :wide] = total.astype(BF)
+            out[:, wide:] = refs[-n_z - 1][:, r * narrow : (r + 1) * narrow]
+
+    return pl.pallas_call(
+        kernel,
+        out_shape=[jax.ShapeDtypeStruct((rows, wide + narrow), BF)] * n_z,
+        compiler_params=params(),
+        cost_estimate=COST,
+        name="attention_parts",
+    )(*terms, beside)
 
 
 class Chain:
@@ -137,9 +181,9 @@
     return [pieces[0]] + [lax.ppermute(pieces[r], "tensor", ring(n_z, sign * r)) for r in range(1, n_z)]
 
 
-def exchange_steps(pieces, n_z, sign):
+def exchange_steps(pieces, n_z, sign, first):
     pieces = list(pieces)
-    for group in ([n_z // 2], [r for r in range(1, n_z) if r != n_z // 2]):
+    for group in (first, [r for r in range(1, n_z) if r not in first]):
         for r in group:
             pieces[r] = lax.ppermute(pieces[r], "tensor", ring(n_z, sign * r))
         pieces = yield pieces
@@ -192,35 +236,26 @@
 
 
 class Pieces:
-    def __init__(self, pieces, width, take, at):
-        self.many, self.pieces = len(at(0)), len(pieces)
-        self.arrays = [p for p in pieces for _ in range(self.many)]
-        self.width, self.take, self.at = width, take, at
-        self.rows = sum(p.shape[0] for p in pieces)
+    def __init__(self, arrays, width):
+        self.arrays, self.width = arrays, width
+        self.rows = sum(a.shape[0] for a in arrays)
 
     def specs(self):
-        return [
-            pl.BlockSpec((a.shape[0], self.width), lambda j, p, i=i % self.many: (0, self.at(j)[i]))
-            for i, a in enumerate(self.arrays)
-        ]
+        return [pl.BlockSpec((a.shape[0], self.width), lambda j, p: (0, j)) for a in self.arrays]
 
     def load(self, refs, places):
-        rows = [
-            jnp.concatenate([r[:, : self.take] for r in refs[i : i + self.many]], axis=1)
-            for i in range(0, len(refs), self.many)
-        ]
-        return jnp.concatenate(rows, axis=0)
+        return jnp.concatenate([r[...] for r in refs], axis=0)
 
 
 class Gathered:
-    def __init__(self, array):
-        self.arrays = [array]
-        self.count, self.width = array.shape[0], array.shape[3]
-        self.rows = array.shape[0] * array.shape[2]
+    def __init__(self, array, which, of):
+        self.arrays, self.which, self.count = [array], which, array.shape[0]
+        self.each = array.shape[2] // of
+        self.rows = self.count * self.each
 
     def specs(self):
-        n_dp, _, rows, columns = self.arrays[0].shape
-        return [pl.BlockSpec((n_dp, 1, rows, columns), lambda j, p: (0, p[n_dp + j], 0, 0))]
+        n_dp, _, _, columns = self.arrays[0].shape
+        return [pl.BlockSpec((n_dp, 1, self.each, columns), lambda j, p: (0, p[n_dp + j], self.which, 0))]
 
     def load(self, refs, places):
         return jnp.concatenate([refs[0][places[k], 0] for k in range(self.count)], axis=0)
@@ -252,34 +287,61 @@
     )(places, x, *weight.arrays, *extra)
 
 
-def rows_times_t(places, x, weight, tile, name):
+def rows_times_t(places, x, weight, tile, finish, by_row, const, row_outs, sums, name):
     length, depth = x.shape
-    count = len(weight.arrays)
+    count, steps, chunk = len(weight.arrays), depth // tile, SPATIAL * 2
+    n_by, n_const, n_out = len(by_row), len(const), len(row_outs)
 
     def kernel(places_ref, x_ref, *refs):
-        term = dot_nt(x_ref[...], weight.load(refs[:count], places_ref))
+        parts = iter(refs)
+        w_refs, by_refs, const_refs, out_refs = ([next(parts) for _ in range(n)] for n in (count, n_by, n_const, n_out))
+        sum_ref = next(parts) if sums else None
+        acc = next(parts)
+        term = dot_nt(x_ref[...], weight.load(w_refs, places_ref))
 
         @pl.when(pl.program_id(0) == 0)
         def _():
-            refs[count][...] = term
+            acc[...] = term
 
         @pl.when(pl.program_id(0) > 0)
         def _():
-            refs[count][...] += term
-
+            acc[...] += term
+
+        @pl.when(pl.program_id(0) == steps - 1)
+        def _():
+            totals = None
+            for i in range(0, length, chunk):
+                rows = slice(i, i + chunk)
+                done, adds = finish(acc[rows], *(r[rows] for r in by_refs), *(r[...] for r in const_refs))
+                for ref, value in zip(out_refs, done):
+                    ref[rows] = value
+                adds = [jnp.sum(v, axis=0, keepdims=True) for v in adds]
+                totals = adds if totals is None else [t + v for t, v in zip(totals, adds)]
+            if sums:
+                sum_ref[...] = jnp.concatenate(totals, axis=0)
+
+    def full(shape):
+        return pl.BlockSpec(shape, lambda j, p: (0, 0))
+
+    shapes = [jax.ShapeDtypeStruct(s, t) for s, t in row_outs]
+    if sums:
+        shapes.append(jax.ShapeDtypeStruct((sums, weight.rows), F32))
     return pl.pallas_call(
         kernel,
         grid_spec=pltpu.PrefetchScalarGridSpec(
             num_scalar_prefetch=1,
-            grid=(depth // tile,),
-            in_specs=[pl.BlockSpec((length, tile), lambda j, p: (0, j))] + weight.specs(),
-            out_specs=pl.BlockSpec((length, weight.rows), lambda j, p: (0, 0)),
+            grid=(steps,),
+            in_specs=[pl.BlockSpec((length, tile), lambda j, p: (0, j))]
+            + weight.specs()
+            + [full(v.shape) for v in (*by_row, *const)],
+            out_specs=[full(v.shape) for v in shapes],
+            scratch_shapes=[pltpu.VMEM((length, weight.rows), F32)],
         ),
-        out_shape=jax.ShapeDtypeStruct((length, weight.rows), F32),
+        out_shape=shapes,
         compiler_params=params(),
         cost_estimate=COST,
         name=name,
-    )(places, x, *weight.arrays)
+    )(places, x, *weight.arrays, *by_row, *const)
 
 
 def rows_against(x, y, tile, name, places=None, n_dp=1):
@@ -470,6 +532,32 @@
     return (u - jnp.mean(u, axis=-1, keepdims=True) - normed * jnp.mean(u * normed, axis=-1, keepdims=True)) * inv_sigma
 
 
+def after_attention(branch_a, resid, mods):
+    middle = resid.astype(F32) + mods[2:3] * branch_a
+    normed = (normalize(middle)[0] * (1.0 + mods[4:5]) + mods[3:4]).astype(BF)
+    return (branch_a, middle, normed), ()
+
+
+def after_mlp(branch_b, middle, grad_result, mods, to_place):
+    result = (middle + mods[5:6] * branch_b).astype(BF)
+    return (dot_nt(result, to_place).astype(BF),), (grad_result.astype(F32) * branch_b,)
+
+
+def back_mlp(grad_nb, middle, branch_a, grad_result, mods):
+    norm_b, inv_b = normalize(middle)
+    grad_middle = grad_result.astype(F32) + norm_back(norm_b, inv_b, mods[4:5], grad_nb)
+    return (
+        (grad_middle, (grad_middle * mods[2:3]).astype(BF)),
+        (grad_middle * branch_a, grad_nb, grad_nb * norm_b),
+    )
+
+
+def back_attention(grad_na, resid, grad_middle, mods, to_place):
+    norm_a, inv_a = normalize(resid.astype(F32))
+    grad_tokens = (grad_middle + norm_back(norm_a, inv_a, mods[1:2], grad_na)).astype(BF)
+    return (dot_nt(grad_tokens, to_place).astype(BF),), (grad_na, grad_na * norm_a)
+
+
 def gelu_and_slope(v):
     c = float(np.sqrt(2 / np.pi))
     square = v * v
@@ -513,7 +601,7 @@
             return shifted(parts, n_z, 1)
 
     def in_order(got):
-        return placed(jnp.stack(got, axis=1).reshape(FRAMES * SPATIAL, model)).astype(F32)
+        return placed(jnp.stack(got, axis=1).reshape(FRAMES * SPATIAL, model))
 
     def from_clip(rows):
         rows = rows.reshape(FRAMES, n_z, part, model)
@@ -525,134 +613,146 @@
             whole_rows = lax.dynamic_update_index_in_dim(whole_rows, got[r], (z + r) % n_z, 0)
         return whole_rows.reshape(tokens.shape)
 
-    def gather(name, shard, direct=True):
-        return Chain("gather_" + name, gather_steps(n_dp, n_z, shard, direct), stages(n_dp) + (2 if direct else n_z))
-
-    def scatter(name, halves, direct=True):
-        return Chain("scatter_" + name, scatter_steps(n_dp, n_z, halves, direct), stages(n_dp) + (2 if direct else n_z))
-
-    def sum_dp(name, halves):
-        return Chain("scatter_" + name, scatter_steps(n_dp, n_z, halves, True), stages(n_dp) + 1)
-
-    def exchange(name, pieces, sign):
-        return Chain(name, exchange_steps(pieces, n_z, sign), 2)
+    few = stages(n_dp) == 2
+
+    def gather(name, shard, at_once=False):
+        at_once = at_once and few
+        return Chain("gather_" + name, gather_steps(n_dp, n_z, shard, at_once), 1 + (1 if at_once else stages(n_dp)))
+
+    def sum_dp(name, halves, at_once=False):
+        return Chain("scatter_" + name, scatter_steps(n_dp, n_z, halves, at_once), 1 + (1 if at_once else stages(n_dp)))
+
+    def exchange(name, pieces, sign, first=(n_z // 2,)):
+        return Chain(name, exchange_steps(pieces, n_z, sign, first), 2)
 
     def butterfly(name, value, axis, size):
         return Chain(name, butterfly_steps(value, axis, size), size.bit_length() - 1)
 
-    both = jnp.concatenate([w_qkv.reshape(feature, -1), w_out], axis=1)
-    per_tile = both.shape[1] // out_tile
-    wa = gather("attention", both)
+    mlp = lax.all_gather(jnp.concatenate([w_up, w_down], axis=0), ("dp", "tensor"), axis=0)
+    wu, wd = (Gathered(mlp.reshape(n_dp, n_z, -1, w_up.shape[1]), i, 2) for i in (0, 1))
+
+    def turned(blocks):
+        return jnp.concatenate([lax.dynamic_slice_in_dim(blocks, (z - r) % n_z, 1) for r in range(n_z)], axis=0)
 
     cond_float = conditioning.astype(F32).reshape(clips, model)
     cond_act = jax.nn.silu(cond_float).astype(BF)
     cond_mine = lax.all_to_all(
         cond_act.reshape(clips, n_dp, feature).transpose(1, 0, 2), "dp", 0, 0, tiled=True
     ).reshape(n_dp * clips, feature)
-    mod_part = lax.all_to_all(dot(cond_mine, w_ada), ("dp", "tensor"), 0, 0, tiled=True)
-    to_place, got_tokens, pos_table, places, count, mod_part = slot(
-        [wa], to_place, for_clips(tokens), pos_table, places, count, mod_part
-    )
-    table = lax.all_to_all(jnp.broadcast_to(pos_table, (n_z,) + pos_table.shape), "tensor", 0, 0, tiled=True)
-    mods = jnp.sum(mod_part.reshape(n_dp, n_z, -1), axis=0).reshape(6, model)
-    mods = jnp.dot(mods, to_place.astype(F32), precision=HIGHEST).reshape(6, 1, model)
-    got_tokens, table, mods, w_up = slot([wa], to_clip(got_tokens), table, mods, w_up)
-    wu = Gathered(lax.all_gather(w_up, ("dp", "tensor"), axis=0).reshape(n_dp, n_z, feature, -1))
+    share = -(-pos_table.size // n_dp)
+    table = jnp.pad(pos_table.reshape(-1), (0, share * n_dp - pos_table.size)).reshape(n_dp, share)
+    table = jnp.broadcast_to(lax.dynamic_slice_in_dim(table, d, 1), (n_dp * n_z, share))
+    mod_part = dot(cond_mine, w_ada)
+    columns = mod_part.shape[1]
+    mod_part = lax.all_to_all(jnp.concatenate([mod_part, table], axis=1), ("dp", "tensor"), 0, 0, tiled=True)
+    blocks = shifted([jnp.concatenate([w_qkv.reshape(feature, -1), w_out], axis=1)] * n_z, n_z, 1)
+    blocks, to_place, got_tokens, places, count, mod_part = slot(
+        [], blocks, to_place, for_clips(tokens), places, count, mod_part
+    )
+    wa, wo = join_parts(blocks, 1, [qkv_tile, out_tile])
+    wa, wo = gather("qkv", wa, True), gather("out", wo, True)
+    table = mod_part[:, columns:].reshape(n_dp, n_z, share).transpose(1, 0, 2).reshape(n_z, -1)[:, : pos_table.size]
+    mods = jnp.sum(mod_part[:, :columns].reshape(n_dp, n_z, -1), axis=0).reshape(6, model)
+    mods = jnp.dot(mods, to_place.astype(F32), precision=HIGHEST)
+    bias = with_layout_constraint(spread_bias(turned(table).reshape(-1, OFFSETS), place), Layout((0, 1, 2, 3)))
+    got_tokens, bias, mods = slot([wa], to_clip(got_tokens), bias, mods)
     resid = in_order(got_tokens)
-    norm_a, inv_a = normalize(resid)
-    normed_a = (norm_a * (1.0 + mods[1]) + mods[0]).astype(BF)
-    normed_a, w_down = lax.optimization_barrier((normed_a, w_down))
-    wd = gather("down", w_down)
-    table = table[::-1]
-    table = lax.dynamic_slice_in_dim(jnp.concatenate([table, table], axis=0), n_z - 1 - z, n_z, axis=0)
-    bias = spread_bias(table.reshape(-1, OFFSETS), place)
-    bias, normed_a, cotangent = slot([wa, wd], bias, normed_a, for_clips(cotangent))
+    normed_a = (normalize(resid.astype(F32))[0] * (1.0 + mods[1:2]) + mods[0:1]).astype(BF)
     normed_a = slot([wa], normed_a)
-
-    w_in = Pieces(whole(wa), both.shape[1], qkv_tile, lambda j: [j])
-    w_mix = Pieces(wa.value, out_tile, out_tile, lambda j: [(2 * j + i) * per_tile + per_tile - 1 for i in (0, 1)])
+    rows_of = (FRAMES * SPATIAL, model)
+
+    w_in = Pieces(whole(wa), qkv_tile)
     qkv, = rows_times(places, normed_a, w_in, qkv_tile * n_z, qkv_tile, lambda v: (v.astype(BF),), (), (BF,), "qkv")
+    qkv = slot([wo], qkv)
     attended, probs = attend(count, qkv, bias, n_z)
-    attended, probs, got_cotangent = slot([], attended, probs, to_clip(cotangent))
-    branch_a = rows_times_t(places, attended, w_mix, 2 * out_tile, "out")
-    middle = resid + mods[2] * branch_a
-    norm_b, inv_b = normalize(middle)
-    normed_b = (norm_b * (1.0 + mods[4]) + mods[3]).astype(BF)
-    normed_b, got_cotangent = slot([wd], normed_b, got_cotangent)
+    attended, probs, got_cotangent = slot([wo], attended, probs, for_clips(cotangent))
+    got_cotangent = to_clip(got_cotangent)
+    wo = Pieces(whole(wo), out_tile * n_z)
+    branch_a, middle, normed_b = rows_times_t(
+        places, attended, wo, out_tile * n_z, after_attention, (resid,), (mods,),
+        ((rows_of, F32), (rows_of, F32), (rows_of, BF)), 0, "out",
+    )
     activ, slope = rows_times(places, normed_b, wu, hidden_tile * n_z, hidden_tile, gelu_and_slope, (), (BF, BF), "up")
+    activ, slope, got_cotangent = slot([], activ, slope, got_cotangent)
     grad_result = in_order(got_cotangent)
-    grad_bb = (grad_result * mods[5]).astype(BF)
+    grad_bb = (grad_result.astype(F32) * mods[5:6]).astype(BF)
     gd = rows_against(grad_bb, activ, hidden_tile, "grad_down")
-    activ, slope, grad_bb, gd = slot([wd], activ, slope, grad_bb, gd)
-    gd = scatter("down", gd)
-    activ, slope, grad_bb = slot([wd, gd], activ, slope, grad_bb)
-
-    wd = Pieces(whole(wd), hidden_tile, hidden_tile, lambda j: [j])
+    activ, slope, grad_bb, gd = slot([], activ, slope, grad_bb, gd)
+    gd = sum_dp("down", gd)
+
     grad_hidden, = rows_times(
         places, grad_bb, wd, hidden_tile * n_z, hidden_tile, lambda v, s: ((v * s.astype(F32)).astype(BF),), (slope,), (BF,),
         "grad_hidden",
     )
-    gu = rows_against(normed_b, grad_hidden, hidden_tile, "grad_up", places, n_dp)
-    grad_hidden, gu, activ = slot([gd], grad_hidden, gu, activ)
-    gu = lax.psum_scatter(gu.reshape(model, -1), "dp", scatter_dimension=0, tiled=True)
-    grad_nb = rows_times_t(places, grad_hidden, wu, hidden_tile, "grad_normed_b")
-    branch_b = rows_times_t(places, activ, wd, hidden_tile, "down")
-    grad_nb, branch_b = slot([gd], grad_nb, branch_b)
-    grad_middle = grad_result + norm_back(norm_b, inv_b, mods[4], grad_nb)
-    grad_ba = (grad_middle * mods[2]).astype(BF)
-    go = rows_against(grad_ba, attended, out_tile * n_z, "grad_out")
+    grad_hidden, activ = slot([gd], grad_hidden, activ)
+    gu = rows_against(normed_b, grad_hidden, hidden_tile, "grad_up")
+    block_out, sums_mlp = rows_times_t(
+        places, activ, wd, hidden_tile, after_mlp, (middle, grad_result), (mods, to_place), ((rows_of, BF),), 1, "down"
+    )
+    grad_hidden, gu, block_out = slot([gd], grad_hidden, gu, from_clip(block_out))
+    gu = sum_dp("up", gu)
+    out_rows = exchange("tokens_out", block_out, -1)
+    grad_middle, grad_ba, sums_mid = rows_times_t(
+        places, grad_hidden, wu, hidden_tile, back_mlp, (middle, branch_a, grad_result), (mods,),
+        ((rows_of, F32), (rows_of, BF)), 3, "grad_normed_b",
+    )
+    grad_middle, grad_ba = slot([gd, gu, out_rows], grad_middle, grad_ba)
+    down_rows = exchange("down_sum", whole(gd), -1)
+    go = rows_against(grad_ba, attended, out_tile * n_z, "grad_out", places, n_dp)
     grad_att, = rows_times(
-        places, grad_ba, w_mix, out_tile * n_z, 2 * out_tile, lambda v: (v.astype(BF),), (), (BF,), "grad_att"
-    )
-    block_out = from_clip(unplaced(middle + mods[5] * branch_b))
-    grad_att, grad_middle, go, block_out = slot([gd], grad_att, grad_middle, go, block_out)
-    go = sum_dp("out", go)
-    out_rows = exchange("tokens_out", block_out, -1)
+        places, grad_ba, wo, out_tile * n_z, out_tile * n_z, lambda v: (v.astype(BF),), (), (BF,), "grad_att"
+    )
     grad_qkv, diag = attend_back(count, qkv, probs, grad_att, n_z)
-    grad_qkv, diag = slot([go, out_rows], grad_qkv, diag)
+    grad_qkv, diag, go = slot([gu, down_rows, out_rows], grad_qkv, diag, go)
+    go = lax.psum_scatter(go.reshape(model, -1), "dp", scatter_dimension=0, tiled=True)
     gq = rows_against(normed_a, grad_qkv, qkv_tile, "grad_qkv")
-    gq, grad_qkv, gu = slot([go, out_rows], gq, grad_qkv, gu)
-    gq = sum_dp("qkv", gq)
-    grad_na = rows_times_t(places, grad_qkv, w_in, qkv_tile, "grad_normed_a")
-    up_rows = shifted([gu[:, r * hidden_tile : (r + 1) * hidden_tile] for r in range(n_z)], n_z, -1)
-    table = fold_bias(diag, place)
-    grad_na, up_rows, table = slot([gq, go], grad_na, up_rows, table)
-    out_up = functools.reduce(lambda a, b: a + b, [p.astype(F32) for p in up_rows])
-    grad_tokens = from_clip(unplaced(grad_middle + norm_back(norm_a, inv_a, mods[1], grad_na)))
-    in_rows = exchange("tokens_out", grad_tokens, -1)
-    heads = table.shape[0] // n_z
-    own = shifted([table[r * heads : (r + 1) * heads] for r in range(n_z)], n_z, -1)
-    grad_mod = unplaced(
-        jnp.stack(
-            [
-                jnp.sum(grad_na, axis=0),
-                jnp.sum(grad_na * norm_a, axis=0),
-                jnp.sum(grad_middle * branch_a, axis=0),
-                jnp.sum(grad_nb, axis=0),
-                jnp.sum(grad_nb * norm_b, axis=0),
-                jnp.sum(grad_result * branch_b, axis=0),
-            ]
-        )
-    ).reshape(1, n_z, -1)
-    grad_mod = jnp.broadcast_to(grad_mod, (n_dp,) + grad_mod.shape[1:]).reshape(n_dp * n_z, -1)
-    grad_mod, own = slot([gq, in_rows], grad_mod, functools.reduce(lambda a, b: a + b, own))
-
-    table = butterfly("table", own, "dp", n_dp)
-    block_out = by_clip(whole(out_rows))
-    mod_cols = lax.all_to_all(grad_mod, ("dp", "tensor"), 0, 0, tiled=True)
-    mod_cols, block_out, out_up = slot([gq, in_rows, table], mod_cols, block_out, out_up)
-    pairs = [jnp.concatenate(p, axis=1) for p in zip(whole(gq), whole(go))]
-    act_part = dot_nt(mod_cols, w_ada).reshape(n_dp, clips, feature)
-    act_part = lax.all_to_all(act_part, "dp", 0, 0, tiled=True)
-    act_part, pairs = slot([table], act_part, shifted(pairs, n_z, -1))
-    pairs = functools.reduce(lambda a, b: a + b, [p.astype(F32) for p in pairs])
+    table = turned(fold_bias(diag, place).reshape(n_z, -1, OFFSETS))
+    table = jnp.pad(table, ((0, 0), (0, 0), (0, -OFFSETS % n_dp)))
+    table = table.reshape(n_z, -1, n_dp, table.shape[2] // n_dp).transpose(2, 0, 1, 3)
+    table = table.reshape((n_dp * n_z,) + table.shape[2:])
+    gq, grad_qkv, table = slot([gu, down_rows], gq, grad_qkv, table)
+    gq = sum_dp("qkv", gq, few)
+    up_rows = exchange("up_sum", whole(gu), -1)
+    grad_tokens, sums_in = rows_times_t(
+        places, grad_qkv, w_in, qkv_tile, back_attention, (resid, grad_middle), (mods, to_place), ((rows_of, BF),), 2,
+        "grad_normed_a",
+    )
+    up_rows.step()
+    in_rows = exchange("tokens_out", from_clip(grad_tokens), -1)
+    in_rows.step()
+    sums_in, block_out = slot([gq, up_rows], sums_in, whole(out_rows))
+    in_rows.step()
+    gq.step()
+    if few:
+        gq.value[1], sums_in = lax.optimization_barrier((gq.value[1], sums_in))
+    grad_mod = unplaced(jnp.concatenate([sums_in, sums_mid, sums_mlp], axis=0)).reshape(1, n_z, -1)
+    grad_mod = jnp.broadcast_to(grad_mod, (n_dp,) + grad_mod.shape[1:]).reshape(n_dp * n_z, -1).astype(F32)
+    small = jnp.concatenate([grad_mod, table.reshape(n_dp * n_z, -1)], axis=1)
+    small = lax.all_to_all(small, ("dp", "tensor"), 0, 0, tiled=True)
+    gq.value, small, grad_tokens, go = slot([], gq.value, small, in_rows.value, go)
+
+    terms = whole(gq) if few else [jnp.concatenate(whole(gq), axis=1)]
+    pairs = attention_parts(terms, go, n_z)
+    pairs, small = lax.optimization_barrier((pairs, small))
+    pairs = functools.reduce(lambda a, b: a + b, [p.astype(F32) for p in shifted(pairs, n_z, -1)])
+    mod_cols = small[:, :columns].astype(BF)
+    act_part = dot_nt(mod_cols, w_ada).reshape(n_dp, 1, -1)
+    act_part = jnp.broadcast_to(act_part, (n_dp, n_z, act_part.shape[2])).reshape(n_dp * n_z, -1)
+    table = jnp.sum(small[:, columns:], axis=0)
+    table = jnp.broadcast_to(table[None], (n_dp * n_z, table.shape[0]))
+    small = lax.all_to_all(jnp.concatenate([act_part, table], axis=1), ("dp", "tensor"), 0, 0, tiled=True)
+    small = small.reshape(n_dp, n_z, -1)
+    grad_act = jnp.sum(small[:, :, : clips * feature], axis=1).reshape(n_dp, clips, feature)
+    grad_act = grad_act.transpose(1, 0, 2).reshape(clips, model)
+    grad_cond = jax.vjp(jax.nn.silu, cond_float)[1](grad_act)[0].reshape(conditioning.shape)
+    table = lax.dynamic_index_in_dim(small[:, :, clips * feature :], z, 1, False)
+    table = table.reshape(n_dp, pos_table.shape[0], -1).transpose(1, 0, 2)
+    grad_table = table.reshape(pos_table.shape[0], -1)[:, :OFFSETS]
     grad_ada = dot_tn(cond_mine, mod_cols)
-    grad_tokens = by_clip(whole(in_rows))
-    act = butterfly("act", act_part, "tensor", n_z)
-    slot([table, act])
-    grad_act = whole(act).transpose(1, 0, 2).reshape(clips, model)
-    grad_cond = jax.vjp(jax.nn.silu, cond_float)[1](grad_act)[0].reshape(conditioning.shape)
-    grad_table = whole(table)
+    block_out, grad_tokens = by_clip(block_out), by_clip(grad_tokens)
+    out_down, out_up = (
+        functools.reduce(lambda a, b: a + b, [p.astype(F32) for p in whole(rows)]) for rows in (down_rows, up_rows)
+    )
     return (
         block_out,
         grad_tokens,
@@ -660,7 +760,7 @@
         pairs[:, :qkv_tile].reshape(w_qkv.shape),
         pairs[:, qkv_tile:],
         out_up,
-        whole(gd),
+        out_down,
         grad_ada,
         grad_table,
     )

time: 511 us -> 472 us (0.924)
  local copies, waits for them, and re-layouts: 49 us -> 77.3 us
  waiting for transfers between devices: 101 us -> 77.2 us
  other arithmetic: 58.1 us -> 40.4 us
  starting transfers between devices: 98.8 us -> 84.3 us
  matrix products: 25.7 us -> 16.8 us
    ppermute x24 -> x12, starting transfers between devices: 49 us -> 28.1 us  [shifted(): lax.ppermute(pieces[r], 'tensor', ring(n_z, sign * r))]
    ppermute x28 -> x24, waiting for transfers between devices: 25.2 us -> 6.5 us  [the longest x6 4.9 us: gather_steps(): lax.ppermute(rows, 'dp', place_perm(n_dp, k))]
    unnamed x154 -> x178, local copies, waits for them, and re-layouts: 12 us -> 28.9 us
    ppermute x6 -> x12, waiting for transfers between devices: 15 us -> 1.03 us  [exchange_steps(): pieces[r] = lax.ppermute(pieces[r], 'tensor', ring(n_z, sign * r))]
    ppermute x24 -> x12, waiting for transfers between devices: 23.9 us -> 35.3 us  [shifted(): lax.ppermute(pieces[r], 'tensor', ring(n_z, sign * r))]
    reshape x6 -> x15, local copies, waits for them, and re-layouts: 1.01 us -> 11 us  [the longest x3 4.95 us: body(): mod_part[:, columns:].reshape(n_dp, n_z, share).transpose(1, 0, 2)]
    pallas_call x4, Pallas kernels: 40.9 us -> 49.3 us  [rows_times_t(): pl.pallas_call(kernel, grid_spec=pltpu.PrefetchScalarGridSpec(num_scalar_...]
    dot_general x4 -> x2, matrix products: 9.61 us -> 1.47 us  [dot_nt(): lax.dot_general(a, b, (((1,), (1,)), ((), ())), preferred_element_type=F32)]
  transfers between devices with their start and end apart: 65 -> 54, of which waited for: 20 -> 8; matrix products, arithmetic and copies ran while one was open for 23% -> 20% of each run, Pallas kernels for 31% -> 31%
where the time goes in v3:
time: 472 us; the launch traced here: 466 us
  Pallas kernels  155 us (33%)
  starting transfers between devices  84.3 us (18%)
  local copies, waits for them, and re-layouts  77.3 us (16%)
  waiting for transfers between devices  77.2 us (16%)
  other arithmetic  40.4 us (9%)
  matrix products  16.8 us (4%)
  between operations  15.6 us (3%)
    pallas_call x4, Pallas kernels, rows_times_t(): pl.pallas_call(kernel, grid_spec=pltpu.PrefetchScalarGridSpec(num_scalar_...  49.3 us
    pallas_call x4, Pallas kernels, rows_times(): pl.pallas_call(kernel, grid_spec=pltpu.PrefetchScalarGridSpec(num_scalar_...  36.3 us
    ppermute x12, waiting for transfers between devices, shifted(): lax.ppermute(pieces[r], 'tensor', ring(n_z, sign * r))  35.3 us
    pallas_call x4, Pallas kernels, rows_against(): pl.pallas_call(kernel, grid_spec=pltpu.PrefetchScalarGridSpec(num_scalar_...  32.5 us
    unnamed x178, local copies, waits for them, and re-layouts  28.9 us
    ppermute x12, starting transfers between devices, shifted(): lax.ppermute(pieces[r], 'tensor', ring(n_z, sign * r))  28.1 us
    all_to_all x1, waiting for transfers between devices, body(): lax.all_to_all(jnp.concatenate([mod_part, table], axis=1), ('dp', 'tensor...  23.5 us
    convert_element_type x7, other arithmetic, add_low(): functools.reduce(lambda a, b: a + b, [o.astype(F32) for o in others], fir...  21.2 us
  transfers between devices with their start and end apart: 54, of which 8 were waited for; matrix products, arithmetic and copies ran while one was open for 20% of the time, Pallas kernels for 31%

profile of v3, /device:TPU:0, one launch (start us, length us, event | category | flops | bytes accessed | tf_op | source)
XLA Modules:
  0.0 466.5 jit_solution(13452694786036741157)
XLA Ops:
  18.2 3.7 all-to-all-start
  33.9 23.5 %all-to-all-done.1 = f32[32,1,2549]{2,1,0:T(1,128)} async-done(((f32[32,1,2549]{2,1,0:T(1,128)}), f32[32,1,2549]{2,1,0:T(1,128)}, u32[]{:S(2)}, u32[]{:S(2)}) %all-to-all-start.1) | async-done | bytes 326304 | tf_op jit(solution)/shard_map/all_to_all | solution.py:647
  78.6 3.4 collective-permute-start.11
  82.0 18.2 %collective-permute-done.10 = bf16[10,16,1024]{2,1,0:T(8,128)(2,1)} collective-permute-done((bf16[10,16,1024]{2,1,0:T(8,128)(2,1)}, bf16[10,16,1024]{2,1,0:T(8,128)(2,1)}, u32[]{:S(2)}, u32[]{:S(2)}) %collective-permute-start.10) | collective-permute-done | bytes 327712 | tf_op jit(solution)/shard_map/tokens_in/ppermute | solution.py:181
  100.1 6.6 %collective-permute-start.9 = (bf16[10,16,1024]{2,1,0:T(8,128)(2,1)}, bf16[10,16,1024]{2,1,0:T(8,128)(2,1)}, u32[]{:S(2)}, u32[]{:S(2)}) collective-permute-start(bf16[10,16,1024]{2,1,0:T(8,128)(2,1)} %get-tuple-element.186), channel_id=1, source_target_pairs={{0,1},{1,2},{2,3},{3,0},{4,5},{5,6},{6,7},{7,4},{8,9},{9,10},{10,1... | collective-permute-start | bytes 983048 | tf_op jit(solution)/shard_map/tokens_in/ppermute | solution.py:181
  106.7 4.9 %fusion.10 = f32[16,9,64,64]{3,1,2,0:T(8,128)S(1)} fusion(pred[64,64,225,1]{2,1,0,3:T(32,128)(4,1)} %bitcast.127, f32[16,9,225]{2,1,0:T(8,128)} %dot_general.30), kind=kOutput, calls=%fused_computation.74 | convolution fusion | flops 1592524800 | bytes 3410496 | tf_op jit(solution)/shard_map/dot_general | solution.py:208
  112.3 3.6 copy.72.bias_ref
  133.2 8.7 %qkv.1.qkv_ref = bf16[640,3072]{1,0:T(8,128)(2,1)} custom-call(s32[12]{0:T(128)S(1)} %pad_add_fusion.places_ref, bf16[640,1024]{1,0:T(8,128)(2,1)} %fusion.7.x_ref, bf16[128,3072]{1,0:T(8,128)(2,1)S(1)} %get-tuple-element.201.refs_0_, bf16[128,3072]{1,0:T(8,128)(2,1)} %collective-permute-done.6.refs_1_, bf16[128,3072]{1,0:T(8,128)(2,1)} %collective-permute-done.7.refs_2_, ...), custom_call_target="tpu_custom_call" | custom-call | flops 1000000 | bytes 10000 | tf_op jit(solution)/shard_map/qkv/pallas_call | solution.py:275
  142.0 4.9 %collective-permute-done.5.refs_3_ = bf16[128,1024]{1,0:T(8,128)(2,1)S(1)} collective-permute-done((bf16[128,1024]{1,0:T(8,128)(2,1)S(1)}, bf16[128,1024]{1,0:T(8,128)(2,1)S(1)}, u32[]{:S(2)}, u32[]{:S(2)}) %collective-permute-start.5) | collective-permute-done | bytes 262176 | tf_op jit(solution)/shard_map/gather_out_2_left/ppermute | solution.py:99
  146.9 4.9 %collective-permute-start.16 = (bf16[128,1024]{1,0:T(8,128)(2,1)S(1)}, bf16[128,1024]{1,0:T(8,128)(2,1)S(1)}, u32[]{:S(2)}, u32[]{:S(2)}) collective-permute-start(bf16[128,1024]{1,0:T(8,128)(2,1)S(1)} %get-tuple-element.219.refs_0_), channel_id=1, source_target_pairs={{0,4},{4,0},{8,12},{12,8},{16,20},{20,16},{24,28},{28,24},{1,5},{5... | collective-permute-start | bytes 786440 | tf_op jit(solution)/shard_map/gather_out_1_left/ppermute | solution.py:105
  155.5 16.6 %attend.1 = (bf16[640,1024]{1,0:T(8,128)(2,1)S(1)}, bf16[2,16,320,320]{3,2,1,0:T(8,128)(2,1)}) custom-call(s32[1]{0:T(128)} %dynamic_slice.67.count_ref, bf16[640,3072]{1,0:T(8,128)(2,1)S(1)} %copy-done.3, f32[16,9,64,64]{3,2,1,0:T(8,128)} %copy.72.bias_ref), custom_call_target="tpu_custom_call" | custom-call | flops 1000000 | bytes 10000 | tf_op jit(solution)/shard_map/attend/pallas_call | solution.py:471
  173.1 3.4 collective-permute-start.21
  177.9 4.6 out.1
  188.8 14.6 %up.1 = (bf16[640,4096]{1,0:T(8,128)(2,1)}, bf16[640,4096]{1,0:T(8,128)(2,1)}) custom-call(s32[12]{0:T(128)S(1)} %pad_add_fusion.places_ref, bf16[640,1024]{1,0:T(8,128)(2,1)S(1)} %copy-done.10, bf16[8,4,256,1024]{3,2,1,0:T(8,128)(2,1)} %bitcast.123), custom_call_target="tpu_custom_call" | custom-call | flops 1000000 | bytes 10000 | tf_op jit(solution)/shard_map/up/pallas_call | solution.py:275
  206.3 10.3 %grad_down.1 = (bf16[512,4096]{1,0:T(8,128)(2,1)S(1)}, bf16[512,4096]{1,0:T(8,128)(2,1)}) custom-call(s32[1]{0:T(128)} %constant.239.clone.1.places_ref, bf16[640,1024]{1,0:T(8,128)(2,1)S(1)} %get-tuple-element.244.x_ref, bf16[640,4096]{1,0:T(8,128)(2,1)} %get-tuple-element.252.y_ref.x_ref), custom_call_target="tpu_custom_call" | custom-call | flops 1000000 | bytes 10000 | tf_op jit(solution)/shard_map/grad_down/pallas_call | solution.py:375
  216.6 10.9 %grad_hidden.1.y_ref.x_ref = bf16[640,4096]{1,0:T(8,128)(2,1)} custom-call(s32[12]{0:T(128)S(1)} %pad_add_fusion.places_ref, bf16[640,1024]{1,0:T(8,128)(2,1)S(1)} %get-tuple-element.244.x_ref, bf16[8,4,256,1024]{3,2,1,0:T(8,128)(2,1)} %bitcast.124, bf16[640,4096]{1,0:T(8,128)(2,1)} %get-tuple-element.245.refs_1_), custom_call_target="tpu_custom_call" | custom-call | flops 1000000 | bytes 10000 | tf_op jit(solution)/shard_map/grad_hidden/pallas_call | solution.py:275
  231.7 10.2 %grad_up.1 = (bf16[512,4096]{1,0:T(8,128)(2,1)S(1)}, bf16[512,4096]{1,0:T(8,128)(2,1)}) custom-call(s32[1]{0:T(128)} %constant.239.clone.1.places_ref, bf16[640,1024]{1,0:T(8,128)(2,1)S(1)} %copy-done.11, bf16[640,4096]{1,0:T(8,128)(2,1)} %grad_hidden.1.y_ref.x_ref), custom_call_target="tpu_custom_call" | custom-call | flops 1000000 | bytes 10000 | tf_op jit(solution)/shard_map/grad_up/pallas_call | solution.py:375
  242.0 14.6 %down.1 = (bf16[640,1024]{1,0:T(8,128)(2,1)S(1)}, f32[1,1024]{1,0:T(1,128)S(1)}) custom-call(s32[12]{0:T(128)S(1)} %pad_add_fusion.places_ref, bf16[640,4096]{1,0:T(8,128)(2,1)} %get-tuple-element.252.y_ref.x_ref, bf16[8,4,256,1024]{3,2,1,0:T(8,128)(2,1)} %bitcast.125, f32[640,1024]{1,0:T(8,128)} %get-tuple-element.253.refs_1_, ...), custom_call_target="tpu_custom_call" | custom-call | flops 1000000 | bytes 10000 | tf_op jit(solution)/shard_map/down/pallas_call | solution.py:329
  264.2 13.9 %grad_normed_b.1 = (f32[640,1024]{1,0:T(8,128)S(1)}, bf16[640,1024]{1,0:T(8,128)(2,1)S(1)}, f32[3,1024]{1,0:T(4,128)S(1)}) custom-call(s32[12]{0:T(128)S(1)} %pad_add_fusion.places_ref, bf16[640,4096]{1,0:T(8,128)(2,1)} %grad_hidden.1.y_ref.x_ref, bf16[8,4,256,1024]{3,2,1,0:T(8,128)(2,1)} %bitcast.126, f32[640,1024]{1,0:T(8,128)} %get-tuple-element.253.refs_1_, ...), custom_call_target="tpu_custom_call" | custom-call | flops 1000000 | bytes 10000 | tf_op jit(solution)/shard_map/grad_normed_b/pallas_call | solution.py:329
  280.7 4.6 add_convert_fusion
  291.1 3.7 grad_out.1
  297.0 19.1 %attend_back.1 = (bf16[640,3072]{1,0:T(8,128)(2,1)S(1)}, f32[16,9,64,64]{3,2,1,0:T(8,128)}) custom-call(s32[1]{0:T(128)} %dynamic_slice.67.count_ref, bf16[640,3072]{1,0:T(8,128)(2,1)} %qkv.1.qkv_ref, bf16[2,16,320,320]{3,2,1,0:T(8,128)(2,1)} %get-tuple-element.277.prob_ref, bf16[640,1024]{1,0:T(8,128)(2,1)S(1)} %grad_att.1.gatt_ref), custom_call_target="tpu_custom_call" | custom-call | flops 1000000 | bytes 10000 | tf_op jit(solution)/shard_map/attend_back/pallas_call | solution.py:499
  321.1 5.3 %reshape.378 = f32[144,4096]{1,0:T(8,128)} reshape(f32[16,9,64,64]{3,2,1,0:T(8,128)} %get-tuple-element.290) | data formatting | bytes 4718592 | tf_op jit(solution)/shard_map/reshape | solution.py:214
  326.4 4.2 fusion.1
  334.6 8.3 %grad_qkv.1 = (bf16[512,3072]{1,0:T(8,128)(2,1)S(1)}, bf16[512,3072]{1,0:T(8,128)(2,1)}) custom-call(s32[1]{0:T(128)} %constant.239.clone.1.places_ref, bf16[640,1024]{1,0:T(8,128)(2,1)S(1)} %copy-done.6, bf16[640,3072]{1,0:T(8,128)(2,1)} %copy-done.5), custom_call_target="tpu_custom_call" | custom-call | flops 1000000 | bytes 10000 | tf_op jit(solution)/shard_map/grad_qkv/pallas_call | solution.py:375
  348.1 4.1 collective-permute-start.36
  354.0 16.2 %grad_normed_a.1 = (bf16[640,1024]{1,0:T(8,128)(2,1)}, f32[2,1024]{1,0:T(2,128)S(1)}) custom-call(s32[12]{0:T(128)S(1)} %pad_add_fusion.places_ref, bf16[640,3072]{1,0:T(8,128)(2,1)} %copy-done.5, bf16[128,3072]{1,0:T(8,128)(2,1)S(1)} %get-tuple-element.201.refs_0_, bf16[128,3072]{1,0:T(8,128)(2,1)} %collective-permute-done.6.refs_1_, ...), custom_call_target="tpu_custom_call" | custom-call | flops 1000000 | bytes 10000 | tf_op jit(solution)/shard_map/grad_normed_a/pallas_call | solution.py:329
  370.2 4.1 add_convert_fusion.8
  400.9 4.3 all-to-all-start.2
  410.8 8.9 %all-to-all-done.2 = f32[32,1,2552]{2,1,0:T(1,128)} async-done(((f32[32,1,2552]{2,1,0:T(1,128)}), f32[32,1,2552]{2,1,0:T(1,128)}, u32[]{:S(2)}, u32[]{:S(2)}) %all-to-all-start.2) | async-done | bytes 326688 | tf_op jit(solution)/shard_map/all_to_all | solution.py:731
  431.0 3.7 all-to-all-start.3
  438.0 17.1 %collective-permute-done.46 = bf16[128,1024]{1,0:T(8,128)(2,1)S(1)} collective-permute-done((bf16[128,1024]{1,0:T(8,128)(2,1)}, bf16[128,1024]{1,0:T(8,128)(2,1)S(1)}, u32[]{:S(2)}, u32[]{:S(2)}) %collective-permute-start.46) | collective-permute-done | bytes 262176 | tf_op jit(solution)/shard_map/ppermute | solution.py:181
  (383 shorter events, 165.6 us)
Async XLA Ops:
  7.2 180.3 %all-gather.3.cloned.1.call-start = ((), (), s32[]{:S(2)}) async-start(), calls=%async_computation.6 | async-start | bytes 17301504 | tf_op jit(solution)/shard_map/all_gather | solution.py:631
  10.5 47.9 %collective-permute-start = (bf16[128,1024]{1,0:T(8,128)(2,1)S(1)}, bf16[128,1024]{1,0:T(8,128)(2,1)S(1)}, u32[]{:S(2)}, u32[]{:S(2)}) collective-permute-start(bf16[128,1024]{1,0:T(8,128)(2,1)S(1)} %pad_maximum_fusion.4.refs_0_), channel_id=1, source_target_pairs={{0,1},{1,2},{2,3},{3,0},{4,5},{5,6},{6,7},{7,4},{8,9},{9,10},{10,1... | collective-permute-start | bytes 786440 | tf_op jit(solution)/shard_map/ppermute | solution.py:181
  13.6 45.6 %collective-permute-start.1 = (bf16[128,1024]{1,0:T(8,128)(2,1)S(1)}, bf16[128,1024]{1,0:T(8,128)(2,1)S(1)}, u32[]{:S(2)}, u32[]{:S(2)}) collective-permute-start(bf16[128,1024]{1,0:T(8,128)(2,1)S(1)} %pad_maximum_fusion.4.refs_0_), channel_id=1, source_target_pairs={{0,2},{1,3},{2,0},{3,1},{4,6},{5,7},{6,4},{7,5},{8,10},{9,11},{10,... | collective-permute-start | bytes 786440 | tf_op jit(solution)/shard_map/ppermute | solution.py:181
  16.2 43.7 %collective-permute-start.2 = (bf16[128,1024]{1,0:T(8,128)(2,1)S(1)}, bf16[128,1024]{1,0:T(8,128)(2,1)S(1)}, u32[]{:S(2)}, u32[]{:S(2)}) collective-permute-start(bf16[128,1024]{1,0:T(8,128)(2,1)S(1)} %pad_maximum_fusion.4.refs_0_), channel_id=1, source_target_pairs={{0,3},{1,0},{2,1},{3,2},{4,7},{5,4},{6,5},{7,6},{8,11},{9,8},{10,9... | collective-permute-start | bytes 786440 | tf_op jit(solution)/shard_map/ppermute | solution.py:181
  28.5 28.9 %all-to-all-start.1 = ((f32[32,1,2549]{2,1,0:T(1,128)}), f32[32,1,2549]{2,1,0:T(1,128)}, u32[]{:S(2)}, u32[]{:S(2)}) async-start(f32[32,1,2549]{2,1,0:T(1,128)} %copy.69), calls=%async_computation.1 | async-start | bytes 655360 | tf_op jit(solution)/shard_map/all_to_all | solution.py:647
  31.8 389.7 %reduce-scatter.2.cloned.1.call-start = ((), (), s32[]{:S(2)}) async-start(), calls=%async_computation.5 | async-start | bytes 2359296 | tf_op jit(solution)/shard_map/reduce_scatter | solution.py:707
  64.5 58.5 %collective-permute-start.6 = (bf16[128,3072]{1,0:T(8,128)(2,1)S(1)}, bf16[128,3072]{1,0:T(8,128)(2,1)}, u32[]{:S(2)}, u32[]{:S(2)}) collective-permute-start(bf16[128,3072]{1,0:T(8,128)(2,1)S(1)} %get-tuple-element.201.refs_0_), channel_id=1, source_target_pairs={{0,8},{4,20},{8,0},{12,28},{16,24},{20,4},{24,16},{28,12},{1,9},{5... | collective-permute-start | bytes 2359304 | tf_op jit(solution)/shard_map/gather_qkv_2_left/ppermute | solution.py:99
  66.0 57.0 %collective-permute-start.7 = (bf16[128,3072]{1,0:T(8,128)(2,1)S(1)}, bf16[128,3072]{1,0:T(8,128)(2,1)}, u32[]{:S(2)}, u32[]{:S(2)}) collective-permute-start(bf16[128,3072]{1,0:T(8,128)(2,1)S(1)} %get-tuple-element.201.refs_0_), channel_id=1, source_target_pairs={{0,16},{4,12},{8,24},{12,4},{16,0},{20,28},{24,8},{28,20},{1,17},{... | collective-permute-start | bytes 2359304 | tf_op jit(solution)/shard_map/gather_qkv_2_left/ppermute | solution.py:99
  67.0 56.0 %collective-permute-start.8 = (bf16[128,3072]{1,0:T(8,128)(2,1)S(1)}, bf16[128,3072]{1,0:T(8,128)(2,1)}, u32[]{:S(2)}, u32[]{:S(2)}) collective-permute-start(bf16[128,3072]{1,0:T(8,128)(2,1)S(1)} %get-tuple-element.201.refs_0_), channel_id=1, source_target_pairs={{0,24},{4,28},{8,16},{12,20},{16,8},{20,12},{24,0},{28,4},{1,25},{... | collective-permute-start | bytes 2359304 | tf_op jit(solution)/shard_map/gather_qkv_2_left/ppermute | solution.py:99
  73.7 26.5 %collective-permute-start.10 = (bf16[10,16,1024]{2,1,0:T(8,128)(2,1)}, bf16[10,16,1024]{2,1,0:T(8,128)(2,1)}, u32[]{:S(2)}, u32[]{:S(2)}) collective-permute-start(bf16[10,16,1024]{2,1,0:T(8,128)(2,1)} %get-tuple-element.187), channel_id=1, source_target_pairs={{0,2},{1,3},{2,0},{3,1},{4,6},{5,7},{6,4},{7,5},{8,10},{9,11},{10,... | collective-permute-start | bytes 983048 | tf_op jit(solution)/shard_map/tokens_in/ppermute | solution.py:181
  78.6 43.7 %collective-permute-start.11 = (bf16[10,16,1024]{2,1,0:T(8,128)(2,1)}, bf16[10,16,1024]{2,1,0:T(8,128)(2,1)}, u32[]{:S(2)}, u32[]{:S(2)}) collective-permute-start(bf16[10,16,1024]{2,1,0:T(8,128)(2,1)} %get-tuple-element.188), channel_id=1, source_target_pairs={{0,3},{1,0},{2,1},{3,2},{4,7},{5,4},{6,5},{7,6},{8,11},{9,8},{10,9... | collective-permute-start | bytes 983048 | tf_op jit(solution)/shard_map/tokens_in/ppermute | solution.py:181
  146.9 25.3 %collective-permute-start.16 = (bf16[128,1024]{1,0:T(8,128)(2,1)S(1)}, bf16[128,1024]{1,0:T(8,128)(2,1)S(1)}, u32[]{:S(2)}, u32[]{:S(2)}) collective-permute-start(bf16[128,1024]{1,0:T(8,128)(2,1)S(1)} %get-tuple-element.219.refs_0_), channel_id=1, source_target_pairs={{0,4},{4,0},{8,12},{12,8},{16,20},{20,16},{24,28},{28,24},{1,5},{5... | collective-permute-start | bytes 786440 | tf_op jit(solution)/shard_map/gather_out_1_left/ppermute | solution.py:105
  172.2 31.2 %collective-permute-start.20 = (bf16[10,16,1024]{2,1,0:T(8,128)(2,1)}, bf16[10,16,1024]{2,1,0:T(8,128)(2,1)}, u32[]{:S(2)}, u32[]{:S(2)}) collective-permute-start(bf16[10,16,1024]{2,1,0:T(8,128)(2,1)} %get-tuple-element.231), channel_id=1, source_target_pairs={{0,1},{1,2},{2,3},{3,0},{4,5},{5,6},{6,7},{7,4},{8,9},{9,10},{10,1... | collective-permute-start | bytes 983048 | tf_op jit(solution)/shard_map/tokens_in/ppermute | solution.py:181
  173.1 30.3 %collective-permute-start.21 = (bf16[10,16,1024]{2,1,0:T(8,128)(2,1)}, bf16[10,16,1024]{2,1,0:T(8,128)(2,1)}, u32[]{:S(2)}, u32[]{:S(2)}) collective-permute-start(bf16[10,16,1024]{2,1,0:T(8,128)(2,1)} %get-tuple-element.232), channel_id=1, source_target_pairs={{0,2},{1,3},{2,0},{3,1},{4,6},{5,7},{6,4},{7,5},{8,10},{9,11},{10,... | collective-permute-start | bytes 983048 | tf_op jit(solution)/shard_map/tokens_in/ppermute | solution.py:181
  176.4 27.0 %collective-permute-start.22 = (bf16[10,16,1024]{2,1,0:T(8,128)(2,1)}, bf16[10,16,1024]{2,1,0:T(8,128)(2,1)}, u32[]{:S(2)}, u32[]{:S(2)}) collective-permute-start(bf16[10,16,1024]{2,1,0:T(8,128)(2,1)} %get-tuple-element.233), channel_id=1, source_target_pairs={{0,3},{1,0},{2,1},{3,2},{4,7},{5,4},{6,5},{7,6},{8,11},{9,8},{10,9... | collective-permute-start | bytes 983048 | tf_op jit(solution)/shard_map/tokens_in/ppermute | solution.py:181
  230.4 27.0 %collective-permute-start.24 = (bf16[256,4096]{1,0:T(8,128)(2,1)}, bf16[256,4096]{1,0:T(8,128)(2,1)}, u32[]{:S(2)}, u32[]{:S(2)}) collective-permute-start(bf16[256,4096]{1,0:T(8,128)(2,1)} %get-tuple-element.248), channel_id=1, source_target_pairs={{0,16},{4,12},{8,24},{12,4},{16,0},{20,28},{24,8},{28,20},{1,17},{... | collective-permute-start | bytes 6291464 | tf_op jit(solution)/shard_map/scatter_down_2_left/ppermute | solution.py:124
  285.5 30.6 %collective-permute-start.28 = (bf16[256,4096]{1,0:T(8,128)(2,1)}, bf16[256,4096]{1,0:T(8,128)(2,1)S(1)}, u32[]{:S(2)}, u32[]{:S(2)}) collective-permute-start(bf16[256,4096]{1,0:T(8,128)(2,1)} %get-tuple-element.268), channel_id=1, source_target_pairs={{0,16},{4,12},{8,24},{12,4},{16,0},{20,28},{24,8},{28,20},{1,17},{... | collective-permute-start | bytes 6291464 | tf_op jit(solution)/shard_map/scatter_up_2_left/ppermute | solution.py:124
  286.3 32.3 %collective-permute-start.30 = (bf16[10,16,1024]{2,1,0:T(8,128)(2,1)S(1)}, bf16[10,16,1024]{2,1,0:T(8,128)(2,1)S(1)}, u32[]{:S(2)}, u32[]{:S(2)}) collective-permute-start(bf16[10,16,1024]{2,1,0:T(8,128)(2,1)S(1)} %get-tuple-element.274), channel_id=1, source_target_pairs={{0,3},{1,0},{2,1},{3,2},{4,7},{5,4},{6,5},{7,6},{8,11},{9,8},{10,9... | collective-permute-start | bytes 983048 | tf_op jit(solution)/shard_map/tokens_out_1_left/ppermute | solution.py:188
  289.7 29.0 %collective-permute-start.31 = (bf16[10,16,1024]{2,1,0:T(8,128)(2,1)S(1)}, bf16[10,16,1024]{2,1,0:T(8,128)(2,1)S(1)}, u32[]{:S(2)}, u32[]{:S(2)}) collective-permute-start(bf16[10,16,1024]{2,1,0:T(8,128)(2,1)S(1)} %get-tuple-element.276), channel_id=1, source_target_pairs={{0,1},{1,2},{2,3},{3,0},{4,5},{5,6},{6,7},{7,4},{8,9},{9,10},{10,1... | collective-permute-start | bytes 983048 | tf_op jit(solution)/shard_map/tokens_out_1_left/ppermute | solution.py:188
  289.9 28.7 %collective-permute-start.29 = (bf16[128,1024]{1,0:T(8,128)(2,1)S(1)}, bf16[128,1024]{1,0:T(8,128)(2,1)S(1)}, u32[]{:S(2)}, u32[]{:S(2)}) collective-permute-start(bf16[128,1024]{1,0:T(8,128)(2,1)S(1)} %get-tuple-element.271), channel_id=1, source_target_pairs={{0,2},{1,3},{2,0},{3,1},{4,6},{5,7},{6,4},{7,5},{8,10},{9,11},{10,... | collective-permute-start | bytes 786440 | tf_op jit(solution)/shard_map/down_sum_2_left/ppermute | solution.py:188
  319.6 25.1 %collective-permute-start.32 = (bf16[128,4096]{1,0:T(8,128)(2,1)}, bf16[128,4096]{1,0:T(8,128)(2,1)}, u32[]{:S(2)}, u32[]{:S(2)}) collective-permute-start(bf16[128,4096]{1,0:T(8,128)(2,1)} %get-tuple-element.282), channel_id=1, source_target_pairs={{0,8},{4,20},{8,0},{12,28},{16,24},{20,4},{24,16},{28,12},{1,9},{5... | collective-permute-start | bytes 3145736 | tf_op jit(solution)/shard_map/scatter_up_1_left/ppermute | solution.py:124
  348.1 26.3 %collective-permute-start.36 = (bf16[128,1024]{1,0:T(8,128)(2,1)}, bf16[128,1024]{1,0:T(8,128)(2,1)S(1)}, u32[]{:S(2)}, u32[]{:S(2)}) collective-permute-start(bf16[128,1024]{1,0:T(8,128)(2,1)} %get-tuple-element.294), channel_id=1, source_target_pairs={{0,3},{1,0},{2,1},{3,2},{4,7},{5,4},{6,5},{7,6},{8,11},{9,8},{10,9... | collective-permute-start | bytes 786440 | tf_op jit(solution)/shard_map/up_sum_1_left/ppermute | solution.py:188
  352.2 23.2 %collective-permute-start.37 = (bf16[128,1024]{1,0:T(8,128)(2,1)}, bf16[128,1024]{1,0:T(8,128)(2,1)S(1)}, u32[]{:S(2)}, u32[]{:S(2)}) collective-permute-start(bf16[128,1024]{1,0:T(8,128)(2,1)} %get-tuple-element.295), channel_id=1, source_target_pairs={{0,2},{1,3},{2,0},{3,1},{4,6},{5,7},{6,4},{7,5},{8,10},{9,11},{10,... | collective-permute-start | bytes 786440 | tf_op jit(solution)/shard_map/up_sum_2_left/ppermute | solution.py:188
  352.2 23.2 %collective-permute-start.38 = (bf16[128,1024]{1,0:T(8,128)(2,1)}, bf16[128,1024]{1,0:T(8,128)(2,1)S(1)}, u32[]{:S(2)}, u32[]{:S(2)}) collective-permute-start(bf16[128,1024]{1,0:T(8,128)(2,1)} %get-tuple-element.296), channel_id=1, source_target_pairs={{0,1},{1,2},{2,3},{3,0},{4,5},{5,6},{6,7},{7,4},{8,9},{9,10},{10,1... | collective-permute-start | bytes 786440 | tf_op jit(solution)/shard_map/up_sum_1_left/ppermute | solution.py:188
  379.2 42.2 %collective-permute-start.42 = (bf16[10,16,1024]{2,1,0:T(8,128)(2,1)}, bf16[10,16,1024]{2,1,0:T(8,128)(2,1)}, u32[]{:S(2)}, u32[]{:S(2)}) collective-permute-start(bf16[10,16,1024]{2,1,0:T(8,128)(2,1)} %get-tuple-element.425), channel_id=1, source_target_pairs={{0,3},{1,0},{2,1},{3,2},{4,7},{5,4},{6,5},{7,6},{8,11},{9,8},{10,9... | collective-permute-start | bytes 983048 | tf_op jit(solution)/shard_map/tokens_out_1_left/ppermute | solution.py:188
  381.2 40.2 %collective-permute-start.43 = (bf16[10,16,1024]{2,1,0:T(8,128)(2,1)}, bf16[10,16,1024]{2,1,0:T(8,128)(2,1)}, u32[]{:S(2)}, u32[]{:S(2)}) collective-permute-start(bf16[10,16,1024]{2,1,0:T(8,128)(2,1)} %get-tuple-element.424), channel_id=1, source_target_pairs={{0,2},{1,3},{2,0},{3,1},{4,6},{5,7},{6,4},{7,5},{8,10},{9,11},{10,... | collective-permute-start | bytes 983048 | tf_op jit(solution)/shard_map/tokens_out_2_left/ppermute | solution.py:188
  382.4 39.0 %collective-permute-start.44 = (bf16[10,16,1024]{2,1,0:T(8,128)(2,1)}, bf16[10,16,1024]{2,1,0:T(8,128)(2,1)}, u32[]{:S(2)}, u32[]{:S(2)}) collective-permute-start(bf16[10,16,1024]{2,1,0:T(8,128)(2,1)} %get-tuple-element.423), channel_id=1, source_target_pairs={{0,1},{1,2},{2,3},{3,0},{4,5},{5,6},{6,7},{7,4},{8,9},{9,10},{10,1... | collective-permute-start | bytes 983048 | tf_op jit(solution)/shard_map/tokens_out_1_left/ppermute | solution.py:188
  385.7 35.8 %collective-permute-start.40 = (bf16[128,3072]{1,0:T(8,128)(2,1)}, bf16[128,3072]{1,0:T(8,128)(2,1)S(1)}, u32[]{:S(2)}, u32[]{:S(2)}) collective-permute-start(bf16[128,3072]{1,0:T(8,128)(2,1)} %get-tuple-element.312), channel_id=1, source_target_pairs={{0,16},{4,12},{8,24},{12,4},{16,0},{20,28},{24,8},{28,20},{1,17},{... | collective-permute-start | bytes 2359304 | tf_op jit(solution)/shard_map/scatter_qkv_1_left/ppermute | solution.py:119
  391.0 30.5 %collective-permute-start.41 = (bf16[128,3072]{1,0:T(8,128)(2,1)}, bf16[128,3072]{1,0:T(8,128)(2,1)S(1)}, u32[]{:S(2)}, u32[]{:S(2)}) collective-permute-start(bf16[128,3072]{1,0:T(8,128)(2,1)} %get-tuple-element.313), channel_id=1, source_target_pairs={{0,24},{4,28},{8,16},{12,20},{16,8},{20,12},{24,0},{28,4},{1,25},{... | collective-permute-start | bytes 2359304 | tf_op jit(solution)/shard_map/scatter_qkv_1_left/ppermute | solution.py:119
  427.9 27.2 %collective-permute-start.46 = (bf16[128,1024]{1,0:T(8,128)(2,1)}, bf16[128,1024]{1,0:T(8,128)(2,1)S(1)}, u32[]{:S(2)}, u32[]{:S(2)}) collective-permute-start(bf16[128,1024]{1,0:T(8,128)(2,1)} %get-tuple-element.337), channel_id=1, source_target_pairs={{0,2},{1,3},{2,0},{3,1},{4,6},{5,7},{6,4},{7,5},{8,10},{9,11},{10,... | collective-permute-start | bytes 786440 | tf_op jit(solution)/shard_map/ppermute | solution.py:181
  428.7 26.3 %collective-permute-start.47 = (bf16[128,1024]{1,0:T(8,128)(2,1)}, bf16[128,1024]{1,0:T(8,128)(2,1)S(1)}, u32[]{:S(2)}, u32[]{:S(2)}) collective-permute-start(bf16[128,1024]{1,0:T(8,128)(2,1)} %get-tuple-element.338), channel_id=1, source_target_pairs={{0,1},{1,2},{2,3},{3,0},{4,5},{5,6},{6,7},{7,4},{8,9},{9,10},{10,1... | collective-permute-start | bytes 786440 | tf_op jit(solution)/shard_map/ppermute | solution.py:181
  431.0 26.0 %all-to-all-start.3 = ((f32[32,1,1528]{2,1,0:T(1,128)}), f32[32,1,1528]{2,1,0:T(1,128)S(1)}, u32[]{:S(2)}, u32[]{:S(2)}) async-start(f32[32,1,1528]{2,1,0:T(1,128)} %all_to_all.32), calls=%async_computation.4 | async-start | bytes 393216 | tf_op jit(solution)/shard_map/all_to_all | solution.py:743
  (109 other events, 1350.8 us)
Sparse Core Ops, SparseCore 0:
  11.6 164.6 all-gather.2
  348.2 44.5 reduce-scatter.1

commit v4 on v3

--- a/solution.py
+++ b/solution.py
@@ -26,7 +26,6 @@
 SPREAD = 2 * WIN_T - 1
 DIAG = SPREAD * SPATIAL
 GROUPS = 4
-VMEM = 48 << 20
 
 
 def stage_bits(n_dp, core):
@@ -115,12 +114,15 @@
     if at_once:
         count = n_dp // 2
         rows = keep.shape[0] // count
-        mine = yield [add_low(keep[k * rows : (k + 1) * rows], got[k * rows : (k + 1) * rows]) for k in range(count)]
-        terms = mine[:1] + [lax.ppermute(mine[k], "dp", place_perm(n_dp, k)) for k in range(1, count)]
+        mine = [add_low(keep[k * rows : (k + 1) * rows], got[k * rows : (k + 1) * rows]) for k in range(count)]
+        sent = yield mine[1:]
+        far = lax.ppermute(sent[-1], "dp", place_perm(n_dp, count - 1))
+        terms = mine[:1] + [lax.ppermute(v, "dp", place_perm(n_dp, k + 1)) for k, v in enumerate(sent[:-1])] + [far]
     else:
         for t in range(stages(n_dp) - 1, -1, -1):
             rows = keep.shape[0] // 2
-            keep, send = yield add_low(keep[:rows], got[:rows]), add_low(keep[rows:], got[rows:])
+            send, = yield [add_low(keep[rows:], got[rows:])]
+            keep = add_low(keep[:rows], got[:rows])
             got = lax.ppermute(send, "dp", stage_perm(n_dp, t))
         terms = [keep, got]
     if at_once:
@@ -228,16 +230,16 @@
     return lax.dot_general(a, b, (((0,), (0,)), ((), ())), preferred_element_type=F32)
 
 
-def params():
-    return pltpu.CompilerParams(vmem_limit_bytes=VMEM)
+def params(mib=28):
+    return pltpu.CompilerParams(vmem_limit_bytes=mib << 20)
 
 
 COST = pl.CostEstimate(flops=10**6, bytes_accessed=10**4, transcendentals=0)
 
 
 class Pieces:
-    def __init__(self, arrays, width):
-        self.arrays, self.width = arrays, width
+    def __init__(self, arrays, width, n_dp):
+        self.arrays, self.width, self.n_dp = arrays, width, n_dp
         self.rows = sum(a.shape[0] for a in arrays)
 
     def specs(self):
@@ -248,28 +250,51 @@
 
 
 class Gathered:
-    def __init__(self, array, which, of):
-        self.arrays, self.which, self.count = [array], which, array.shape[0]
-        self.each = array.shape[2] // of
-        self.rows = self.count * self.each
+    def __init__(self, array, rows):
+        self.arrays, self.each, self.n_dp = [array], rows, array.shape[0]
+        self.rows = self.n_dp * rows
 
     def specs(self):
         n_dp, _, _, columns = self.arrays[0].shape
-        return [pl.BlockSpec((n_dp, 1, self.each, columns), lambda j, p: (0, p[n_dp + j], self.which, 0))]
+        return [pl.BlockSpec((n_dp, 1, self.each, columns), lambda j, p: (0, p[n_dp + j], 0, 0))]
 
     def load(self, refs, places):
-        return jnp.concatenate([refs[0][places[k], 0] for k in range(self.count)], axis=0)
-
-
-def rows_times(places, x, weight, columns, tile, finish, extra, outs, name):
+        return jnp.concatenate([refs[0][places[k], 0] for k in range(self.n_dp)], axis=0)
+
+
+class Folded:
+    def __init__(self, array, before, rows, width):
+        self.arrays, self.before, self.width = [array], before, width
+        self.n_dp, self.n_z, self.each = array.shape[0], array.shape[1], rows * width // array.shape[3]
+        self.rows = self.n_dp * rows
+
+    def specs(self):
+        columns = self.arrays[0].shape[3]
+        at = self.before // self.each
+        return [pl.BlockSpec((self.n_dp, self.n_z, self.each, columns), lambda j, p: (0, 0, at, 0))]
+
+    def load(self, refs, places):
+        times = self.arrays[0].shape[3] // self.width
+
+        def block(k, r):
+            held = refs[0][places[k], places[self.n_dp + r]]
+            return jnp.concatenate([held[:, i * self.width : (i + 1) * self.width] for i in range(times)], axis=0)
+
+        rows = [jnp.concatenate([block(k, r) for r in range(self.n_z)], axis=1) for k in range(self.n_dp)]
+        return jnp.concatenate(rows, axis=0)
+
+
+def rows_times(places, x, weight, columns, tile, finish, extra, outs, name, chunks=1):
     length, depth = x.shape
     count = len(weight.arrays)
 
     def kernel(places_ref, x_ref, *refs):
         w = weight.load(refs[:count], places_ref)
-        done = finish(dot(x_ref[...], w), *(r[...] for r in refs[count : count + len(extra)]))
-        for ref, value in zip(refs[count + len(extra) :], done):
-            ref[...] = value
+        for low in range(0, tile, tile // chunks):
+            cols = slice(low, low + tile // chunks)
+            done = finish(dot(x_ref[...], w[:, cols]), *(r[:, cols] for r in refs[count : count + len(extra)]))
+            for ref, value in zip(refs[count + len(extra) :], done):
+                ref[:, cols] = value
 
     tall = pl.BlockSpec((length, tile), lambda j, p: (0, j))
     return pl.pallas_call(
@@ -287,7 +312,11 @@
     )(places, x, *weight.arrays, *extra)
 
 
-def rows_times_t(places, x, weight, tile, finish, by_row, const, row_outs, sums, name):
+def rows_times_t(places, x, weight, tile, finish, by_row, mods, row_outs, sums, name, to_place=None):
+    n_dp = weight.n_dp
+    feature = weight.rows // n_dp
+    aligned = to_place is not None and feature % 128 == 0
+    const = (mods,) if to_place is None or aligned else (mods, to_place)
     length, depth = x.shape
     count, steps, chunk = len(weight.arrays), depth // tile, SPATIAL * 2
     n_by, n_const, n_out = len(by_row), len(const), len(row_outs)
@@ -312,16 +341,21 @@
             totals = None
             for i in range(0, length, chunk):
                 rows = slice(i, i + chunk)
-                done, adds = finish(acc[rows], *(r[rows] for r in by_refs), *(r[...] for r in const_refs))
+                done, adds = finish(acc[rows], *(r[rows] for r in by_refs), const_refs[0][...])
                 for ref, value in zip(out_refs, done):
-                    ref[rows] = value
+                    if aligned:
+                        for k in range(n_dp):
+                            at = pl.multiple_of(places_ref[k] * feature, 128)
+                            ref[rows, pl.ds(at, feature)] = value[:, k * feature : (k + 1) * feature]
+                    else:
+                        ref[rows] = value if to_place is None else dot_nt(value, const_refs[1][...]).astype(BF)
                 adds = [jnp.sum(v, axis=0, keepdims=True) for v in adds]
                 totals = adds if totals is None else [t + v for t, v in zip(totals, adds)]
             if sums:
                 sum_ref[...] = jnp.concatenate(totals, axis=0)
 
-    def full(shape):
-        return pl.BlockSpec(shape, lambda j, p: (0, 0))
+    def full(shape, **how):
+        return pl.BlockSpec(shape, lambda j, p: (0, 0), **how)
 
     shapes = [jax.ShapeDtypeStruct(s, t) for s, t in row_outs]
     if sums:
@@ -333,12 +367,12 @@
             grid=(steps,),
             in_specs=[pl.BlockSpec((length, tile), lambda j, p: (0, j))]
             + weight.specs()
-            + [full(v.shape) for v in (*by_row, *const)],
+            + [full(v.shape, pipeline_mode=pl.Buffered(1)) for v in (*by_row, *const)],
             out_specs=[full(v.shape) for v in shapes],
             scratch_shapes=[pltpu.VMEM((length, weight.rows), F32)],
         ),
         out_shape=shapes,
-        compiler_params=params(),
+        compiler_params=params(40),
         cost_estimate=COST,
         name=name,
     )(places, x, *weight.arrays, *by_row, *const)
@@ -538,9 +572,8 @@
     return (branch_a, middle, normed), ()
 
 
-def after_mlp(branch_b, middle, grad_result, mods, to_place):
-    result = (middle + mods[5:6] * branch_b).astype(BF)
-    return (dot_nt(result, to_place).astype(BF),), (grad_result.astype(F32) * branch_b,)
+def after_mlp(branch_b, middle, grad_result, mods):
+    return ((middle + mods[5:6] * branch_b).astype(BF),), (grad_result.astype(F32) * branch_b,)
 
 
 def back_mlp(grad_nb, middle, branch_a, grad_result, mods):
@@ -552,10 +585,10 @@
     )
 
 
-def back_attention(grad_na, resid, grad_middle, mods, to_place):
+def back_attention(grad_na, resid, grad_middle, mods):
     norm_a, inv_a = normalize(resid.astype(F32))
     grad_tokens = (grad_middle + norm_back(norm_a, inv_a, mods[1:2], grad_na)).astype(BF)
-    return (dot_nt(grad_tokens, to_place).astype(BF),), (grad_na, grad_na * norm_a)
+    return (grad_tokens,), (grad_na, grad_na * norm_a)
 
 
 def gelu_and_slope(v):
@@ -628,8 +661,16 @@
     def butterfly(name, value, axis, size):
         return Chain(name, butterfly_steps(value, axis, size), size.bit_length() - 1)
 
-    mlp = lax.all_gather(jnp.concatenate([w_up, w_down], axis=0), ("dp", "tensor"), axis=0)
-    wu, wd = (Gathered(mlp.reshape(n_dp, n_z, -1, w_up.shape[1]), i, 2) for i in (0, 1))
+    def gathered(shard):
+        return lax.all_gather(shard, ("dp", "tensor"), axis=0).reshape((n_dp, n_z) + shard.shape)
+
+    times = hidden_tile // out_tile
+    if feature % (16 * times) == 0:
+        folded = jnp.concatenate(jnp.split(w_out, times, axis=0), axis=1)
+        held = gathered(jnp.concatenate([w_up, folded], axis=0))
+        wu, wo = Gathered(held, feature), Folded(held, feature, feature, out_tile)
+    else:
+        wu, wo = Gathered(gathered(w_up), feature), Folded(gathered(w_out), 0, feature, out_tile)
 
     def turned(blocks):
         return jnp.concatenate([lax.dynamic_slice_in_dim(blocks, (z - r) % n_z, 1) for r in range(n_z)], axis=0)
@@ -645,12 +686,11 @@
     mod_part = dot(cond_mine, w_ada)
     columns = mod_part.shape[1]
     mod_part = lax.all_to_all(jnp.concatenate([mod_part, table], axis=1), ("dp", "tensor"), 0, 0, tiled=True)
-    blocks = shifted([jnp.concatenate([w_qkv.reshape(feature, -1), w_out], axis=1)] * n_z, n_z, 1)
+    blocks = shifted([w_qkv.reshape(feature, -1)] * n_z, n_z, 1)
     blocks, to_place, got_tokens, places, count, mod_part = slot(
         [], blocks, to_place, for_clips(tokens), places, count, mod_part
     )
-    wa, wo = join_parts(blocks, 1, [qkv_tile, out_tile])
-    wa, wo = gather("qkv", wa, True), gather("out", wo, True)
+    wa = gather("qkv", join(blocks, 1), True)
     table = mod_part[:, columns:].reshape(n_dp, n_z, share).transpose(1, 0, 2).reshape(n_z, -1)[:, : pos_table.size]
     mods = jnp.sum(mod_part[:, :columns].reshape(n_dp, n_z, -1), axis=0).reshape(6, model)
     mods = jnp.dot(mods, to_place.astype(F32), precision=HIGHEST)
@@ -658,42 +698,43 @@
     got_tokens, bias, mods = slot([wa], to_clip(got_tokens), bias, mods)
     resid = in_order(got_tokens)
     normed_a = (normalize(resid.astype(F32))[0] * (1.0 + mods[1:2]) + mods[0:1]).astype(BF)
-    normed_a = slot([wa], normed_a)
+    normed_a, w_down = slot([wa], normed_a, w_down)
     rows_of = (FRAMES * SPATIAL, model)
 
-    w_in = Pieces(whole(wa), qkv_tile)
+    w_in = Pieces(whole(wa), qkv_tile, n_dp)
     qkv, = rows_times(places, normed_a, w_in, qkv_tile * n_z, qkv_tile, lambda v: (v.astype(BF),), (), (BF,), "qkv")
-    qkv = slot([wo], qkv)
+    blocks = shifted([w_down] * n_z, n_z, 1)
     attended, probs = attend(count, qkv, bias, n_z)
-    attended, probs, got_cotangent = slot([wo], attended, probs, for_clips(cotangent))
+    qkv, blocks, attended, probs, got_cotangent = slot([], qkv, blocks, attended, probs, for_clips(cotangent))
+    wd = gather("down", join(blocks, 1))
     got_cotangent = to_clip(got_cotangent)
-    wo = Pieces(whole(wo), out_tile * n_z)
     branch_a, middle, normed_b = rows_times_t(
-        places, attended, wo, out_tile * n_z, after_attention, (resid,), (mods,),
+        places, attended, wo, out_tile * n_z, after_attention, (resid,), mods,
         ((rows_of, F32), (rows_of, F32), (rows_of, BF)), 0, "out",
     )
-    activ, slope = rows_times(places, normed_b, wu, hidden_tile * n_z, hidden_tile, gelu_and_slope, (), (BF, BF), "up")
-    activ, slope, got_cotangent = slot([], activ, slope, got_cotangent)
+    activ, slope = rows_times(places, normed_b, wu, hidden_tile * n_z, hidden_tile, gelu_and_slope, (), (BF, BF), "up", 4)
+    activ, slope, got_cotangent = slot([wd], activ, slope, got_cotangent)
     grad_result = in_order(got_cotangent)
     grad_bb = (grad_result.astype(F32) * mods[5:6]).astype(BF)
     gd = rows_against(grad_bb, activ, hidden_tile, "grad_down")
-    activ, slope, grad_bb, gd = slot([], activ, slope, grad_bb, gd)
+    activ, slope, grad_bb, gd = slot([wd], activ, slope, grad_bb, gd)
     gd = sum_dp("down", gd)
+    activ, slope, grad_bb = slot([wd, gd], activ, slope, grad_bb)
+    wd = Pieces(whole(wd), hidden_tile, n_dp)
 
     grad_hidden, = rows_times(
         places, grad_bb, wd, hidden_tile * n_z, hidden_tile, lambda v, s: ((v * s.astype(F32)).astype(BF),), (slope,), (BF,),
         "grad_hidden",
     )
-    grad_hidden, activ = slot([gd], grad_hidden, activ)
     gu = rows_against(normed_b, grad_hidden, hidden_tile, "grad_up")
     block_out, sums_mlp = rows_times_t(
-        places, activ, wd, hidden_tile, after_mlp, (middle, grad_result), (mods, to_place), ((rows_of, BF),), 1, "down"
+        places, activ, wd, hidden_tile, after_mlp, (middle, grad_result), mods, ((rows_of, BF),), 1, "down", to_place
     )
     grad_hidden, gu, block_out = slot([gd], grad_hidden, gu, from_clip(block_out))
     gu = sum_dp("up", gu)
     out_rows = exchange("tokens_out", block_out, -1)
     grad_middle, grad_ba, sums_mid = rows_times_t(
-        places, grad_hidden, wu, hidden_tile, back_mlp, (middle, branch_a, grad_result), (mods,),
+        places, grad_hidden, wu, hidden_tile, back_mlp, (middle, branch_a, grad_result), mods,
         ((rows_of, F32), (rows_of, BF)), 3, "grad_normed_b",
     )
     grad_middle, grad_ba = slot([gd, gu, out_rows], grad_middle, grad_ba)
@@ -714,8 +755,8 @@
     gq = sum_dp("qkv", gq, few)
     up_rows = exchange("up_sum", whole(gu), -1)
     grad_tokens, sums_in = rows_times_t(
-        places, grad_qkv, w_in, qkv_tile, back_attention, (resid, grad_middle), (mods, to_place), ((rows_of, BF),), 2,
-        "grad_normed_a",
+        places, grad_qkv, w_in, qkv_tile, back_attention, (resid, grad_middle), mods, ((rows_of, BF),), 2,
+        "grad_normed_a", to_place,
     )
     up_rows.step()
     in_rows = exchange("tokens_out", from_clip(grad_tokens), -1)

time: 472 us -> 466 us (0.987)
  waiting for transfers between devices: 77.2 us -> 104 us
  Pallas kernels: 155 us -> 132 us
  starting transfers between devices: 84.3 us -> 77.3 us
    ppermute x3 -> x5, waiting for transfers between devices: 1.56 us -> 20.5 us  [the longest x2 13 us: gather_steps(): got = lax.ppermute(rows, 'dp', stage_perm(n_dp, t))]
    all_to_all x1, waiting for transfers between devices: 23.5 us -> 11.2 us  [body(): lax.all_to_all(jnp.concatenate([mod_part, table], axis=1), ('dp', 'tensor...]
    unnamed x178 -> x170, local copies, waits for them, and re-layouts: 28.9 us -> 40.3 us
    pallas_call x4, Pallas kernels: 49.3 us -> 38 us  [rows_times_t(): pl.pallas_call(kernel, grid_spec=pltpu.PrefetchScalarGridSpec(num_scalar_...]
    ppermute x3, waiting for transfers between devices: 0.01 us -> 6.65 us  [scatter_steps(): got = lax.ppermute(send, 'dp', core_perm(n_dp))]
    pallas_call x4, Pallas kernels: 36.3 us -> 29.8 us  [rows_times(): pl.pallas_call(kernel, grid_spec=pltpu.PrefetchScalarGridSpec(num_scalar_...]
    ppermute x8 -> x6, waiting for transfers between devices: 0.02 us -> 5.89 us  [gather_steps(): yield (rows + [lax.ppermute(p, 'dp', core_perm(n_dp)) for p in rows])]
    pallas_call x4, Pallas kernels: 32.5 us -> 26.7 us  [rows_against(): pl.pallas_call(kernel, grid_spec=pltpu.PrefetchScalarGridSpec(num_scalar_...]
  transfers between devices with their start and end apart: 54 -> 54, of which waited for: 8 -> 20; matrix products, arithmetic and copies ran while one was open for 20% -> 19% of each run, Pallas kernels for 31% -> 28%
where the time goes in v4:
time: 466 us; the launch traced here: 461 us
  Pallas kernels  132 us (28%)
  waiting for transfers between devices  104 us (22%)
  local copies, waits for them, and re-layouts  78.8 us (17%)
  starting transfers between devices  77.3 us (17%)
  other arithmetic  37.4 us (8%)
  matrix products  15.8 us (3%)
  between operations  15.5 us (3%)
    ppermute x15, waiting for transfers between devices, shifted(): lax.ppermute(pieces[r], 'tensor', ring(n_z, sign * r))  41 us
    unnamed x170, local copies, waits for them, and re-layouts  40.3 us
    pallas_call x4, Pallas kernels, rows_times_t(): pl.pallas_call(kernel, grid_spec=pltpu.PrefetchScalarGridSpec(num_scalar_...  38 us
    ppermute x15, starting transfers between devices, shifted(): lax.ppermute(pieces[r], 'tensor', ring(n_z, sign * r))  32.3 us
    pallas_call x4, Pallas kernels, rows_times(): pl.pallas_call(kernel, grid_spec=pltpu.PrefetchScalarGridSpec(num_scalar_...  29.8 us
    pallas_call x4, Pallas kernels, rows_against(): pl.pallas_call(kernel, grid_spec=pltpu.PrefetchScalarGridSpec(num_scalar_...  26.7 us
    convert_element_type x7, other arithmetic, add_low(): functools.reduce(lambda a, b: a + b, [o.astype(F32) for o in others], fir...  22.2 us
    pallas_call x1, Pallas kernels, attend_back(): pl.pallas_call(functools.partial(attend_back_kernel, heads), grid_spec=pl...  17.5 us
  transfers between devices with their start and end apart: 54, of which 20 were waited for; matrix products, arithmetic and copies ran while one was open for 19% of the time, Pallas kernels for 28%

profile of v4, /device:TPU:0, one launch (start us, length us, event | category | flops | bytes accessed | tf_op | source)
XLA Modules:
  0.0 460.7 jit_solution(15536400997469989377)
XLA Ops:
  19.4 3.7 all-to-all-start
  36.8 11.2 %all-to-all-done.1 = f32[32,1,2549]{2,1,0:T(1,128)} async-done(((f32[32,1,2549]{2,1,0:T(1,128)}), f32[32,1,2549]{2,1,0:T(1,128)}, u32[]{:S(2)}, u32[]{:S(2)}) %all-to-all-start.1) | async-done | bytes 326304 | tf_op jit(solution)/shard_map/all_to_all | solution.py:688
  59.4 11.3 %collective-permute-done.6 = bf16[10,16,1024]{2,1,0:T(8,128)(2,1)S(1)} collective-permute-done((bf16[10,16,1024]{2,1,0:T(8,128)(2,1)}, bf16[10,16,1024]{2,1,0:T(8,128)(2,1)S(1)}, u32[]{:S(2)}, u32[]{:S(2)}) %collective-permute-start.6) | collective-permute-done | bytes 327712 | tf_op jit(solution)/shard_map/tokens_in/ppermute | solution.py:183
  71.4 4.8 %fusion.10 = f32[16,9,64,64]{3,1,2,0:T(8,128)S(1)} fusion(pred[64,64,225,1]{2,1,0,3:T(32,128)(4,1)} %bitcast.139, f32[16,9,225]{2,1,0:T(8,128)S(1)} %dot_general.30), kind=kOutput, calls=%fused_computation.73 | convolution fusion | flops 1592524800 | bytes 3410496 | tf_op jit(solution)/shard_map/dot_general | solution.py:210
  76.3 3.6 copy.87.bias_ref
  81.0 7.3 %collective-permute-done.7 = bf16[10,16,1024]{2,1,0:T(8,128)(2,1)} collective-permute-done((bf16[10,16,1024]{2,1,0:T(8,128)(2,1)}, bf16[10,16,1024]{2,1,0:T(8,128)(2,1)}, u32[]{:S(2)}, u32[]{:S(2)}) %collective-permute-start.7) | collective-permute-done | bytes 327712 | tf_op jit(solution)/shard_map/tokens_in/ppermute | solution.py:183
  91.1 3.7 collective-permute-done.5.refs_3_
  109.3 7.1 %qkv.1.qkv_ref = bf16[640,3072]{1,0:T(8,128)(2,1)S(1)} custom-call(s32[12]{0:T(128)S(1)} %pad_add_fusion.places_ref, bf16[640,1024]{1,0:T(8,128)(2,1)S(1)} %fusion.7.x_ref, bf16[128,3072]{1,0:T(8,128)(2,1)} %join.3.refs_0_, bf16[128,3072]{1,0:T(8,128)(2,1)} %collective-permute-done.3.refs_1_, bf16[128,3072]{1,0:T(8,128)(2,1)} %collective-permute-done.4.refs_2_, ...), custom_call_target="tpu_custom_call" | custom-call | flops 1000000 | bytes 10000 | tf_op jit(solution)/shard_map/qkv/pallas_call | solution.py:300
  117.3 14.9 %attend.1 = (bf16[640,1024]{1,0:T(8,128)(2,1)S(1)}, bf16[2,16,320,320]{3,2,1,0:T(8,128)(2,1)S(1)}) custom-call(s32[1]{0:T(128)} %dynamic_slice.67.count_ref, bf16[640,3072]{1,0:T(8,128)(2,1)S(1)} %qkv.1.qkv_ref, f32[16,9,64,64]{3,2,1,0:T(8,128)S(1)} %bitcast.131), custom_call_target="tpu_custom_call" | custom-call | flops 1000000 | bytes 10000 | tf_op jit(solution)/shard_map/attend/pallas_call | solution.py:505
  141.2 9.8 %collective-permute-start.17 = (bf16[10,16,1024]{2,1,0:T(8,128)(2,1)}, bf16[10,16,1024]{2,1,0:T(8,128)(2,1)}, u32[]{:S(2)}, u32[]{:S(2)}) collective-permute-start(bf16[10,16,1024]{2,1,0:T(8,128)(2,1)} %get-tuple-element.216), channel_id=1, source_target_pairs={{0,1},{1,2},{2,3},{3,0},{4,5},{5,6},{6,7},{7,4},{8,9},{9,10},{10,1... | collective-permute-start | bytes 983048 | tf_op jit(solution)/shard_map/tokens_in/ppermute | solution.py:183
  154.7 4.7 %out.1 = (f32[640,1024]{1,0:T(8,128)S(1)}, f32[640,1024]{1,0:T(8,128)S(1)}, bf16[640,1024]{1,0:T(8,128)(2,1)S(1)}) custom-call(s32[12]{0:T(128)S(1)} %pad_add_fusion.places_ref, bf16[640,1024]{1,0:T(8,128)(2,1)S(1)} %copy-done.14, bf16[8,4,160,1024]{3,2,1,0:T(8,128)(2,1)} %bitcast.122, bf16[640,1024]{1,0:T(8,128)(2,1)S(1)} %get-tuple-element.445.refs_1_.refs_8_, ...), custom_call_target="tpu_custom_call" | custom-call | flops 1000000 | bytes 10000 | tf_op jit(solution)/shard_map/out/pallas_call | solution.py:363
  164.7 12.6 %up.1 = (bf16[640,4096]{1,0:T(8,128)(2,1)S(1)}, bf16[640,4096]{1,0:T(8,128)(2,1)S(1)}) custom-call(s32[12]{0:T(128)S(1)} %pad_add_fusion.places_ref, bf16[640,1024]{1,0:T(8,128)(2,1)S(1)} %copy-done.17, bf16[8,4,160,1024]{3,2,1,0:T(8,128)(2,1)S(1)} %bitcast.124), custom_call_target="tpu_custom_call" | custom-call | flops 1000000 | bytes 10000 | tf_op jit(solution)/shard_map/up/pallas_call | solution.py:300
  188.4 8.5 %grad_down.1 = (bf16[512,4096]{1,0:T(8,128)(2,1)S(1)}, bf16[512,4096]{1,0:T(8,128)(2,1)S(1)}) custom-call(s32[1]{0:T(128)} %constant.239.clone.1.places_ref, bf16[640,1024]{1,0:T(8,128)(2,1)S(1)} %get-tuple-element.237.x_ref, bf16[640,4096]{1,0:T(8,128)(2,1)S(1)} %bitcast.129), custom_call_target="tpu_custom_call" | custom-call | flops 1000000 | bytes 10000 | tf_op jit(solution)/shard_map/grad_down/pallas_call | solution.py:409
  196.9 13.0 %collective-permute-done.20.refs_1_ = bf16[256,4096]{1,0:T(8,128)(2,1)S(1)} collective-permute-done((bf16[256,4096]{1,0:T(8,128)(2,1)S(1)}, bf16[256,4096]{1,0:T(8,128)(2,1)S(1)}, u32[]{:S(2)}, u32[]{:S(2)}) %collective-permute-start.20) | collective-permute-done | bytes 2097184 | tf_op jit(solution)/shard_map/gather_down_2_left/ppermute | solution.py:101
  210.4 6.6 %collective-permute-done.21 = bf16[512,4096]{1,0:T(8,128)(2,1)S(1)} collective-permute-done((bf16[512,4096]{1,0:T(8,128)(2,1)S(1)}, bf16[512,4096]{1,0:T(8,128)(2,1)S(1)}, u32[]{:S(2)}, u32[]{:S(2)}) %collective-permute-start.21) | collective-permute-done | bytes 4194336 | tf_op jit(solution)/shard_map/scatter_down_3_left/ppermute | solution.py:113
  224.6 7.9 %grad_hidden.1.y_ref.x_ref = bf16[640,4096]{1,0:T(8,128)(2,1)S(1)} custom-call(s32[12]{0:T(128)S(1)} %pad_add_fusion.places_ref, bf16[640,1024]{1,0:T(8,128)(2,1)S(1)} %get-tuple-element.237.x_ref, bf16[256,4096]{1,0:T(8,128)(2,1)S(1)} %join.5.refs_0_, bf16[256,4096]{1,0:T(8,128)(2,1)S(1)} %collective-permute-done.20.refs_1_, ...), custom_call_target="tpu_custom_call" | custom-call | flops 1000000 | bytes 10000 | tf_op jit(solution)/shard_map/grad_hidden/pallas_call | solution.py:300
  232.5 8.5 %grad_up.1 = (bf16[512,4096]{1,0:T(8,128)(2,1)S(1)}, bf16[512,4096]{1,0:T(8,128)(2,1)S(1)}) custom-call(s32[1]{0:T(128)} %constant.239.clone.1.places_ref, bf16[640,1024]{1,0:T(8,128)(2,1)S(1)} %copy-done.18, bf16[640,4096]{1,0:T(8,128)(2,1)S(1)} %grad_hidden.1.y_ref.x_ref), custom_call_target="tpu_custom_call" | custom-call | flops 1000000 | bytes 10000 | tf_op jit(solution)/shard_map/grad_up/pallas_call | solution.py:409
  244.7 10.3 %down.1 = (bf16[640,1024]{1,0:T(8,128)(2,1)S(1)}, f32[1,1024]{1,0:T(1,128)S(1)}) custom-call(s32[12]{0:T(128)S(1)} %pad_add_fusion.places_ref, bf16[640,4096]{1,0:T(8,128)(2,1)} %copy-done.5, bf16[256,4096]{1,0:T(8,128)(2,1)S(1)} %join.5.refs_0_, bf16[256,4096]{1,0:T(8,128)(2,1)S(1)} %collective-permute-done.20.refs_1_, ...), custom_call_target="tpu_custom_call" | custom-call | flops 1000000 | bytes 10000 | tf_op jit(solution)/shard_map/down/pallas_call | solution.py:363
  256.0 3.8 add_convert_fusion.6
  260.9 12.3 %grad_normed_b.1 = (f32[640,1024]{1,0:T(8,128)S(1)}, bf16[640,1024]{1,0:T(8,128)(2,1)S(1)}, f32[3,1024]{1,0:T(4,128)S(1)}) custom-call(s32[12]{0:T(128)S(1)} %pad_add_fusion.places_ref, bf16[640,4096]{1,0:T(8,128)(2,1)} %copy-done.2, bf16[8,4,160,1024]{3,2,1,0:T(8,128)(2,1)} %bitcast.123, f32[640,1024]{1,0:T(8,128)S(1)} %copy-done.10, ...), custom_call_target="tpu_custom_call" | custom-call | flops 1000000 | bytes 10000 | tf_op jit(solution)/shard_map/grad_normed_b/pallas_call | solution.py:363
  289.1 17.5 %attend_back.1 = (bf16[640,3072]{1,0:T(8,128)(2,1)S(1)}, f32[16,9,64,64]{3,2,1,0:T(8,128)S(1)}) custom-call(s32[1]{0:T(128)} %dynamic_slice.67.count_ref, bf16[640,3072]{1,0:T(8,128)(2,1)S(1)} %copy-done.4, bf16[2,16,320,320]{3,2,1,0:T(8,128)(2,1)S(1)} %bitcast.134, bf16[640,1024]{1,0:T(8,128)(2,1)S(1)} %grad_att.1.gatt_ref), custom_call_target="tpu_custom_call" | custom-call | flops 1000000 | bytes 10000 | tf_op jit(solution)/shard_map/attend_back/pallas_call | solution.py:533
  308.8 5.1 %add_convert_fusion.5 = (bf16[128,4096]{1,0:T(8,128)(2,1)}, bf16[128,4096]{1,0:T(8,128)(2,1)}) fusion(bf16[256,4096]{1,0:T(8,128)(2,1)} %collective-permute-done.28, bf16[256,4096]{1,0:T(8,128)(2,1)S(1)} %copy-done.44), kind=kLoop, calls=%fused_computation.19 | loop fusion | flops 4194304 | bytes 6291456 | tf_op jit(solution)/shard_map/scatter_up_1_left/convert_element_type | solution.py:108
  315.3 5.4 %reshape.377 = f32[144,4096]{1,0:T(8,128)} reshape(f32[16,9,64,64]{3,2,1,0:T(8,128)} %copy-done.20) | data formatting | bytes 4718592 | tf_op jit(solution)/shard_map/reshape | solution.py:216
  320.7 4.1 fusion.1
  330.9 7.4 %grad_qkv.1 = (bf16[512,3072]{1,0:T(8,128)(2,1)S(1)}, bf16[512,3072]{1,0:T(8,128)(2,1)}) custom-call(s32[1]{0:T(128)} %constant.239.clone.1.places_ref, bf16[640,1024]{1,0:T(8,128)(2,1)S(1)} %fusion.7.x_ref, bf16[640,3072]{1,0:T(8,128)(2,1)S(1)} %copy-done.7), custom_call_target="tpu_custom_call" | custom-call | flops 1000000 | bytes 10000 | tf_op jit(solution)/shard_map/grad_qkv/pallas_call | solution.py:409
  352.1 10.9 %grad_normed_a.1 = (bf16[640,1024]{1,0:T(8,128)(2,1)S(1)}, f32[2,1024]{1,0:T(2,128)S(1)}) custom-call(s32[12]{0:T(128)S(1)} %pad_add_fusion.places_ref, bf16[640,3072]{1,0:T(8,128)(2,1)} %copy-done.6, bf16[128,3072]{1,0:T(8,128)(2,1)} %join.3.refs_0_, bf16[128,3072]{1,0:T(8,128)(2,1)} %collective-permute-done.3.refs_1_, ...), custom_call_target="tpu_custom_call" | custom-call | flops 1000000 | bytes 10000 | tf_op jit(solution)/shard_map/grad_normed_a/pallas_call | solution.py:363
  363.0 4.1 add_convert_fusion.8
  367.1 4.1 collective-permute-done.37
  381.4 7.6 %collective-permute-done.39.refs_1_ = bf16[128,3072]{1,0:T(8,128)(2,1)S(1)} collective-permute-done((bf16[128,3072]{1,0:T(8,128)(2,1)}, bf16[128,3072]{1,0:T(8,128)(2,1)S(1)}, u32[]{:S(2)}, u32[]{:S(2)}) %collective-permute-start.39) | collective-permute-done | bytes 786464 | tf_op jit(solution)/shard_map/scatter_qkv_1_left/ppermute | solution.py:120
  398.4 4.1 all-to-all-start.2
  408.1 7.3 %all-to-all-done.2 = f32[32,1,2552]{2,1,0:T(1,128)} async-done(((f32[32,1,2552]{2,1,0:T(1,128)}), f32[32,1,2552]{2,1,0:T(1,128)}, u32[]{:S(2)}, u32[]{:S(2)}) %all-to-all-start.2) | async-done | bytes 326688 | tf_op jit(solution)/shard_map/all_to_all | solution.py:772
  432.3 17.2 %collective-permute-done.46 = bf16[128,1024]{1,0:T(8,128)(2,1)S(1)} collective-permute-done((bf16[128,1024]{1,0:T(8,128)(2,1)}, bf16[128,1024]{1,0:T(8,128)(2,1)S(1)}, u32[]{:S(2)}, u32[]{:S(2)}) %collective-permute-start.46) | collective-permute-done | bytes 262176 | tf_op jit(solution)/shard_map/ppermute | solution.py:183
  (383 shorter events, 185.0 us)
Async XLA Ops:
  7.2 146.2 %all-gather.3.cloned.1.call-start = ((), (), s32[]{:S(2)}) async-start(), calls=%async_computation.6 | async-start | bytes 10813440 | tf_op jit(solution)/shard_map/all_gather | solution.py:665
  11.0 38.8 %collective-permute-start = (bf16[128,768]{1,0:T(8,128)(2,1)S(1)}, bf16[128,768]{1,0:T(8,128)(2,1)S(1)}, u32[]{:S(2)}, u32[]{:S(2)}) collective-permute-start(bf16[128,768]{1,0:T(8,128)(2,1)S(1)} %copy.79), channel_id=1, source_target_pairs={{0,1},{1,2},{2,3},{3,0},{4,5},{5,6},{6,7},{7,4},{8,9},{9,10},{10,1... | collective-permute-start | bytes 589832 | tf_op jit(solution)/shard_map/ppermute | solution.py:183
  14.1 35.7 %collective-permute-start.1 = (bf16[128,768]{1,0:T(8,128)(2,1)S(1)}, bf16[128,768]{1,0:T(8,128)(2,1)S(1)}, u32[]{:S(2)}, u32[]{:S(2)}) collective-permute-start(bf16[128,768]{1,0:T(8,128)(2,1)S(1)} %copy.79), channel_id=1, source_target_pairs={{0,2},{1,3},{2,0},{3,1},{4,6},{5,7},{6,4},{7,5},{8,10},{9,11},{10,... | collective-permute-start | bytes 589832 | tf_op jit(solution)/shard_map/ppermute | solution.py:183
  16.7 33.1 %collective-permute-start.2 = (bf16[128,768]{1,0:T(8,128)(2,1)S(1)}, bf16[128,768]{1,0:T(8,128)(2,1)S(1)}, u32[]{:S(2)}, u32[]{:S(2)}) collective-permute-start(bf16[128,768]{1,0:T(8,128)(2,1)S(1)} %copy.79), channel_id=1, source_target_pairs={{0,3},{1,0},{2,1},{3,2},{4,7},{5,4},{6,5},{7,6},{8,11},{9,8},{10,9... | collective-permute-start | bytes 589832 | tf_op jit(solution)/shard_map/ppermute | solution.py:183
  32.5 384.7 %reduce-scatter.2.cloned.1.call-start = ((), (), s32[]{:S(2)}) async-start(), calls=%async_computation.5 | async-start | bytes 2359296 | tf_op jit(solution)/shard_map/reduce_scatter | solution.py:748
  51.0 40.2 %collective-permute-start.3 = (bf16[128,3072]{1,0:T(8,128)(2,1)}, bf16[128,3072]{1,0:T(8,128)(2,1)}, u32[]{:S(2)}, u32[]{:S(2)}) collective-permute-start(bf16[128,3072]{1,0:T(8,128)(2,1)} %join.3.refs_0_), channel_id=1, source_target_pairs={{0,8},{4,20},{8,0},{12,28},{16,24},{20,4},{24,16},{28,12},{1,9},{5... | collective-permute-start | bytes 2359304 | tf_op jit(solution)/shard_map/gather_qkv_2_left/ppermute | solution.py:98
  52.3 38.9 %collective-permute-start.4 = (bf16[128,3072]{1,0:T(8,128)(2,1)}, bf16[128,3072]{1,0:T(8,128)(2,1)}, u32[]{:S(2)}, u32[]{:S(2)}) collective-permute-start(bf16[128,3072]{1,0:T(8,128)(2,1)} %join.3.refs_0_), channel_id=1, source_target_pairs={{0,16},{4,12},{8,24},{12,4},{16,0},{20,28},{24,8},{28,20},{1,17},{... | collective-permute-start | bytes 2359304 | tf_op jit(solution)/shard_map/gather_qkv_2_left/ppermute | solution.py:98
  53.3 41.5 %collective-permute-start.5 = (bf16[128,3072]{1,0:T(8,128)(2,1)}, bf16[128,3072]{1,0:T(8,128)(2,1)}, u32[]{:S(2)}, u32[]{:S(2)}) collective-permute-start(bf16[128,3072]{1,0:T(8,128)(2,1)} %join.3.refs_0_), channel_id=1, source_target_pairs={{0,24},{4,28},{8,16},{12,20},{16,8},{20,12},{24,0},{28,4},{1,25},{... | collective-permute-start | bytes 2359304 | tf_op jit(solution)/shard_map/gather_qkv_2_left/ppermute | solution.py:98
  58.2 30.0 %collective-permute-start.7 = (bf16[10,16,1024]{2,1,0:T(8,128)(2,1)}, bf16[10,16,1024]{2,1,0:T(8,128)(2,1)}, u32[]{:S(2)}, u32[]{:S(2)}) collective-permute-start(bf16[10,16,1024]{2,1,0:T(8,128)(2,1)} %get-tuple-element.180), channel_id=1, source_target_pairs={{0,2},{1,3},{2,0},{3,1},{4,6},{5,7},{6,4},{7,5},{8,10},{9,11},{10,... | collective-permute-start | bytes 983048 | tf_op jit(solution)/shard_map/tokens_in/ppermute | solution.py:183
  102.4 33.9 %collective-permute-start.13 = (bf16[128,1024]{1,0:T(8,128)(2,1)S(1)}, bf16[128,1024]{1,0:T(8,128)(2,1)S(1)}, u32[]{:S(2)}, u32[]{:S(2)}) collective-permute-start(bf16[128,1024]{1,0:T(8,128)(2,1)S(1)} %copy-done.37), channel_id=1, source_target_pairs={{0,1},{1,2},{2,3},{3,0},{4,5},{5,6},{6,7},{7,4},{8,9},{9,10},{10,1... | collective-permute-start | bytes 786440 | tf_op jit(solution)/shard_map/ppermute | solution.py:183
  104.1 33.9 %collective-permute-start.14 = (bf16[128,1024]{1,0:T(8,128)(2,1)S(1)}, bf16[128,1024]{1,0:T(8,128)(2,1)S(1)}, u32[]{:S(2)}, u32[]{:S(2)}) collective-permute-start(bf16[128,1024]{1,0:T(8,128)(2,1)S(1)} %copy-done.37), channel_id=1, source_target_pairs={{0,2},{1,3},{2,0},{3,1},{4,6},{5,7},{6,4},{7,5},{8,10},{9,11},{10,... | collective-permute-start | bytes 786440 | tf_op jit(solution)/shard_map/ppermute | solution.py:183
  106.5 32.1 %collective-permute-start.15 = (bf16[128,1024]{1,0:T(8,128)(2,1)S(1)}, bf16[128,1024]{1,0:T(8,128)(2,1)S(1)}, u32[]{:S(2)}, u32[]{:S(2)}) collective-permute-start(bf16[128,1024]{1,0:T(8,128)(2,1)S(1)} %copy-done.37), channel_id=1, source_target_pairs={{0,3},{1,0},{2,1},{3,2},{4,7},{5,4},{6,5},{7,6},{8,11},{9,8},{10,9... | collective-permute-start | bytes 786440 | tf_op jit(solution)/shard_map/ppermute | solution.py:183
  139.7 42.3 %collective-permute-start.16 = (bf16[128,4096]{1,0:T(8,128)(2,1)}, bf16[128,4096]{1,0:T(8,128)(2,1)}, u32[]{:S(2)}, u32[]{:S(2)}) collective-permute-start(bf16[128,4096]{1,0:T(8,128)(2,1)} %join.4.refs_0_), channel_id=1, source_target_pairs={{0,8},{4,20},{8,0},{12,28},{16,24},{20,4},{24,16},{28,12},{1,9},{5... | collective-permute-start | bytes 3145736 | tf_op jit(solution)/shard_map/gather_down_3_left/ppermute | solution.py:101
  141.2 40.8 %collective-permute-start.17 = (bf16[10,16,1024]{2,1,0:T(8,128)(2,1)}, bf16[10,16,1024]{2,1,0:T(8,128)(2,1)}, u32[]{:S(2)}, u32[]{:S(2)}) collective-permute-start(bf16[10,16,1024]{2,1,0:T(8,128)(2,1)} %get-tuple-element.216), channel_id=1, source_target_pairs={{0,1},{1,2},{2,3},{3,0},{4,5},{5,6},{6,7},{7,4},{8,9},{9,10},{10,1... | collective-permute-start | bytes 983048 | tf_op jit(solution)/shard_map/tokens_in/ppermute | solution.py:183
  151.0 31.0 %collective-permute-start.18 = (bf16[10,16,1024]{2,1,0:T(8,128)(2,1)}, bf16[10,16,1024]{2,1,0:T(8,128)(2,1)}, u32[]{:S(2)}, u32[]{:S(2)}) collective-permute-start(bf16[10,16,1024]{2,1,0:T(8,128)(2,1)} %get-tuple-element.217), channel_id=1, source_target_pairs={{0,2},{1,3},{2,0},{3,1},{4,6},{5,7},{6,4},{7,5},{8,10},{9,11},{10,... | collective-permute-start | bytes 983048 | tf_op jit(solution)/shard_map/tokens_in/ppermute | solution.py:183
  152.4 29.6 %collective-permute-start.19 = (bf16[10,16,1024]{2,1,0:T(8,128)(2,1)}, bf16[10,16,1024]{2,1,0:T(8,128)(2,1)}, u32[]{:S(2)}, u32[]{:S(2)}) collective-permute-start(bf16[10,16,1024]{2,1,0:T(8,128)(2,1)} %get-tuple-element.218), channel_id=1, source_target_pairs={{0,3},{1,0},{2,1},{3,2},{4,7},{5,4},{6,5},{7,6},{8,11},{9,8},{10,9... | collective-permute-start | bytes 983048 | tf_op jit(solution)/shard_map/tokens_in/ppermute | solution.py:183
  183.8 26.1 %collective-permute-start.20 = (bf16[256,4096]{1,0:T(8,128)(2,1)S(1)}, bf16[256,4096]{1,0:T(8,128)(2,1)S(1)}, u32[]{:S(2)}, u32[]{:S(2)}) collective-permute-start(bf16[256,4096]{1,0:T(8,128)(2,1)S(1)} %join.5.refs_0_), channel_id=1, source_target_pairs={{0,16},{4,12},{8,24},{12,4},{16,0},{20,28},{24,8},{28,20},{1,17},{... | collective-permute-start | bytes 6291464 | tf_op jit(solution)/shard_map/gather_down_2_left/ppermute | solution.py:101
  223.1 32.9 %collective-permute-start.24 = (bf16[256,4096]{1,0:T(8,128)(2,1)}, bf16[256,4096]{1,0:T(8,128)(2,1)}, u32[]{:S(2)}, u32[]{:S(2)}) collective-permute-start(bf16[256,4096]{1,0:T(8,128)(2,1)} %get-tuple-element.236), channel_id=1, source_target_pairs={{0,16},{4,12},{8,24},{12,4},{16,0},{20,28},{24,8},{28,20},{1,17},{... | collective-permute-start | bytes 6291464 | tf_op jit(solution)/shard_map/scatter_down_2_left/ppermute | solution.py:126
  279.0 29.9 %collective-permute-start.28 = (bf16[256,4096]{1,0:T(8,128)(2,1)}, bf16[256,4096]{1,0:T(8,128)(2,1)}, u32[]{:S(2)}, u32[]{:S(2)}) collective-permute-start(bf16[256,4096]{1,0:T(8,128)(2,1)} %get-tuple-element.259), channel_id=1, source_target_pairs={{0,16},{4,12},{8,24},{12,4},{16,0},{20,28},{24,8},{28,20},{1,17},{... | collective-permute-start | bytes 6291464 | tf_op jit(solution)/shard_map/scatter_up_2_left/ppermute | solution.py:126
  279.6 35.0 %collective-permute-start.30 = (bf16[10,16,1024]{2,1,0:T(8,128)(2,1)}, bf16[10,16,1024]{2,1,0:T(8,128)(2,1)}, u32[]{:S(2)}, u32[]{:S(2)}) collective-permute-start(bf16[10,16,1024]{2,1,0:T(8,128)(2,1)} %get-tuple-element.265), channel_id=1, source_target_pairs={{0,3},{1,0},{2,1},{3,2},{4,7},{5,4},{6,5},{7,6},{8,11},{9,8},{10,9... | collective-permute-start | bytes 983048 | tf_op jit(solution)/shard_map/tokens_out_1_left/ppermute | solution.py:190
  281.6 33.0 %collective-permute-start.31 = (bf16[10,16,1024]{2,1,0:T(8,128)(2,1)}, bf16[10,16,1024]{2,1,0:T(8,128)(2,1)}, u32[]{:S(2)}, u32[]{:S(2)}) collective-permute-start(bf16[10,16,1024]{2,1,0:T(8,128)(2,1)} %get-tuple-element.267), channel_id=1, source_target_pairs={{0,1},{1,2},{2,3},{3,0},{4,5},{5,6},{6,7},{7,4},{8,9},{9,10},{10,1... | collective-permute-start | bytes 983048 | tf_op jit(solution)/shard_map/tokens_out_1_left/ppermute | solution.py:190
  281.7 32.2 %collective-permute-start.29 = (bf16[128,1024]{1,0:T(8,128)(2,1)S(1)}, bf16[128,1024]{1,0:T(8,128)(2,1)S(1)}, u32[]{:S(2)}, u32[]{:S(2)}) collective-permute-start(bf16[128,1024]{1,0:T(8,128)(2,1)S(1)} %get-tuple-element.262), channel_id=1, source_target_pairs={{0,2},{1,3},{2,0},{3,1},{4,6},{5,7},{6,4},{7,5},{8,10},{9,11},{10,... | collective-permute-start | bytes 786440 | tf_op jit(solution)/shard_map/down_sum_2_left/ppermute | solution.py:190
  314.6 25.4 %collective-permute-start.32 = (bf16[128,4096]{1,0:T(8,128)(2,1)}, bf16[128,4096]{1,0:T(8,128)(2,1)}, u32[]{:S(2)}, u32[]{:S(2)}) collective-permute-start(bf16[128,4096]{1,0:T(8,128)(2,1)} %get-tuple-element.273), channel_id=1, source_target_pairs={{0,8},{4,20},{8,0},{12,28},{16,24},{20,4},{24,16},{28,12},{1,9},{5... | collective-permute-start | bytes 3145736 | tf_op jit(solution)/shard_map/scatter_up_1_left/ppermute | solution.py:126
  347.2 23.9 %collective-permute-start.37 = (bf16[128,1024]{1,0:T(8,128)(2,1)}, bf16[128,1024]{1,0:T(8,128)(2,1)S(1)}, u32[]{:S(2)}, u32[]{:S(2)}) collective-permute-start(bf16[128,1024]{1,0:T(8,128)(2,1)} %get-tuple-element.286), channel_id=1, source_target_pairs={{0,2},{1,3},{2,0},{3,1},{4,6},{5,7},{6,4},{7,5},{8,10},{9,11},{10,... | collective-permute-start | bytes 786440 | tf_op jit(solution)/shard_map/up_sum_2_left/ppermute | solution.py:190
  373.8 43.3 %collective-permute-start.42 = (bf16[10,16,1024]{2,1,0:T(8,128)(2,1)}, bf16[10,16,1024]{2,1,0:T(8,128)(2,1)}, u32[]{:S(2)}, u32[]{:S(2)}) collective-permute-start(bf16[10,16,1024]{2,1,0:T(8,128)(2,1)} %get-tuple-element.415), channel_id=1, source_target_pairs={{0,3},{1,0},{2,1},{3,2},{4,7},{5,4},{6,5},{7,6},{8,11},{9,8},{10,9... | collective-permute-start | bytes 983048 | tf_op jit(solution)/shard_map/tokens_out_1_left/ppermute | solution.py:190
  373.8 43.3 %collective-permute-start.43 = (bf16[10,16,1024]{2,1,0:T(8,128)(2,1)}, bf16[10,16,1024]{2,1,0:T(8,128)(2,1)}, u32[]{:S(2)}, u32[]{:S(2)}) collective-permute-start(bf16[10,16,1024]{2,1,0:T(8,128)(2,1)} %get-tuple-element.414), channel_id=1, source_target_pairs={{0,2},{1,3},{2,0},{3,1},{4,6},{5,7},{6,4},{7,5},{8,10},{9,11},{10,... | collective-permute-start | bytes 983048 | tf_op jit(solution)/shard_map/tokens_out_2_left/ppermute | solution.py:190
  375.7 41.5 %collective-permute-start.44 = (bf16[10,16,1024]{2,1,0:T(8,128)(2,1)}, bf16[10,16,1024]{2,1,0:T(8,128)(2,1)}, u32[]{:S(2)}, u32[]{:S(2)}) collective-permute-start(bf16[10,16,1024]{2,1,0:T(8,128)(2,1)} %get-tuple-element.413), channel_id=1, source_target_pairs={{0,1},{1,2},{2,3},{3,0},{4,5},{5,6},{6,7},{7,4},{8,9},{9,10},{10,1... | collective-permute-start | bytes 983048 | tf_op jit(solution)/shard_map/tokens_out_1_left/ppermute | solution.py:190
  378.7 38.5 %collective-permute-start.40 = (bf16[128,3072]{1,0:T(8,128)(2,1)}, bf16[128,3072]{1,0:T(8,128)(2,1)S(1)}, u32[]{:S(2)}, u32[]{:S(2)}) collective-permute-start(bf16[128,3072]{1,0:T(8,128)(2,1)} %get-tuple-element.302), channel_id=1, source_target_pairs={{0,16},{4,12},{8,24},{12,4},{16,0},{20,28},{24,8},{28,20},{1,17},{... | collective-permute-start | bytes 2359304 | tf_op jit(solution)/shard_map/scatter_qkv_1_left/ppermute | solution.py:120
  388.9 28.3 %collective-permute-start.41 = (bf16[128,3072]{1,0:T(8,128)(2,1)}, bf16[128,3072]{1,0:T(8,128)(2,1)S(1)}, u32[]{:S(2)}, u32[]{:S(2)}) collective-permute-start(bf16[128,3072]{1,0:T(8,128)(2,1)} %get-tuple-element.303), channel_id=1, source_target_pairs={{0,24},{4,28},{8,16},{12,20},{16,8},{20,12},{24,0},{28,4},{1,25},{... | collective-permute-start | bytes 2359304 | tf_op jit(solution)/shard_map/scatter_qkv_1_left/ppermute | solution.py:119
  423.2 26.3 %collective-permute-start.46 = (bf16[128,1024]{1,0:T(8,128)(2,1)}, bf16[128,1024]{1,0:T(8,128)(2,1)S(1)}, u32[]{:S(2)}, u32[]{:S(2)}) collective-permute-start(bf16[128,1024]{1,0:T(8,128)(2,1)} %get-tuple-element.327), channel_id=1, source_target_pairs={{0,2},{1,3},{2,0},{3,1},{4,6},{5,7},{6,4},{7,5},{8,10},{9,11},{10,... | collective-permute-start | bytes 786440 | tf_op jit(solution)/shard_map/ppermute | solution.py:183
  423.2 26.3 %collective-permute-start.47 = (bf16[128,1024]{1,0:T(8,128)(2,1)}, bf16[128,1024]{1,0:T(8,128)(2,1)S(1)}, u32[]{:S(2)}, u32[]{:S(2)}) collective-permute-start(bf16[128,1024]{1,0:T(8,128)(2,1)} %get-tuple-element.328), channel_id=1, source_target_pairs={{0,1},{1,2},{2,3},{3,0},{4,5},{5,6},{6,7},{7,4},{8,9},{9,10},{10,1... | collective-permute-start | bytes 786440 | tf_op jit(solution)/shard_map/ppermute | solution.py:183
  426.2 25.3 %all-to-all-start.3 = ((f32[32,1,1528]{2,1,0:T(1,128)}), f32[32,1,1528]{2,1,0:T(1,128)S(1)}, u32[]{:S(2)}, u32[]{:S(2)}) async-start(f32[32,1,1528]{2,1,0:T(1,128)} %all_to_all.32), calls=%async_computation.4 | async-start | bytes 393216 | tf_op jit(solution)/shard_map/all_to_all | solution.py:784
  (105 other events, 957.2 us)
Sparse Core Ops, SparseCore 0:
  10.9 136.7 all-gather.2
  344.1 46.1 reduce-scatter.1

commit v5 on v4

--- a/solution.py
+++ b/solution.py
@@ -707,25 +707,27 @@
     attended, probs = attend(count, qkv, bias, n_z)
     qkv, blocks, attended, probs, got_cotangent = slot([], qkv, blocks, attended, probs, for_clips(cotangent))
     wd = gather("down", join(blocks, 1))
-    got_cotangent = to_clip(got_cotangent)
+    cot_rows = exchange("tokens_in", got_cotangent, 1)
     branch_a, middle, normed_b = rows_times_t(
         places, attended, wo, out_tile * n_z, after_attention, (resid,), mods,
         ((rows_of, F32), (rows_of, F32), (rows_of, BF)), 0, "out",
     )
+    branch_a, middle, normed_b = slot([wd, cot_rows], branch_a, middle, normed_b)
     activ, slope = rows_times(places, normed_b, wu, hidden_tile * n_z, hidden_tile, gelu_and_slope, (), (BF, BF), "up", 4)
-    activ, slope, got_cotangent = slot([wd], activ, slope, got_cotangent)
-    grad_result = in_order(got_cotangent)
+    cot_rows.step()
+    grad_result = in_order(cot_rows.value)
     grad_bb = (grad_result.astype(F32) * mods[5:6]).astype(BF)
+    activ, slope, grad_bb = slot([wd], activ, slope, grad_bb)
     gd = rows_against(grad_bb, activ, hidden_tile, "grad_down")
     activ, slope, grad_bb, gd = slot([wd], activ, slope, grad_bb, gd)
     gd = sum_dp("down", gd)
-    activ, slope, grad_bb = slot([wd, gd], activ, slope, grad_bb)
     wd = Pieces(whole(wd), hidden_tile, n_dp)
 
     grad_hidden, = rows_times(
         places, grad_bb, wd, hidden_tile * n_z, hidden_tile, lambda v, s: ((v * s.astype(F32)).astype(BF),), (slope,), (BF,),
         "grad_hidden",
     )
+    grad_hidden, activ = slot([gd], grad_hidden, activ)
     gu = rows_against(normed_b, grad_hidden, hidden_tile, "grad_up")
     block_out, sums_mlp = rows_times_t(
         places, activ, wd, hidden_tile, after_mlp, (middle, grad_result), mods, ((rows_of, BF),), 1, "down", to_place

time: 466 us -> 464 us (level)
  waiting for transfers between devices: 104 us -> 96 us
  local copies, waits for them, and re-layouts: 78.8 us -> 71.5 us
  other arithmetic: 37.4 us -> 42.8 us
    ppermute x12 -> x15, starting transfers between devices: 15.4 us -> 30.6 us  [exchange_steps(): pieces[r] = lax.ppermute(pieces[r], 'tensor', ring(n_z, sign * r))]
    ppermute x15 -> x12, starting transfers between devices: 32.3 us -> 20.3 us  [shifted(): lax.ppermute(pieces[r], 'tensor', ring(n_z, sign * r))]
    ppermute x12 -> x15, waiting for transfers between devices: 4.08 us -> 13.5 us  [exchange_steps(): pieces[r] = lax.ppermute(pieces[r], 'tensor', ring(n_z, sign * r))]
    ppermute x2, waiting for transfers between devices: 13 us -> 4.28 us  [gather_steps(): got = lax.ppermute(rows, 'dp', stage_perm(n_dp, t))]
    ppermute x3, waiting for transfers between devices: 6.65 us -> 0.01 us  [scatter_steps(): got = lax.ppermute(send, 'dp', core_perm(n_dp))]
    unnamed x170 -> x176, local copies, waits for them, and re-layouts: 40.3 us -> 34 us
    convert_element_type x7, other arithmetic: 22.2 us -> 27.3 us  [add_low(): functools.reduce(lambda a, b: a + b, [o.astype(F32) for o in others], fir...]
    ppermute x15 -> x12, waiting for transfers between devices: 41 us -> 40.6 us  [shifted(): lax.ppermute(pieces[r], 'tensor', ring(n_z, sign * r))]
  transfers between devices with their start and end apart: 54 -> 54, of which waited for: 20 -> 20; matrix products, arithmetic and copies ran while one was open for 19% -> 18% of each run, Pallas kernels for 28% -> 29%
where the time goes in v5:
time: 464 us; the launch traced here: 459 us
  Pallas kernels  135 us (29%)
  waiting for transfers between devices  96 us (21%)
  starting transfers between devices  81.9 us (18%)
  local copies, waits for them, and re-layouts  71.5 us (15%)
  other arithmetic  42.8 us (9%)
  matrix products  15.9 us (3%)
  between operations  15.6 us (3%)
    ppermute x12, waiting for transfers between devices, shifted(): lax.ppermute(pieces[r], 'tensor', ring(n_z, sign * r))  40.6 us
    pallas_call x4, Pallas kernels, rows_times_t(): pl.pallas_call(kernel, grid_spec=pltpu.PrefetchScalarGridSpec(num_scalar_...  38.2 us
    unnamed x176, local copies, waits for them, and re-layouts  34 us
    pallas_call x4, Pallas kernels, rows_times(): pl.pallas_call(kernel, grid_spec=pltpu.PrefetchScalarGridSpec(num_scalar_...  30.9 us
    ppermute x15, starting transfers between devices, exchange_steps(): pieces[r] = lax.ppermute(pieces[r], 'tensor', ring(n_z, sign * r))  30.6 us
    pallas_call x4, Pallas kernels, rows_against(): pl.pallas_call(kernel, grid_spec=pltpu.PrefetchScalarGridSpec(num_scalar_...  27.5 us
    convert_element_type x7, other arithmetic, add_low(): functools.reduce(lambda a, b: a + b, [o.astype(F32) for o in others], fir...  27.3 us
    ppermute x12, starting transfers between devices, shifted(): lax.ppermute(pieces[r], 'tensor', ring(n_z, sign * r))  20.3 us
  transfers between devices with their start and end apart: 54, of which 20 were waited for; matrix products, arithmetic and copies ran while one was open for 18% of the time, Pallas kernels for 29%

profile of v5, /device:TPU:0, one launch (start us, length us, event | category | flops | bytes accessed | tf_op | source)
XLA Modules:
  0.0 458.6 jit_solution(10507746999124211090)
XLA Ops:
  36.8 11.2 %all-to-all-done.1 = f32[32,1,2549]{2,1,0:T(1,128)} async-done(((f32[32,1,2549]{2,1,0:T(1,128)}), f32[32,1,2549]{2,1,0:T(1,128)}, u32[]{:S(2)}, u32[]{:S(2)}) %all-to-all-start.1) | async-done | bytes 326304 | tf_op jit(solution)/shard_map/all_to_all | solution.py:688
  59.4 11.3 %collective-permute-done.6 = bf16[10,16,1024]{2,1,0:T(8,128)(2,1)S(1)} collective-permute-done((bf16[10,16,1024]{2,1,0:T(8,128)(2,1)}, bf16[10,16,1024]{2,1,0:T(8,128)(2,1)S(1)}, u32[]{:S(2)}, u32[]{:S(2)}) %collective-permute-start.6) | collective-permute-done | bytes 327712 | tf_op jit(solution)/shard_map/tokens_in/ppermute | solution.py:183
  71.4 4.8 %fusion.10 = f32[16,9,64,64]{3,1,2,0:T(8,128)S(1)} fusion(pred[64,64,225,1]{2,1,0,3:T(32,128)(4,1)} %bitcast.135, f32[16,9,225]{2,1,0:T(8,128)S(1)} %dot_general.30), kind=kOutput, calls=%fused_computation.73 | convolution fusion | flops 1592524800 | bytes 3410496 | tf_op jit(solution)/shard_map/dot_general | solution.py:210
  81.0 7.3 %collective-permute-done.7 = bf16[10,16,1024]{2,1,0:T(8,128)(2,1)} collective-permute-done((bf16[10,16,1024]{2,1,0:T(8,128)(2,1)}, bf16[10,16,1024]{2,1,0:T(8,128)(2,1)}, u32[]{:S(2)}, u32[]{:S(2)}) %collective-permute-start.7) | collective-permute-done | bytes 327712 | tf_op jit(solution)/shard_map/tokens_in/ppermute | solution.py:183
  91.0 3.8 collective-permute-done.5.refs_3_
  109.2 7.2 %qkv.1.qkv_ref = bf16[640,3072]{1,0:T(8,128)(2,1)S(1)} custom-call(s32[12]{0:T(128)S(1)} %pad_add_fusion.places_ref, bf16[640,1024]{1,0:T(8,128)(2,1)S(1)} %fusion.7.x_ref, bf16[128,3072]{1,0:T(8,128)(2,1)} %join.3.refs_0_, bf16[128,3072]{1,0:T(8,128)(2,1)} %collective-permute-done.3.refs_1_, bf16[128,3072]{1,0:T(8,128)(2,1)} %collective-permute-done.4.refs_2_, ...), custom_call_target="tpu_custom_call" | custom-call | flops 1000000 | bytes 10000 | tf_op jit(solution)/shard_map/qkv/pallas_call | solution.py:300
  117.4 14.9 %attend.1 = (bf16[640,1024]{1,0:T(8,128)(2,1)S(1)}, bf16[2,16,320,320]{3,2,1,0:T(8,128)(2,1)S(1)}) custom-call(s32[1]{0:T(128)} %dynamic_slice.67.count_ref, bf16[640,3072]{1,0:T(8,128)(2,1)S(1)} %qkv.1.qkv_ref, f32[16,9,64,64]{3,2,1,0:T(8,128)S(1)} %bitcast.129), custom_call_target="tpu_custom_call" | custom-call | flops 1000000 | bytes 10000 | tf_op jit(solution)/shard_map/attend/pallas_call | solution.py:505
  141.2 8.8 %collective-permute-start.17 = (bf16[10,16,1024]{2,1,0:T(8,128)(2,1)}, bf16[10,16,1024]{2,1,0:T(8,128)(2,1)}, u32[]{:S(2)}, u32[]{:S(2)}) collective-permute-start(bf16[10,16,1024]{2,1,0:T(8,128)(2,1)} %get-tuple-element.216), channel_id=1, source_target_pairs={{0,2},{1,3},{2,0},{3,1},{4,6},{5,7},{6,4},{7,5},{8,10},{9,11},{10,... | collective-permute-start | bytes 983048 | tf_op jit(solution)/shard_map/tokens_in_2_left/ppermute | solution.py:190
  151.3 4.7 %out.1 = (f32[640,1024]{1,0:T(8,128)S(1)}, f32[640,1024]{1,0:T(8,128)S(1)}, bf16[640,1024]{1,0:T(8,128)(2,1)S(1)}) custom-call(s32[12]{0:T(128)S(1)} %pad_add_fusion.places_ref, bf16[640,1024]{1,0:T(8,128)(2,1)S(1)} %copy-done.18, bf16[8,4,160,1024]{3,2,1,0:T(8,128)(2,1)} %bitcast.122, bf16[640,1024]{1,0:T(8,128)(2,1)S(1)} %get-tuple-element.451.refs_1_.refs_8_, ...), custom_call_target="tpu_custom_call" | custom-call | flops 1000000 | bytes 10000 | tf_op jit(solution)/shard_map/out/pallas_call | solution.py:363
  157.4 7.5 %collective-permute-done.17 = bf16[10,16,1024]{2,1,0:T(8,128)(2,1)} collective-permute-done((bf16[10,16,1024]{2,1,0:T(8,128)(2,1)}, bf16[10,16,1024]{2,1,0:T(8,128)(2,1)}, u32[]{:S(2)}, u32[]{:S(2)}) %collective-permute-start.17) | collective-permute-done | bytes 327712 | tf_op jit(solution)/shard_map/tokens_in_2_left/ppermute | solution.py:190
  172.8 12.2 %up.1 = (bf16[640,4096]{1,0:T(8,128)(2,1)S(1)}, bf16[640,4096]{1,0:T(8,128)(2,1)S(1)}) custom-call(s32[12]{0:T(128)S(1)} %pad_add_fusion.places_ref, bf16[640,1024]{1,0:T(8,128)(2,1)S(1)} %get-tuple-element.224.x_ref, bf16[8,4,160,1024]{3,2,1,0:T(8,128)(2,1)S(1)} %bitcast.124), custom_call_target="tpu_custom_call" | custom-call | flops 1000000 | bytes 10000 | tf_op jit(solution)/shard_map/up/pallas_call | solution.py:300
  190.1 4.3 collective-permute-done.18.refs_1_
  197.4 9.2 %grad_down.1 = (bf16[512,4096]{1,0:T(8,128)(2,1)S(1)}, bf16[512,4096]{1,0:T(8,128)(2,1)}) custom-call(s32[1]{0:T(128)} %constant.239.clone.1.places_ref, bf16[640,1024]{1,0:T(8,128)(2,1)S(1)} %get-tuple-element.240.x_ref, bf16[640,4096]{1,0:T(8,128)(2,1)S(1)} %copy-done.6), custom_call_target="tpu_custom_call" | custom-call | flops 1000000 | bytes 10000 | tf_op jit(solution)/shard_map/grad_down/pallas_call | solution.py:409
  206.7 9.3 %grad_hidden.1.y_ref.x_ref = bf16[640,4096]{1,0:T(8,128)(2,1)S(1)} custom-call(s32[12]{0:T(128)S(1)} %pad_add_fusion.places_ref, bf16[640,1024]{1,0:T(8,128)(2,1)S(1)} %get-tuple-element.240.x_ref, bf16[256,4096]{1,0:T(8,128)(2,1)} %join.5.refs_0_, bf16[256,4096]{1,0:T(8,128)(2,1)} %collective-permute-done.18.refs_1_, ...), custom_call_target="tpu_custom_call" | custom-call | flops 1000000 | bytes 10000 | tf_op jit(solution)/shard_map/grad_hidden/pallas_call | solution.py:300
  216.1 6.3 %add_convert_fusion.3 = (bf16[256,4096]{1,0:T(8,128)(2,1)}, bf16[256,4096]{1,0:T(8,128)(2,1)}) fusion(bf16[512,4096]{1,0:T(8,128)(2,1)} %collective-permute-done.23, bf16[512,4096]{1,0:T(8,128)(2,1)S(1)} %get-tuple-element.238), kind=kLoop, calls=%fused_computation.3 | loop fusion | flops 8388608 | bytes 12582912 | tf_op jit(solution)/shard_map/scatter_down_2_left/convert_element_type | solution.py:108
  223.0 8.5 %grad_up.1 = (bf16[512,4096]{1,0:T(8,128)(2,1)S(1)}, bf16[512,4096]{1,0:T(8,128)(2,1)S(1)}) custom-call(s32[1]{0:T(128)} %constant.239.clone.1.places_ref, bf16[640,1024]{1,0:T(8,128)(2,1)S(1)} %get-tuple-element.224.x_ref, bf16[640,4096]{1,0:T(8,128)(2,1)S(1)} %grad_hidden.1.y_ref.x_ref), custom_call_target="tpu_custom_call" | custom-call | flops 1000000 | bytes 10000 | tf_op jit(solution)/shard_map/grad_up/pallas_call | solution.py:409
  233.5 10.4 %down.1 = (bf16[640,1024]{1,0:T(8,128)(2,1)S(1)}, f32[1,1024]{1,0:T(1,128)S(1)}) custom-call(s32[12]{0:T(128)S(1)} %pad_add_fusion.places_ref, bf16[640,4096]{1,0:T(8,128)(2,1)} %copy-done.5, bf16[256,4096]{1,0:T(8,128)(2,1)} %join.5.refs_0_, bf16[256,4096]{1,0:T(8,128)(2,1)} %collective-permute-done.18.refs_1_, bf16[256,4096]{1,0:T(8,128)(2,1)S(1)} %copy-done.12, ...), custom_call_target="tpu_custom_call" | custom-call | flops 1000000 | bytes 10000 | tf_op jit(solution)/shard_map/down/pallas_call | solution.py:363
  244.9 3.8 collective-permute-done.24
  254.9 12.3 %grad_normed_b.1 = (f32[640,1024]{1,0:T(8,128)S(1)}, bf16[640,1024]{1,0:T(8,128)(2,1)S(1)}, f32[3,1024]{1,0:T(4,128)S(1)}) custom-call(s32[12]{0:T(128)S(1)} %pad_add_fusion.places_ref, bf16[640,4096]{1,0:T(8,128)(2,1)} %copy-done.2, bf16[8,4,160,1024]{3,2,1,0:T(8,128)(2,1)} %bitcast.123, f32[640,1024]{1,0:T(8,128)S(1)} %copy-done.10, ...), custom_call_target="tpu_custom_call" | custom-call | flops 1000000 | bytes 10000 | tf_op jit(solution)/shard_map/grad_normed_b/pallas_call | solution.py:363
  269.7 4.8 %add_convert_fusion.1 = (bf16[256,4096]{1,0:T(8,128)(2,1)S(1)}, bf16[256,4096]{1,0:T(8,128)(2,1)}) fusion(bf16[512,4096]{1,0:T(8,128)(2,1)} %collective-permute-done.25, bf16[512,4096]{1,0:T(8,128)(2,1)S(1)} %get-tuple-element.254), kind=kLoop, calls=%fused_computation.1 | loop fusion | flops 8388608 | bytes 12582912 | tf_op jit(solution)/shard_map/scatter_up_2_left/convert_element_type | solution.py:108
  286.5 17.4 %attend_back.1 = (bf16[640,3072]{1,0:T(8,128)(2,1)S(1)}, f32[16,9,64,64]{3,2,1,0:T(8,128)S(1)}) custom-call(s32[1]{0:T(128)} %dynamic_slice.67.count_ref, bf16[640,3072]{1,0:T(8,128)(2,1)S(1)} %copy-done.4, bf16[2,16,320,320]{3,2,1,0:T(8,128)(2,1)S(1)} %bitcast.132, bf16[640,1024]{1,0:T(8,128)(2,1)S(1)} %grad_att.1.gatt_ref), custom_call_target="tpu_custom_call" | custom-call | flops 1000000 | bytes 10000 | tf_op jit(solution)/shard_map/attend_back/pallas_call | solution.py:533
  306.0 5.1 %add_convert_fusion.5 = (bf16[128,4096]{1,0:T(8,128)(2,1)}, bf16[128,4096]{1,0:T(8,128)(2,1)}) fusion(bf16[256,4096]{1,0:T(8,128)(2,1)} %collective-permute-done.28, bf16[256,4096]{1,0:T(8,128)(2,1)S(1)} %get-tuple-element.399), kind=kLoop, calls=%fused_computation.19 | loop fusion | flops 4194304 | bytes 6291456 | tf_op jit(solution)/shard_map/scatter_up_1_left/convert_element_type | solution.py:108
  312.6 5.3 %reshape.377 = f32[144,4096]{1,0:T(8,128)} reshape(f32[16,9,64,64]{3,2,1,0:T(8,128)} %copy-done.20) | data formatting | bytes 4718592 | tf_op jit(solution)/shard_map/reshape | solution.py:216
  317.9 4.1 fusion.1
  328.1 7.4 %grad_qkv.1 = (bf16[512,3072]{1,0:T(8,128)(2,1)S(1)}, bf16[512,3072]{1,0:T(8,128)(2,1)}) custom-call(s32[1]{0:T(128)} %constant.239.clone.1.places_ref, bf16[640,1024]{1,0:T(8,128)(2,1)S(1)} %fusion.7.x_ref, bf16[640,3072]{1,0:T(8,128)(2,1)S(1)} %copy-done.8), custom_call_target="tpu_custom_call" | custom-call | flops 1000000 | bytes 10000 | tf_op jit(solution)/shard_map/grad_qkv/pallas_call | solution.py:409
  349.3 10.9 %grad_normed_a.1 = (bf16[640,1024]{1,0:T(8,128)(2,1)S(1)}, f32[2,1024]{1,0:T(2,128)S(1)}) custom-call(s32[12]{0:T(128)S(1)} %pad_add_fusion.places_ref, bf16[640,3072]{1,0:T(8,128)(2,1)} %copy-done.7, bf16[128,3072]{1,0:T(8,128)(2,1)} %join.3.refs_0_, bf16[128,3072]{1,0:T(8,128)(2,1)} %collective-permute-done.3.refs_1_, ...), custom_call_target="tpu_custom_call" | custom-call | flops 1000000 | bytes 10000 | tf_op jit(solution)/shard_map/grad_normed_a/pallas_call | solution.py:363
  360.2 4.0 add_convert_fusion.8
  364.3 4.2 collective-permute-done.37
  378.5 5.8 %collective-permute-done.39.refs_1_ = bf16[128,3072]{1,0:T(8,128)(2,1)S(1)} collective-permute-done((bf16[128,3072]{1,0:T(8,128)(2,1)}, bf16[128,3072]{1,0:T(8,128)(2,1)S(1)}, u32[]{:S(2)}, u32[]{:S(2)}) %collective-permute-start.39) | collective-permute-done | bytes 786464 | tf_op jit(solution)/shard_map/scatter_qkv_1_left/ppermute | solution.py:120
  393.3 7.1 %all-to-all-start.2 = ((f32[32,1,2552]{2,1,0:T(1,128)}), f32[32,1,2552]{2,1,0:T(1,128)}, u32[]{:S(2)}, u32[]{:S(2)}) async-start(f32[32,1,2552]{2,1,0:T(1,128)} %all_to_all.29), calls=%async_computation.2 | async-start | bytes 655360 | tf_op jit(solution)/shard_map/all_to_all | solution.py:774
  406.0 7.1 %all-to-all-done.2 = f32[32,1,2552]{2,1,0:T(1,128)} async-done(((f32[32,1,2552]{2,1,0:T(1,128)}), f32[32,1,2552]{2,1,0:T(1,128)}, u32[]{:S(2)}, u32[]{:S(2)}) %all-to-all-start.2) | async-done | bytes 326688 | tf_op jit(solution)/shard_map/all_to_all | solution.py:774
  430.4 16.9 %collective-permute-done.46 = bf16[128,1024]{1,0:T(8,128)(2,1)S(1)} collective-permute-done((bf16[128,1024]{1,0:T(8,128)(2,1)}, bf16[128,1024]{1,0:T(8,128)(2,1)S(1)}, u32[]{:S(2)}, u32[]{:S(2)}) %collective-permute-start.46) | collective-permute-done | bytes 262176 | tf_op jit(solution)/shard_map/ppermute | solution.py:183
  (387 shorter events, 185.1 us)
Async XLA Ops:
  7.2 142.8 %all-gather.3.cloned.1.call-start = ((), (), s32[]{:S(2)}) async-start(), calls=%async_computation.6 | async-start | bytes 10813440 | tf_op jit(solution)/shard_map/all_gather | solution.py:665
  11.0 38.8 %collective-permute-start = (bf16[128,768]{1,0:T(8,128)(2,1)S(1)}, bf16[128,768]{1,0:T(8,128)(2,1)S(1)}, u32[]{:S(2)}, u32[]{:S(2)}) collective-permute-start(bf16[128,768]{1,0:T(8,128)(2,1)S(1)} %copy.79), channel_id=1, source_target_pairs={{0,1},{1,2},{2,3},{3,0},{4,5},{5,6},{6,7},{7,4},{8,9},{9,10},{10,1... | collective-permute-start | bytes 589832 | tf_op jit(solution)/shard_map/ppermute | solution.py:183
  14.1 35.8 %collective-permute-start.1 = (bf16[128,768]{1,0:T(8,128)(2,1)S(1)}, bf16[128,768]{1,0:T(8,128)(2,1)S(1)}, u32[]{:S(2)}, u32[]{:S(2)}) collective-permute-start(bf16[128,768]{1,0:T(8,128)(2,1)S(1)} %copy.79), channel_id=1, source_target_pairs={{0,2},{1,3},{2,0},{3,1},{4,6},{5,7},{6,4},{7,5},{8,10},{9,11},{10,... | collective-permute-start | bytes 589832 | tf_op jit(solution)/shard_map/ppermute | solution.py:183
  16.7 33.2 %collective-permute-start.2 = (bf16[128,768]{1,0:T(8,128)(2,1)S(1)}, bf16[128,768]{1,0:T(8,128)(2,1)S(1)}, u32[]{:S(2)}, u32[]{:S(2)}) collective-permute-start(bf16[128,768]{1,0:T(8,128)(2,1)S(1)} %copy.79), channel_id=1, source_target_pairs={{0,3},{1,0},{2,1},{3,2},{4,7},{5,4},{6,5},{7,6},{8,11},{9,8},{10,9... | collective-permute-start | bytes 589832 | tf_op jit(solution)/shard_map/ppermute | solution.py:183
  32.5 382.4 %reduce-scatter.2.cloned.1.call-start = ((), (), s32[]{:S(2)}) async-start(), calls=%async_computation.5 | async-start | bytes 2359296 | tf_op jit(solution)/shard_map/reduce_scatter | solution.py:750
  51.0 40.1 %collective-permute-start.3 = (bf16[128,3072]{1,0:T(8,128)(2,1)}, bf16[128,3072]{1,0:T(8,128)(2,1)}, u32[]{:S(2)}, u32[]{:S(2)}) collective-permute-start(bf16[128,3072]{1,0:T(8,128)(2,1)} %join.3.refs_0_), channel_id=1, source_target_pairs={{0,8},{4,20},{8,0},{12,28},{16,24},{20,4},{24,16},{28,12},{1,9},{5... | collective-permute-start | bytes 2359304 | tf_op jit(solution)/shard_map/gather_qkv_2_left/ppermute | solution.py:98
  52.3 38.8 %collective-permute-start.4 = (bf16[128,3072]{1,0:T(8,128)(2,1)}, bf16[128,3072]{1,0:T(8,128)(2,1)}, u32[]{:S(2)}, u32[]{:S(2)}) collective-permute-start(bf16[128,3072]{1,0:T(8,128)(2,1)} %join.3.refs_0_), channel_id=1, source_target_pairs={{0,16},{4,12},{8,24},{12,4},{16,0},{20,28},{24,8},{28,20},{1,17},{... | collective-permute-start | bytes 2359304 | tf_op jit(solution)/shard_map/gather_qkv_2_left/ppermute | solution.py:98
  53.3 41.5 %collective-permute-start.5 = (bf16[128,3072]{1,0:T(8,128)(2,1)}, bf16[128,3072]{1,0:T(8,128)(2,1)}, u32[]{:S(2)}, u32[]{:S(2)}) collective-permute-start(bf16[128,3072]{1,0:T(8,128)(2,1)} %join.3.refs_0_), channel_id=1, source_target_pairs={{0,24},{4,28},{8,16},{12,20},{16,8},{20,12},{24,0},{28,4},{1,25},{... | collective-permute-start | bytes 2359304 | tf_op jit(solution)/shard_map/gather_qkv_2_left/ppermute | solution.py:98
  58.3 30.0 %collective-permute-start.7 = (bf16[10,16,1024]{2,1,0:T(8,128)(2,1)}, bf16[10,16,1024]{2,1,0:T(8,128)(2,1)}, u32[]{:S(2)}, u32[]{:S(2)}) collective-permute-start(bf16[10,16,1024]{2,1,0:T(8,128)(2,1)} %get-tuple-element.183), channel_id=1, source_target_pairs={{0,2},{1,3},{2,0},{3,1},{4,6},{5,7},{6,4},{7,5},{8,10},{9,11},{10,... | collective-permute-start | bytes 983048 | tf_op jit(solution)/shard_map/tokens_in/ppermute | solution.py:183
  102.4 34.0 %collective-permute-start.13 = (bf16[128,1024]{1,0:T(8,128)(2,1)S(1)}, bf16[128,1024]{1,0:T(8,128)(2,1)S(1)}, u32[]{:S(2)}, u32[]{:S(2)}) collective-permute-start(bf16[128,1024]{1,0:T(8,128)(2,1)S(1)} %copy-done.37), channel_id=1, source_target_pairs={{0,1},{1,2},{2,3},{3,0},{4,5},{5,6},{6,7},{7,4},{8,9},{9,10},{10,1... | collective-permute-start | bytes 786440 | tf_op jit(solution)/shard_map/ppermute | solution.py:183
  104.1 33.9 %collective-permute-start.14 = (bf16[128,1024]{1,0:T(8,128)(2,1)S(1)}, bf16[128,1024]{1,0:T(8,128)(2,1)S(1)}, u32[]{:S(2)}, u32[]{:S(2)}) collective-permute-start(bf16[128,1024]{1,0:T(8,128)(2,1)S(1)} %copy-done.37), channel_id=1, source_target_pairs={{0,2},{1,3},{2,0},{3,1},{4,6},{5,7},{6,4},{7,5},{8,10},{9,11},{10,... | collective-permute-start | bytes 786440 | tf_op jit(solution)/shard_map/ppermute | solution.py:183
  106.5 32.1 %collective-permute-start.15 = (bf16[128,1024]{1,0:T(8,128)(2,1)S(1)}, bf16[128,1024]{1,0:T(8,128)(2,1)S(1)}, u32[]{:S(2)}, u32[]{:S(2)}) collective-permute-start(bf16[128,1024]{1,0:T(8,128)(2,1)S(1)} %copy-done.37), channel_id=1, source_target_pairs={{0,3},{1,0},{2,1},{3,2},{4,7},{5,4},{6,5},{7,6},{8,11},{9,8},{10,9... | collective-permute-start | bytes 786440 | tf_op jit(solution)/shard_map/ppermute | solution.py:183
  139.7 25.3 %collective-permute-start.16 = (bf16[128,4096]{1,0:T(8,128)(2,1)}, bf16[128,4096]{1,0:T(8,128)(2,1)}, u32[]{:S(2)}, u32[]{:S(2)}) collective-permute-start(bf16[128,4096]{1,0:T(8,128)(2,1)} %join.4.refs_0_), channel_id=1, source_target_pairs={{0,8},{4,20},{8,0},{12,28},{16,24},{20,4},{24,16},{28,12},{1,9},{5... | collective-permute-start | bytes 3145736 | tf_op jit(solution)/shard_map/gather_down_3_left/ppermute | solution.py:101
  141.2 23.8 %collective-permute-start.17 = (bf16[10,16,1024]{2,1,0:T(8,128)(2,1)}, bf16[10,16,1024]{2,1,0:T(8,128)(2,1)}, u32[]{:S(2)}, u32[]{:S(2)}) collective-permute-start(bf16[10,16,1024]{2,1,0:T(8,128)(2,1)} %get-tuple-element.216), channel_id=1, source_target_pairs={{0,2},{1,3},{2,0},{3,1},{4,6},{5,7},{6,4},{7,5},{8,10},{9,11},{10,... | collective-permute-start | bytes 983048 | tf_op jit(solution)/shard_map/tokens_in_2_left/ppermute | solution.py:190
  168.0 26.4 %collective-permute-start.18 = (bf16[256,4096]{1,0:T(8,128)(2,1)}, bf16[256,4096]{1,0:T(8,128)(2,1)}, u32[]{:S(2)}, u32[]{:S(2)}) collective-permute-start(bf16[256,4096]{1,0:T(8,128)(2,1)} %join.5.refs_0_), channel_id=1, source_target_pairs={{0,16},{4,12},{8,24},{12,4},{16,0},{20,28},{24,8},{28,20},{1,17},{... | collective-permute-start | bytes 6291464 | tf_op jit(solution)/shard_map/gather_down_2_left/ppermute | solution.py:101
  222.4 26.3 %collective-permute-start.24 = (bf16[256,4096]{1,0:T(8,128)(2,1)}, bf16[256,4096]{1,0:T(8,128)(2,1)S(1)}, u32[]{:S(2)}, u32[]{:S(2)}) collective-permute-start(bf16[256,4096]{1,0:T(8,128)(2,1)} %get-tuple-element.247), channel_id=1, source_target_pairs={{0,16},{4,12},{8,24},{12,4},{16,0},{20,28},{24,8},{28,20},{1,17},{... | collective-permute-start | bytes 6291464 | tf_op jit(solution)/shard_map/scatter_down_2_left/ppermute | solution.py:126
  274.5 31.5 %collective-permute-start.28 = (bf16[256,4096]{1,0:T(8,128)(2,1)}, bf16[256,4096]{1,0:T(8,128)(2,1)}, u32[]{:S(2)}, u32[]{:S(2)}) collective-permute-start(bf16[256,4096]{1,0:T(8,128)(2,1)} %get-tuple-element.265), channel_id=1, source_target_pairs={{0,16},{4,12},{8,24},{12,4},{16,0},{20,28},{24,8},{28,20},{1,17},{... | collective-permute-start | bytes 6291464 | tf_op jit(solution)/shard_map/scatter_up_2_left/ppermute | solution.py:126
  275.1 36.0 %collective-permute-start.30 = (bf16[10,16,1024]{2,1,0:T(8,128)(2,1)S(1)}, bf16[10,16,1024]{2,1,0:T(8,128)(2,1)S(1)}, u32[]{:S(2)}, u32[]{:S(2)}) collective-permute-start(bf16[10,16,1024]{2,1,0:T(8,128)(2,1)S(1)} %copy-done.58), channel_id=1, source_target_pairs={{0,3},{1,0},{2,1},{3,2},{4,7},{5,4},{6,5},{7,6},{8,11},{9,8},{10,9... | collective-permute-start | bytes 983048 | tf_op jit(solution)/shard_map/tokens_out_1_left/ppermute | solution.py:190
  278.7 32.5 %collective-permute-start.31 = (bf16[10,16,1024]{2,1,0:T(8,128)(2,1)S(1)}, bf16[10,16,1024]{2,1,0:T(8,128)(2,1)S(1)}, u32[]{:S(2)}, u32[]{:S(2)}) collective-permute-start(bf16[10,16,1024]{2,1,0:T(8,128)(2,1)S(1)} %get-tuple-element.273), channel_id=1, source_target_pairs={{0,1},{1,2},{2,3},{3,0},{4,5},{5,6},{6,7},{7,4},{8,9},{9,10},{10,1... | collective-permute-start | bytes 983048 | tf_op jit(solution)/shard_map/tokens_out_1_left/ppermute | solution.py:190
  279.1 32.0 %collective-permute-start.29 = (bf16[128,1024]{1,0:T(8,128)(2,1)S(1)}, bf16[128,1024]{1,0:T(8,128)(2,1)S(1)}, u32[]{:S(2)}, u32[]{:S(2)}) collective-permute-start(bf16[128,1024]{1,0:T(8,128)(2,1)S(1)} %get-tuple-element.268), channel_id=1, source_target_pairs={{0,2},{1,3},{2,0},{3,1},{4,6},{5,7},{6,4},{7,5},{8,10},{9,11},{10,... | collective-permute-start | bytes 786440 | tf_op jit(solution)/shard_map/down_sum_2_left/ppermute | solution.py:190
  312.0 25.2 %collective-permute-start.32 = (bf16[128,4096]{1,0:T(8,128)(2,1)}, bf16[128,4096]{1,0:T(8,128)(2,1)}, u32[]{:S(2)}, u32[]{:S(2)}) collective-permute-start(bf16[128,4096]{1,0:T(8,128)(2,1)} %get-tuple-element.279), channel_id=1, source_target_pairs={{0,8},{4,20},{8,0},{12,28},{16,24},{20,4},{24,16},{28,12},{1,9},{5... | collective-permute-start | bytes 3145736 | tf_op jit(solution)/shard_map/scatter_up_1_left/ppermute | solution.py:126
  341.3 23.0 %collective-permute-start.36 = (bf16[128,1024]{1,0:T(8,128)(2,1)}, bf16[128,1024]{1,0:T(8,128)(2,1)S(1)}, u32[]{:S(2)}, u32[]{:S(2)}) collective-permute-start(bf16[128,1024]{1,0:T(8,128)(2,1)} %get-tuple-element.291), channel_id=1, source_target_pairs={{0,3},{1,0},{2,1},{3,2},{4,7},{5,4},{6,5},{7,6},{8,11},{9,8},{10,9... | collective-permute-start | bytes 786440 | tf_op jit(solution)/shard_map/up_sum_1_left/ppermute | solution.py:190
  344.6 23.9 %collective-permute-start.37 = (bf16[128,1024]{1,0:T(8,128)(2,1)}, bf16[128,1024]{1,0:T(8,128)(2,1)S(1)}, u32[]{:S(2)}, u32[]{:S(2)}) collective-permute-start(bf16[128,1024]{1,0:T(8,128)(2,1)} %get-tuple-element.292), channel_id=1, source_target_pairs={{0,2},{1,3},{2,0},{3,1},{4,6},{5,7},{6,4},{7,5},{8,10},{9,11},{10,... | collective-permute-start | bytes 786440 | tf_op jit(solution)/shard_map/up_sum_2_left/ppermute | solution.py:190
  344.7 23.7 %collective-permute-start.38 = (bf16[128,1024]{1,0:T(8,128)(2,1)}, bf16[128,1024]{1,0:T(8,128)(2,1)S(1)}, u32[]{:S(2)}, u32[]{:S(2)}) collective-permute-start(bf16[128,1024]{1,0:T(8,128)(2,1)} %get-tuple-element.293), channel_id=1, source_target_pairs={{0,1},{1,2},{2,3},{3,0},{4,5},{5,6},{6,7},{7,4},{8,9},{9,10},{10,1... | collective-permute-start | bytes 786440 | tf_op jit(solution)/shard_map/up_sum_1_left/ppermute | solution.py:190
  371.1 43.7 %collective-permute-start.42 = (bf16[10,16,1024]{2,1,0:T(8,128)(2,1)}, bf16[10,16,1024]{2,1,0:T(8,128)(2,1)}, u32[]{:S(2)}, u32[]{:S(2)}) collective-permute-start(bf16[10,16,1024]{2,1,0:T(8,128)(2,1)} %get-tuple-element.421), channel_id=1, source_target_pairs={{0,3},{1,0},{2,1},{3,2},{4,7},{5,4},{6,5},{7,6},{8,11},{9,8},{10,9... | collective-permute-start | bytes 983048 | tf_op jit(solution)/shard_map/tokens_out_1_left/ppermute | solution.py:190
  371.1 43.7 %collective-permute-start.43 = (bf16[10,16,1024]{2,1,0:T(8,128)(2,1)}, bf16[10,16,1024]{2,1,0:T(8,128)(2,1)}, u32[]{:S(2)}, u32[]{:S(2)}) collective-permute-start(bf16[10,16,1024]{2,1,0:T(8,128)(2,1)} %get-tuple-element.420), channel_id=1, source_target_pairs={{0,2},{1,3},{2,0},{3,1},{4,6},{5,7},{6,4},{7,5},{8,10},{9,11},{10,... | collective-permute-start | bytes 983048 | tf_op jit(solution)/shard_map/tokens_out_2_left/ppermute | solution.py:190
  373.8 41.1 %collective-permute-start.44 = (bf16[10,16,1024]{2,1,0:T(8,128)(2,1)}, bf16[10,16,1024]{2,1,0:T(8,128)(2,1)}, u32[]{:S(2)}, u32[]{:S(2)}) collective-permute-start(bf16[10,16,1024]{2,1,0:T(8,128)(2,1)} %get-tuple-element.419), channel_id=1, source_target_pairs={{0,1},{1,2},{2,3},{3,0},{4,5},{5,6},{6,7},{7,4},{8,9},{9,10},{10,1... | collective-permute-start | bytes 983048 | tf_op jit(solution)/shard_map/tokens_out_1_left/ppermute | solution.py:190
  376.8 38.1 %collective-permute-start.40 = (bf16[128,3072]{1,0:T(8,128)(2,1)}, bf16[128,3072]{1,0:T(8,128)(2,1)S(1)}, u32[]{:S(2)}, u32[]{:S(2)}) collective-permute-start(bf16[128,3072]{1,0:T(8,128)(2,1)} %get-tuple-element.308), channel_id=1, source_target_pairs={{0,16},{4,12},{8,24},{12,4},{16,0},{20,28},{24,8},{28,20},{1,17},{... | collective-permute-start | bytes 2359304 | tf_op jit(solution)/shard_map/scatter_qkv_1_left/ppermute | solution.py:120
  384.3 30.6 %collective-permute-start.41 = (bf16[128,3072]{1,0:T(8,128)(2,1)}, bf16[128,3072]{1,0:T(8,128)(2,1)S(1)}, u32[]{:S(2)}, u32[]{:S(2)}) collective-permute-start(bf16[128,3072]{1,0:T(8,128)(2,1)} %get-tuple-element.309), channel_id=1, source_target_pairs={{0,24},{4,28},{8,16},{12,20},{16,8},{20,12},{24,0},{28,4},{1,25},{... | collective-permute-start | bytes 2359304 | tf_op jit(solution)/shard_map/scatter_qkv_1_left/ppermute | solution.py:119
  421.2 26.1 %collective-permute-start.46 = (bf16[128,1024]{1,0:T(8,128)(2,1)}, bf16[128,1024]{1,0:T(8,128)(2,1)S(1)}, u32[]{:S(2)}, u32[]{:S(2)}) collective-permute-start(bf16[128,1024]{1,0:T(8,128)(2,1)} %get-tuple-element.333), channel_id=1, source_target_pairs={{0,2},{1,3},{2,0},{3,1},{4,6},{5,7},{6,4},{7,5},{8,10},{9,11},{10,... | collective-permute-start | bytes 786440 | tf_op jit(solution)/shard_map/ppermute | solution.py:183
  421.2 26.1 %collective-permute-start.47 = (bf16[128,1024]{1,0:T(8,128)(2,1)}, bf16[128,1024]{1,0:T(8,128)(2,1)S(1)}, u32[]{:S(2)}, u32[]{:S(2)}) collective-permute-start(bf16[128,1024]{1,0:T(8,128)(2,1)} %get-tuple-element.334), channel_id=1, source_target_pairs={{0,1},{1,2},{2,3},{3,0},{4,5},{5,6},{6,7},{7,4},{8,9},{9,10},{10,1... | collective-permute-start | bytes 786440 | tf_op jit(solution)/shard_map/ppermute | solution.py:183
  424.0 25.3 %all-to-all-start.3 = ((f32[32,1,1528]{2,1,0:T(1,128)}), f32[32,1,1528]{2,1,0:T(1,128)S(1)}, u32[]{:S(2)}, u32[]{:S(2)}) async-start(f32[32,1,1528]{2,1,0:T(1,128)} %all_to_all.32), calls=%async_computation.4 | async-start | bytes 393216 | tf_op jit(solution)/shard_map/all_to_all | solution.py:786
  (108 other events, 994.7 us)
Sparse Core Ops, SparseCore 0:
  10.9 136.7 all-gather.2
  341.4 46.2 reduce-scatter.1
